TPU v7x, 32 devices: a whole 2x2x4 slice. The times are simulated.
32 devices in a mesh: seq: 8 (over z, x), head: 4 (over y, core).
Axes of the slice: x: 2, y: 2, z: 4, core: 2. Of those that a mesh axis runs over, the one named last changes fastest.
Arguments:
- queries: bfloat16 [2048, 2048], P(('seq', 'head')), may hold values from -64 to 64
- keys: bfloat16 [2048, 1024], P(('seq', 'head')), may hold values from -6 to 6
- values: bfloat16 [2048, 1024], P(('seq', 'head')), may hold values from -6 to 6
- output_gradient: bfloat16 [2048, 2048], P(('seq', 'head')), may hold values from -6 to 6
- block_lo: int32 [16], P('seq'), may hold values from 0 to 15, as said below
Outputs:
- attended: bfloat16 [2048, 2048], P(('seq', 'head'))
- query_grads: bfloat16 [2048, 2048], P(('seq', 'head'))
- key_gradient_rows: bfloat16 [2048, 1024], P(('seq', 'head'))
- value_gradient_rows: bfloat16 [2048, 1024], P(('seq', 'head'))
Inputs may be any that keep to these rules, and one draw needn't show every extreme that they name: block_lo[b] is the larger of b - 8 and the first block of the document that holds block b; documents begin at block boundaries, block 0 begins one and blocks 1 to 8 begin none; block_lo never falls from one block to the next.
All inputs are finite; a program needn't handle non-finite values.
Results may differ from a plain program's by a relative error of at most 0.025.
Values may be sent and summed in bfloat16 or wider, within the bound.
No kernel may reach another device: no remote copies, remote signals or barrier semaphores. Data moves between devices by JAX's collectives and lax.ppermute only.
A program may use at most 64 MiB of HBM per device.

v0:
```python
import jax
import jax.numpy as jnp
from jax import lax
from jax.sharding import PartitionSpec as P

HEAD_SIZE = 128
BLOCK = 128
WBLOCKS = 8


query_scale = 168.0 ** (-0.5)
neg_fill = -1e30


def passed_along(x, axis, by):
    devices = lax.axis_size(axis)
    pairs = [(i, i + by) for i in range(devices) if 0 <= i + by < devices]
    return lax.ppermute(x, axis, pairs)


def body(queries, keys, values, output_gradient, block_lo):
    q_local, k_local, v_local, g_local = (
        lax.all_to_all(queries, "head", split_axis=1, concat_axis=0, tiled=True),
        lax.all_to_all(keys, "head", split_axis=1, concat_axis=0, tiled=True),
        lax.all_to_all(values, "head", split_axis=1, concat_axis=0, tiled=True),
        lax.all_to_all(output_gradient, "head", split_axis=1, concat_axis=0, tiled=True),
    )
    tok_dev = q_local.shape[0]
    window = WBLOCKS * BLOCK
    rim_count = window // tok_dev
    kv_cols = k_local.shape[1]
    heads_kv = kv_cols // HEAD_SIZE
    queries_per_group = q_local.shape[1] // kv_cols
    paired = jnp.stack([k_local, v_local])
    pieces = []
    for distance in range(rim_count, 0, -1):
        pieces.append(passed_along(paired, "seq", distance))
    extended = jnp.concatenate(pieces + [paired], axis=1)
    all_keys = extended[0]
    all_values = extended[1]
    seq_index = lax.axis_index("seq")
    q_pos = seq_index * tok_dev + jnp.arange(tok_dev, dtype=jnp.int32)
    k_pos = seq_index * tok_dev - window + jnp.arange(window + tok_dev, dtype=jnp.int32)
    lowest = jnp.broadcast_to(block_lo[:, None] * BLOCK, (block_lo.shape[0], BLOCK)).reshape(
        tok_dev
    )
    visible = (k_pos[None, :] <= q_pos[:, None]) & (q_pos[:, None] - k_pos[None, :] < window)
    visible = visible & (k_pos[None, :] >= lowest[:, None])
    out_parts, dq_parts, dk_parts, dv_parts = ([], [], [], [])
    for kv_head in range(heads_kv):
        low_col = kv_head * queries_per_group * HEAD_SIZE
        high_col = (kv_head + 1) * queries_per_group * HEAD_SIZE
        q_head = q_local[:, low_col:high_col].reshape(tok_dev, queries_per_group, HEAD_SIZE)
        g_head = g_local[:, low_col:high_col].reshape(tok_dev, queries_per_group, HEAD_SIZE)
        k_head = all_keys[:, kv_head * HEAD_SIZE : (kv_head + 1) * HEAD_SIZE]
        v_head = all_values[:, kv_head * HEAD_SIZE : (kv_head + 1) * HEAD_SIZE]
        scores = (
            jnp.einsum("thd,kd->htk", q_head, k_head, preferred_element_type=jnp.float32)
            * query_scale
        )
        scores = jnp.where(visible[None], scores, neg_fill)
        row_max = jnp.max(scores, axis=-1, keepdims=True)
        norm_logarithm = row_max + jnp.log(
            jnp.sum(jnp.exp(scores - row_max), axis=-1, keepdims=True)
        )
        probs = jnp.exp(scores - norm_logarithm)
        probs_b = probs.astype(jnp.bfloat16)
        attended = jnp.einsum(
            "htk,kd->thd", probs_b, v_head, preferred_element_type=jnp.float32
        ).astype(jnp.bfloat16)
        row_dot_products = jnp.sum(
            g_head.astype(jnp.float32) * attended.astype(jnp.float32), axis=-1
        )
        row_dot_products = jnp.transpose(row_dot_products)[:, :, None]
        prob_grads = jnp.einsum("thd,kd->htk", g_head, v_head, preferred_element_type=jnp.float32)
        score_grads = (probs * (prob_grads - row_dot_products)).astype(jnp.bfloat16)
        q_grad = query_scale * jnp.einsum(
            "htk,kd->thd", score_grads, k_head, preferred_element_type=jnp.float32
        )
        key_gradient = query_scale * jnp.einsum(
            "htk,thd->kd", score_grads, q_head, preferred_element_type=jnp.float32
        )
        value_gradient = jnp.einsum(
            "htk,thd->kd", probs_b, g_head, preferred_element_type=jnp.float32
        )
        out_parts.append(attended.reshape(tok_dev, queries_per_group * HEAD_SIZE))
        dq_parts.append(q_grad.astype(jnp.bfloat16).reshape(tok_dev, queries_per_group * HEAD_SIZE))
        dk_parts.append(key_gradient)
        dv_parts.append(value_gradient)
    grads = jnp.stack([jnp.concatenate(dk_parts, axis=1), jnp.concatenate(dv_parts, axis=1)])
    rim_grads = grads[:, :window]
    own_grads = grads[:, window:]
    for distance in range(1, rim_count + 1):
        block_index = rim_count - distance
        sent = rim_grads[:, block_index * tok_dev : (block_index + 1) * tok_dev]
        own_grads = own_grads + passed_along(sent, "seq", -distance)
    out_local = jnp.concatenate(out_parts, axis=1)
    dq_local = jnp.concatenate(dq_parts, axis=1)
    dk_local = own_grads[0].astype(jnp.bfloat16)
    dv_local = own_grads[1].astype(jnp.bfloat16)
    attended_all, q_grads, k_grads, v_grads = (
        lax.all_to_all(out_local, "head", split_axis=0, concat_axis=1, tiled=True),
        lax.all_to_all(dq_local, "head", split_axis=0, concat_axis=1, tiled=True),
        lax.all_to_all(dk_local, "head", split_axis=0, concat_axis=1, tiled=True),
        lax.all_to_all(dv_local, "head", split_axis=0, concat_axis=1, tiled=True),
    )
    return (attended_all, q_grads, k_grads, v_grads)


def solution(mesh):
    placed = (
        P(("seq", "head"), None),
        P(("seq", "head"), None),
        P(("seq", "head"), None),
        P(("seq", "head"), None),
        P("seq"),
    )
    return jax.shard_map(
        body,
        mesh=mesh,
        in_specs=placed,
        out_specs=(
            P(("seq", "head"), None),
            P(("seq", "head"), None),
            P(("seq", "head"), None),
            P(("seq", "head"), None),
        ),
        check_vma=False,
    )
```

profile of v0, /device:TPU:2, one launch (start us, length us, event | category | flops | bytes accessed | tf_op | source)
XLA Modules:
  0.0 172.1 jit_solution(16218341593211534168)
XLA Ops:
  0.6 1.6 copy.163
  2.3 3.3 %all-to-all-start = ((bf16[64,4,256]{2,0,1:T(8,128)(2,1)}), bf16[64,4,256]{2,0,1:T(8,128)(2,1)S(1)}, u32[]{:S(2)}, u32[]{:S(2)}) async-start(bf16[64,4,256]{2,0,1:T(8,128)(2,1)} %bitcast.143), calls=%async_computation | async-start | bytes 262144 | tf_op jit(solution)/shard_map/all_to_all | solution.py:24
  6.3 1.6 copy.162
  7.9 1.7 copy.161
  10.2 3.3 %all-to-all-start.1 = ((bf16[64,4,256]{2,0,1:T(8,128)(2,1)}), bf16[64,4,256]{2,0,1:T(8,128)(2,1)S(1)}, u32[]{:S(2)}, u32[]{:S(2)}) async-start(bf16[64,4,256]{2,0,1:T(8,128)(2,1)} %bitcast.142), calls=%async_computation.1 | async-start | bytes 262144 | tf_op jit(solution)/shard_map/all_to_all | solution.py:25
  13.5 4.6 %all-to-all-done.1 = bf16[64,4,256]{2,0,1:T(8,128)(2,1)S(1)} async-done(((bf16[64,4,256]{2,0,1:T(8,128)(2,1)}), bf16[64,4,256]{2,0,1:T(8,128)(2,1)S(1)}, u32[]{:S(2)}, u32[]{:S(2)}) %all-to-all-start.1) | async-done | bytes 131104 | tf_op jit(solution)/shard_map/all_to_all | solution.py:25
  18.1 3.4 %all-to-all-start.2 = ((bf16[64,4,512]{2,0,1:T(8,128)(2,1)}), bf16[64,4,512]{2,0,1:T(8,128)(2,1)S(1)}, u32[]{:S(2)}, u32[]{:S(2)}) async-start(bf16[64,4,512]{2,0,1:T(8,128)(2,1)} %bitcast.141), calls=%async_computation.2 | async-start | bytes 524288 | tf_op jit(solution)/shard_map/all_to_all | solution.py:23
  22.7 3.5 %collective-permute-start.3 = (bf16[2,256,256]{2,1,0:T(8,128)(2,1)S(1)}, bf16[2,256,256]{2,1,0:T(8,128)(2,1)S(1)}, u32[]{:S(2)}, u32[]{:S(2)}) collective-permute-start(bf16[2,256,256]{2,1,0:T(8,128)(2,1)S(1)} %pad_maximum_fusion.1), channel_id=1, source_target_pairs={{0,4},{4,8},{8,12},{12,16},{16,20},{20,24},{24,28},{1,5},{5,9},{9,... | collective-permute-start | bytes 786440 | tf_op jit(solution)/shard_map/ppermute | solution.py:18
  26.2 3.5 %collective-permute-start.2 = (bf16[2,256,256]{2,1,0:T(8,128)(2,1)S(1)}, bf16[2,256,256]{2,1,0:T(8,128)(2,1)S(1)}, u32[]{:S(2)}, u32[]{:S(2)}) collective-permute-start(bf16[2,256,256]{2,1,0:T(8,128)(2,1)S(1)} %pad_maximum_fusion.1), channel_id=1, source_target_pairs={{0,8},{4,12},{8,16},{12,20},{16,24},{20,28},{1,9},{5,13},{9,17},{1... | collective-permute-start | bytes 786440 | tf_op jit(solution)/shard_map/ppermute | solution.py:18
  29.7 4.4 %collective-permute-start.1 = (bf16[2,256,256]{2,1,0:T(8,128)(2,1)S(1)}, bf16[2,256,256]{2,1,0:T(8,128)(2,1)S(1)}, u32[]{:S(2)}, u32[]{:S(2)}) collective-permute-start(bf16[2,256,256]{2,1,0:T(8,128)(2,1)S(1)} %pad_maximum_fusion.1), channel_id=1, source_target_pairs={{0,12},{4,16},{8,20},{12,24},{16,28},{1,13},{5,17},{9,21},{13,25},... | collective-permute-start | bytes 786440 | tf_op jit(solution)/shard_map/ppermute | solution.py:18
  34.1 2.0 %collective-permute-start = (bf16[2,256,256]{2,1,0:T(8,128)(2,1)S(1)}, bf16[2,256,256]{2,1,0:T(8,128)(2,1)}, u32[]{:S(2)}, u32[]{:S(2)}) collective-permute-start(bf16[2,256,256]{2,1,0:T(8,128)(2,1)S(1)} %pad_maximum_fusion.1), channel_id=1, source_target_pairs={{0,16},{4,20},{8,24},{12,28},{1,17},{5,21},{9,25},{13,29},{2,18},{... | collective-permute-start | bytes 786440 | tf_op jit(solution)/shard_map/ppermute | solution.py:18
  36.1 3.4 %all-to-all-start.4 = ((bf16[64,4,512]{2,0,1:T(8,128)(2,1)}), bf16[64,4,512]{2,0,1:T(8,128)(2,1)S(1)}, u32[]{:S(2)}, u32[]{:S(2)}) async-start(bf16[64,4,512]{2,0,1:T(8,128)(2,1)} %bitcast.140), calls=%async_computation.4 | async-start | bytes 524288 | tf_op jit(solution)/shard_map/all_to_all | solution.py:26
  39.5 5.9 %all-to-all-done.4 = bf16[64,4,512]{2,0,1:T(8,128)(2,1)S(1)} async-done(((bf16[64,4,512]{2,0,1:T(8,128)(2,1)}), bf16[64,4,512]{2,0,1:T(8,128)(2,1)S(1)}, u32[]{:S(2)}, u32[]{:S(2)}) %all-to-all-start.4) | async-done | bytes 262176 | tf_op jit(solution)/shard_map/all_to_all | solution.py:26
  45.9 3.3 %collective-permute-done = bf16[2,256,256]{2,1,0:T(8,128)(2,1)} collective-permute-done((bf16[2,256,256]{2,1,0:T(8,128)(2,1)S(1)}, bf16[2,256,256]{2,1,0:T(8,128)(2,1)}, u32[]{:S(2)}, u32[]{:S(2)}) %collective-permute-start) | collective-permute-done | bytes 262176 | tf_op jit(solution)/shard_map/ppermute | solution.py:18
  58.2 1.4 fusion.29
  59.6 1.9 %collective-permute-start.4 = (f32[2,256,256]{1,2,0:T(8,128)}, f32[2,256,256]{1,2,0:T(8,128)}, u32[]{:S(2)}, u32[]{:S(2)}) collective-permute-start(f32[2,256,256]{1,2,0:T(8,128)} %get-tuple-element.4), channel_id=1, source_target_pairs={{4,0},{8,4},{12,8},{16,12},{20,16},{24,20},{28,24},{5,1},{9,5},{13... | collective-permute-start | bytes 1572872 | tf_op jit(solution)/shard_map/ppermute | solution.py:18
  61.5 1.3 collective-permute-start.5
  67.3 1.6 concatenate.27
  70.9 1.6 pad_maximum_fusion.2
  72.5 3.4 %all-to-all-start.3 = ((bf16[4,64,512]{2,1,0:T(8,128)(2,1)}), bf16[4,64,512]{2,1,0:T(8,128)(2,1)S(1)}, u32[]{:S(2)}, u32[]{:S(2)}) async-start(bf16[4,64,512]{2,1,0:T(8,128)(2,1)} %pad_maximum_fusion.2), calls=%async_computation.3 | async-start | bytes 524288 | tf_op jit(solution)/shard_map/all_to_all | solution.py:102
  75.9 2.3 %fusion.21 = bf16[256,2,128]{0,2,1:T(8,128)(2,1)} fusion(bf16[2,256,1280]{1,2,0:T(8,128)(2,1)} %copy-done, bf16[1280,256]{1,0:T(8,128)(2,1)S(1)} %get-tuple-element.9), kind=kOutput, calls=%fused_computation.48 | convolution fusion | flops 167903232 | bytes 1769472 | tf_op jit(solution)/shard_map/htk,kd->thd/dot_general | solution.py:77
  79.4 1.6 pad_maximum_fusion.3
  81.0 9.2 %collective-permute-done.5 = f32[2,256,256]{1,2,0:T(8,128)} collective-permute-done((f32[2,256,256]{1,2,0:T(8,128)}, f32[2,256,256]{1,2,0:T(8,128)}, u32[]{:S(2)}, u32[]{:S(2)}) %collective-permute-start.5) | collective-permute-done | bytes 524320 | tf_op jit(solution)/shard_map/ppermute | solution.py:18
  90.2 23.0 %collective-permute-done.7 = f32[2,256,256]{1,2,0:T(8,128)} collective-permute-done((f32[2,256,256]{1,2,0:T(8,128)}, f32[2,256,256]{1,2,0:T(8,128)}, u32[]{:S(2)}, u32[]{:S(2)}) %collective-permute-start.7) | collective-permute-done | bytes 524320 | tf_op jit(solution)/shard_map/ppermute | solution.py:18
  113.2 31.3 %collective-permute-done.6 = f32[2,256,256]{1,2,0:T(8,128)} collective-permute-done((f32[2,256,256]{1,2,0:T(8,128)}, f32[2,256,256]{1,2,0:T(8,128)}, u32[]{:S(2)}, u32[]{:S(2)}) %collective-permute-start.6) | collective-permute-done | bytes 524320 | tf_op jit(solution)/shard_map/ppermute | solution.py:18
  144.5 1.7 fusion.28
  146.2 3.4 %all-to-all-start.5 = ((bf16[4,64,512]{2,1,0:T(8,128)(2,1)}), bf16[4,64,512]{2,1,0:T(8,128)(2,1)S(1)}, u32[]{:S(2)}, u32[]{:S(2)}) async-start(bf16[4,64,512]{2,1,0:T(8,128)(2,1)} %pad_maximum_fusion.3), calls=%async_computation.5 | async-start | bytes 524288 | tf_op jit(solution)/shard_map/all_to_all | solution.py:103
  150.4 5.2 %all-to-all-done.5 = bf16[4,64,512]{2,1,0:T(8,128)(2,1)S(1)} async-done(((bf16[4,64,512]{2,1,0:T(8,128)(2,1)}), bf16[4,64,512]{2,1,0:T(8,128)(2,1)S(1)}, u32[]{:S(2)}, u32[]{:S(2)}) %all-to-all-start.5) | async-done | bytes 262176 | tf_op jit(solution)/shard_map/all_to_all | solution.py:103
  155.6 3.3 %all-to-all-start.7 = ((bf16[4,64,256]{2,1,0:T(8,128)(2,1)}), bf16[4,64,256]{2,1,0:T(8,128)(2,1)S(1)}, u32[]{:S(2)}, u32[]{:S(2)}) async-start(bf16[4,64,256]{2,1,0:T(8,128)(2,1)} %bitcast.45), calls=%async_computation.7 | async-start | bytes 262144 | tf_op jit(solution)/shard_map/all_to_all | solution.py:105
  159.7 3.8 %all-to-all-done.7 = bf16[4,64,256]{2,1,0:T(8,128)(2,1)S(1)} async-done(((bf16[4,64,256]{2,1,0:T(8,128)(2,1)}), bf16[4,64,256]{2,1,0:T(8,128)(2,1)S(1)}, u32[]{:S(2)}, u32[]{:S(2)}) %all-to-all-start.7) | async-done | bytes 131104 | tf_op jit(solution)/shard_map/all_to_all | solution.py:105
  163.5 3.3 %all-to-all-start.6 = ((bf16[4,64,256]{2,1,0:T(8,128)(2,1)}), bf16[4,64,256]{2,1,0:T(8,128)(2,1)S(1)}, u32[]{:S(2)}, u32[]{:S(2)}) async-start(bf16[4,64,256]{2,1,0:T(8,128)(2,1)} %bitcast.43), calls=%async_computation.6 | async-start | bytes 262144 | tf_op jit(solution)/shard_map/all_to_all | solution.py:104
  169.0 2.4 %all-to-all-done.6 = bf16[4,64,256]{2,1,0:T(8,128)(2,1)S(1)} async-done(((bf16[4,64,256]{2,1,0:T(8,128)(2,1)}), bf16[4,64,256]{2,1,0:T(8,128)(2,1)S(1)}, u32[]{:S(2)}, u32[]{:S(2)}) %all-to-all-start.6) | async-done | bytes 131104 | tf_op jit(solution)/shard_map/all_to_all | solution.py:104
  (62 shorter events, 23.6 us)
Async XLA Ops:
  0.6 21.3 %copy-start.1 = (bf16[64,2048]{1,0:T(8,128)(2,1)S(1)}, bf16[64,2048]{1,0:T(8,128)(2,1)}, u32[]{:S(2)}) copy-start(bf16[64,2048]{1,0:T(8,128)(2,1)} %param.8) | copy-start | bytes 786436
  2.3 7.9 %all-to-all-start = ((bf16[64,4,256]{2,0,1:T(8,128)(2,1)}), bf16[64,4,256]{2,0,1:T(8,128)(2,1)S(1)}, u32[]{:S(2)}, u32[]{:S(2)}) async-start(bf16[64,4,256]{2,0,1:T(8,128)(2,1)} %bitcast.143), calls=%async_computation | async-start | bytes 262144 | tf_op jit(solution)/shard_map/all_to_all | solution.py:24
  10.2 7.9 %all-to-all-start.1 = ((bf16[64,4,256]{2,0,1:T(8,128)(2,1)}), bf16[64,4,256]{2,0,1:T(8,128)(2,1)S(1)}, u32[]{:S(2)}, u32[]{:S(2)}) async-start(bf16[64,4,256]{2,0,1:T(8,128)(2,1)} %bitcast.142), calls=%async_computation.1 | async-start | bytes 262144 | tf_op jit(solution)/shard_map/all_to_all | solution.py:25
  18.1 18.0 %all-to-all-start.2 = ((bf16[64,4,512]{2,0,1:T(8,128)(2,1)}), bf16[64,4,512]{2,0,1:T(8,128)(2,1)S(1)}, u32[]{:S(2)}, u32[]{:S(2)}) async-start(bf16[64,4,512]{2,0,1:T(8,128)(2,1)} %bitcast.141), calls=%async_computation.2 | async-start | bytes 524288 | tf_op jit(solution)/shard_map/all_to_all | solution.py:23
  22.7 27.6 %collective-permute-start.3 = (bf16[2,256,256]{2,1,0:T(8,128)(2,1)S(1)}, bf16[2,256,256]{2,1,0:T(8,128)(2,1)S(1)}, u32[]{:S(2)}, u32[]{:S(2)}) collective-permute-start(bf16[2,256,256]{2,1,0:T(8,128)(2,1)S(1)} %pad_maximum_fusion.1), channel_id=1, source_target_pairs={{0,4},{4,8},{8,12},{12,16},{16,20},{20,24},{24,28},{1,5},{5,9},{9,... | collective-permute-start | bytes 786440 | tf_op jit(solution)/shard_map/ppermute | solution.py:18
  26.2 24.1 %collective-permute-start.2 = (bf16[2,256,256]{2,1,0:T(8,128)(2,1)S(1)}, bf16[2,256,256]{2,1,0:T(8,128)(2,1)S(1)}, u32[]{:S(2)}, u32[]{:S(2)}) collective-permute-start(bf16[2,256,256]{2,1,0:T(8,128)(2,1)S(1)} %pad_maximum_fusion.1), channel_id=1, source_target_pairs={{0,8},{4,12},{8,16},{12,20},{16,24},{20,28},{1,9},{5,13},{9,17},{1... | collective-permute-start | bytes 786440 | tf_op jit(solution)/shard_map/ppermute | solution.py:18
  29.7 20.5 %collective-permute-start.1 = (bf16[2,256,256]{2,1,0:T(8,128)(2,1)S(1)}, bf16[2,256,256]{2,1,0:T(8,128)(2,1)S(1)}, u32[]{:S(2)}, u32[]{:S(2)}) collective-permute-start(bf16[2,256,256]{2,1,0:T(8,128)(2,1)S(1)} %pad_maximum_fusion.1), channel_id=1, source_target_pairs={{0,12},{4,16},{8,20},{12,24},{16,28},{1,13},{5,17},{9,21},{13,25},... | collective-permute-start | bytes 786440 | tf_op jit(solution)/shard_map/ppermute | solution.py:18
  34.1 15.2 %collective-permute-start = (bf16[2,256,256]{2,1,0:T(8,128)(2,1)S(1)}, bf16[2,256,256]{2,1,0:T(8,128)(2,1)}, u32[]{:S(2)}, u32[]{:S(2)}) collective-permute-start(bf16[2,256,256]{2,1,0:T(8,128)(2,1)S(1)} %pad_maximum_fusion.1), channel_id=1, source_target_pairs={{0,16},{4,20},{8,24},{12,28},{1,17},{5,21},{9,25},{13,29},{2,18},{... | collective-permute-start | bytes 786440 | tf_op jit(solution)/shard_map/ppermute | solution.py:18
  36.1 9.4 %all-to-all-start.4 = ((bf16[64,4,512]{2,0,1:T(8,128)(2,1)}), bf16[64,4,512]{2,0,1:T(8,128)(2,1)S(1)}, u32[]{:S(2)}, u32[]{:S(2)}) async-start(bf16[64,4,512]{2,0,1:T(8,128)(2,1)} %bitcast.140), calls=%async_computation.4 | async-start | bytes 524288 | tf_op jit(solution)/shard_map/all_to_all | solution.py:26
  56.4 1.1 copy-start
  59.6 21.4 %collective-permute-start.4 = (f32[2,256,256]{1,2,0:T(8,128)}, f32[2,256,256]{1,2,0:T(8,128)}, u32[]{:S(2)}, u32[]{:S(2)}) collective-permute-start(f32[2,256,256]{1,2,0:T(8,128)} %get-tuple-element.4), channel_id=1, source_target_pairs={{4,0},{8,4},{12,8},{16,12},{20,16},{24,20},{28,24},{5,1},{9,5},{13... | collective-permute-start | bytes 1572872 | tf_op jit(solution)/shard_map/ppermute | solution.py:18
  61.5 28.7 %collective-permute-start.5 = (f32[2,256,256]{1,2,0:T(8,128)}, f32[2,256,256]{1,2,0:T(8,128)}, u32[]{:S(2)}, u32[]{:S(2)}) collective-permute-start(f32[2,256,256]{1,2,0:T(8,128)} %get-tuple-element.5), channel_id=1, source_target_pairs={{8,0},{12,4},{16,8},{20,12},{24,16},{28,20},{9,1},{13,5},{17,9},{2... | collective-permute-start | bytes 1572872 | tf_op jit(solution)/shard_map/ppermute | solution.py:18
  62.8 50.4 %collective-permute-start.7 = (f32[2,256,256]{1,2,0:T(8,128)}, f32[2,256,256]{1,2,0:T(8,128)}, u32[]{:S(2)}, u32[]{:S(2)}) collective-permute-start(f32[2,256,256]{1,2,0:T(8,128)} %get-tuple-element.6), channel_id=1, source_target_pairs={{16,0},{20,4},{24,8},{28,12},{17,1},{21,5},{25,9},{29,13},{18,2},{... | collective-permute-start | bytes 1572872 | tf_op jit(solution)/shard_map/ppermute | solution.py:18
  64.1 80.4 %collective-permute-start.6 = (f32[2,256,256]{1,2,0:T(8,128)}, f32[2,256,256]{1,2,0:T(8,128)}, u32[]{:S(2)}, u32[]{:S(2)}) collective-permute-start(f32[2,256,256]{1,2,0:T(8,128)} %get-tuple-element.7), channel_id=1, source_target_pairs={{12,0},{16,4},{20,8},{24,12},{28,16},{13,1},{17,5},{21,9},{25,13},... | collective-permute-start | bytes 1572872 | tf_op jit(solution)/shard_map/ppermute | solution.py:18
  72.5 73.7 %all-to-all-start.3 = ((bf16[4,64,512]{2,1,0:T(8,128)(2,1)}), bf16[4,64,512]{2,1,0:T(8,128)(2,1)S(1)}, u32[]{:S(2)}, u32[]{:S(2)}) async-start(bf16[4,64,512]{2,1,0:T(8,128)(2,1)} %pad_maximum_fusion.2), calls=%async_computation.3 | async-start | bytes 524288 | tf_op jit(solution)/shard_map/all_to_all | solution.py:102
  146.2 9.4 %all-to-all-start.5 = ((bf16[4,64,512]{2,1,0:T(8,128)(2,1)}), bf16[4,64,512]{2,1,0:T(8,128)(2,1)S(1)}, u32[]{:S(2)}, u32[]{:S(2)}) async-start(bf16[4,64,512]{2,1,0:T(8,128)(2,1)} %pad_maximum_fusion.3), calls=%async_computation.5 | async-start | bytes 524288 | tf_op jit(solution)/shard_map/all_to_all | solution.py:103
  155.6 7.9 %all-to-all-start.7 = ((bf16[4,64,256]{2,1,0:T(8,128)(2,1)}), bf16[4,64,256]{2,1,0:T(8,128)(2,1)S(1)}, u32[]{:S(2)}, u32[]{:S(2)}) async-start(bf16[4,64,256]{2,1,0:T(8,128)(2,1)} %bitcast.45), calls=%async_computation.7 | async-start | bytes 262144 | tf_op jit(solution)/shard_map/all_to_all | solution.py:105
  163.5 7.9 %all-to-all-start.6 = ((bf16[4,64,256]{2,1,0:T(8,128)(2,1)}), bf16[4,64,256]{2,1,0:T(8,128)(2,1)S(1)}, u32[]{:S(2)}, u32[]{:S(2)}) async-start(bf16[4,64,256]{2,1,0:T(8,128)(2,1)} %bitcast.43), calls=%async_computation.6 | async-start | bytes 262144 | tf_op jit(solution)/shard_map/all_to_all | solution.py:104
where the time goes:
time: 173 us; the launch traced here: 172 us
  waiting for transfers between devices  89.3 us (52%)
  starting transfers between devices  46.1 us (27%)
  local copies, waits for them, and re-layouts  18.1 us (10%)
  matrix products  9.1 us (5%)
  other arithmetic  8.37 us (5%)
    ppermute x8, waiting for transfers between devices, passed_along(): return lax.ppermute(x, axis, pairs)  66.8 us
    ppermute x8, starting transfers between devices, passed_along(): return lax.ppermute(x, axis, pairs)  19.2 us
    all_to_all x1, waiting for transfers between devices, body(): lax.all_to_all(output_gradient, 'head', split_axis=1, concat_axis=0, tile...  5.94 us
    all_to_all x1, waiting for transfers between devices, body(): lax.all_to_all(dq_local, 'head', split_axis=0, concat_axis=1, tiled=True)  5.18 us
    all_to_all x1, waiting for transfers between devices, body(): lax.all_to_all(values, 'head', split_axis=1, concat_axis=0, tiled=True)  4.56 us
    all_to_all x1, waiting for transfers between devices, body(): lax.all_to_all(dv_local, 'head', split_axis=0, concat_axis=1, tiled=True)  3.81 us
  transfers between devices with their start and end apart: 16, of which 10 were waited for; matrix products, arithmetic and copies ran while one was open for 14% of the time, Pallas kernels for 0%

commit v1 on v0

v1 whole, which is shorter than its diff:
```python
import functools

import jax
import jax.numpy as jnp
from jax import lax
from jax.experimental import pallas as pl
from jax.experimental.pallas import tpu as pltpu
from jax.sharding import Mesh, PartitionSpec as P

HEAD_SIZE = 128
BLOCK = 128
WBLOCKS = 8
LOG2E = 1.4426950408889634

query_scale = 168.0 ** (-0.5)
neg_fill = -1e30
EXTRA = 8

VM = pl.BlockSpec(memory_space=pltpu.VMEM)
SM = pl.BlockSpec(memory_space=pltpu.SMEM)


def pack_kv_kernel(k_ref, v_ref, o_ref):
    n = o_ref.shape[0]
    for i in range(n):
        cols = slice(i * HEAD_SIZE, (i + 1) * HEAD_SIZE)
        o_ref[i, :, :HEAD_SIZE] = k_ref[:, cols]
        o_ref[i, :, HEAD_SIZE:] = v_ref[:, cols]


def pack_qg_kernel(base_ref, lo_ref, q_ref, g_ref, o_ref):
    n, rows, _ = o_ref.shape
    rows -= EXTRA
    wide = q_ref.shape[1] // n
    for i in range(n):
        cols = slice(i * wide, (i + 1) * wide)
        o_ref[i, :rows, :wide] = q_ref[:, cols]
        o_ref[i, :rows, wide:] = g_ref[:, cols]
    lane = lax.broadcasted_iota(jnp.int32, (EXTRA, 2 * wide), 1)
    told = jnp.zeros((EXTRA, 2 * wide), jnp.float32)
    for j in range(lo_ref.shape[0]):
        back = (base_ref[0] + j - lo_ref[j]).astype(jnp.float32)
        told = jnp.where(lane // BLOCK == j, back, told)
    for i in range(n):
        o_ref[i, rows:, :] = told.astype(jnp.bfloat16)


def attention_kernel(head_count, qg_ref, kv0_ref, kv1_ref, kv2_ref,
                     od_ref, g0_ref, g1_ref, g2_ref, k_s, v_s, dk_s, dv_s):
    n, rows, _ = kv0_ref.shape
    tok = n * rows
    blocks = tok // BLOCK
    for part, ref in enumerate((kv2_ref, kv1_ref, kv0_ref)):
        k_s[part * tok : (part + 1) * tok] = ref[:, :, :HEAD_SIZE].reshape(tok, HEAD_SIZE)
        v_s[part * tok : (part + 1) * tok] = ref[:, :, HEAD_SIZE:].reshape(tok, HEAD_SIZE)
    dk_s[...] = jnp.zeros_like(dk_s)
    dv_s[...] = jnp.zeros_like(dv_s)
    span = (WBLOCKS + 1) * BLOCK
    per = BLOCK // rows
    seq_blocks = head_count * rows // BLOCK
    col = lax.broadcasted_iota(jnp.int32, (BLOCK, span), 1)
    row = lax.broadcasted_iota(jnp.int32, (BLOCK, span), 0)
    band = (col > row) & (col <= row + WBLOCKS * BLOCK)
    hi = lax.axis_index("hi")
    for i in range(blocks):
        first = 2 * tok + (i - WBLOCKS) * BLOCK
        keys = slice(first, first + span)
        chunk = slice(i * per, (i + 1) * per)

        def head_of(j):
            return qg_ref[chunk, :rows, j * HEAD_SIZE : (j + 1) * HEAD_SIZE].reshape(
                BLOCK, HEAD_SIZE
            )

        q = jnp.concatenate([head_of(0), head_of(1)], axis=0)
        g = jnp.concatenate([head_of(2), head_of(3)], axis=0)
        owner = (i // seq_blocks) * head_count
        lane = (i % seq_blocks) * BLOCK
        back = qg_ref[owner, rows : rows + 1, lane : lane + 1].astype(jnp.float32)
        least = jnp.maximum(
            (WBLOCKS - back) * BLOCK,
            (WBLOCKS - (hi * blocks + i)).astype(jnp.float32) * BLOCK,
        )
        seen = band & (col.astype(jnp.float32) >= least)
        seen = jnp.concatenate([seen, seen], axis=0)
        k = k_s[keys]
        v = v_s[keys]
        s = lax.dot_general(q, k, (((1,), (1,)), ((), ())), preferred_element_type=jnp.float32)
        s = jnp.where(seen, s * (query_scale * LOG2E), neg_fill)
        e = jnp.exp2(s - jnp.max(s, axis=1, keepdims=True))
        p = e * (1.0 / jnp.sum(e, axis=1, keepdims=True))
        pb = p.astype(jnp.bfloat16)
        o = jnp.dot(pb, v, preferred_element_type=jnp.float32).astype(jnp.bfloat16)
        dots = jnp.sum(g.astype(jnp.float32) * o.astype(jnp.float32), axis=1, keepdims=True)
        dp = lax.dot_general(g, v, (((1,), (1,)), ((), ())), preferred_element_type=jnp.float32)
        ds = (p * (dp - dots)).astype(jnp.bfloat16)
        dq = (query_scale * jnp.dot(ds, k, preferred_element_type=jnp.float32)).astype(jnp.bfloat16)
        dk_s[keys] += lax.dot_general(
            ds, q, (((0,), (0,)), ((), ())), preferred_element_type=jnp.float32
        )
        dv_s[keys] += lax.dot_general(
            pb, g, (((0,), (0,)), ((), ())), preferred_element_type=jnp.float32
        )
        for u in range(2):
            part = slice(u * BLOCK, (u + 1) * BLOCK)
            od_ref[chunk, :, u * HEAD_SIZE : (u + 1) * HEAD_SIZE] = o[part].reshape(
                per, rows, HEAD_SIZE
            )
            od_ref[chunk, :, (2 + u) * HEAD_SIZE : (3 + u) * HEAD_SIZE] = dq[part].reshape(
                per, rows, HEAD_SIZE
            )
    for part, ref in enumerate((g2_ref, g1_ref, g0_ref)):
        own = slice(part * tok, (part + 1) * tok)
        ref[:, :, :HEAD_SIZE] = (
            (query_scale * dk_s[own]).astype(ref.dtype).reshape(n, rows, HEAD_SIZE)
        )
        ref[:, :, HEAD_SIZE:] = dv_s[own].astype(ref.dtype).reshape(n, rows, HEAD_SIZE)


def add_kernel(a_ref, b_ref, o_ref):
    o_ref[...] = (a_ref[...].astype(jnp.float32) + b_ref[...].astype(jnp.float32)).astype(
        jnp.bfloat16
    )


def unpack_kernel(a_ref, x_ref, y_ref):
    n = a_ref.shape[0]
    wide = a_ref.shape[2] // 2
    for i in range(n):
        x_ref[:, i * wide : (i + 1) * wide] = a_ref[i, :, :wide]
        y_ref[:, i * wide : (i + 1) * wide] = a_ref[i, :, wide:]


def call(kernel, outs, args, scratch=(), smem=0):
    return pl.pallas_call(
        kernel,
        out_shape=outs,
        in_specs=[SM] * smem + [VM] * (len(args) - smem),
        out_specs=jax.tree.map(lambda _: VM, outs),
        scratch_shapes=list(scratch),
    )(*args)


def ring(x, by):
    n = lax.axis_size("hi")
    return lax.ppermute(x, "hi", [(i, (i + by) % n) for i in range(n)])


def exchange(x):
    return lax.all_to_all(x, ("lo", "head"), split_axis=0, concat_axis=0, tiled=True)


def body(queries, keys, values, output_gradient, block_lo):
    rows = queries.shape[0]
    n = lax.axis_size("lo") * lax.axis_size("head")
    tok = n * rows
    heads = lax.axis_size("head")
    bf = functools.partial(jax.ShapeDtypeStruct, dtype=jnp.bfloat16)
    f32 = functools.partial(jax.ShapeDtypeStruct, dtype=jnp.float32)
    seq = lax.axis_index("hi") * lax.axis_size("lo") + lax.axis_index("lo")
    base = (seq * block_lo.shape[0]).astype(jnp.int32).reshape(1)

    kv_out = call(pack_kv_kernel, bf((n, rows, 2 * HEAD_SIZE)), (keys, values))
    qg_out = call(
        pack_qg_kernel,
        bf((n, rows + EXTRA, 4 * HEAD_SIZE)),
        (base, block_lo, queries, output_gradient),
        smem=2,
    )
    kv0 = exchange(kv_out)
    kv1 = ring(kv0, 1)
    kv0, qg_out = lax.optimization_barrier((kv0, qg_out))
    qg = exchange(qg_out)
    kv2 = ring(kv1, 1)
    od, g0, g1, g2 = call(
        functools.partial(attention_kernel, heads),
        (
            bf((n, rows, 4 * HEAD_SIZE)),
            f32((n, rows, 2 * HEAD_SIZE)),
            f32((n, rows, 2 * HEAD_SIZE)),
            bf((n, rows, 2 * HEAD_SIZE)),
        ),
        (qg, kv0, kv1, kv2),
        scratch=[
            pltpu.VMEM((3 * tok, HEAD_SIZE), jnp.bfloat16),
            pltpu.VMEM((3 * tok, HEAD_SIZE), jnp.bfloat16),
            pltpu.VMEM((3 * tok, HEAD_SIZE), jnp.float32),
            pltpu.VMEM((3 * tok, HEAD_SIZE), jnp.float32),
        ],
    )
    r1 = ring(g2, -1)
    od_in = exchange(od)
    t = call(add_kernel, bf(g1.shape), (g1, r1))
    r2 = ring(t, -1)
    final = call(add_kernel, bf(g0.shape), (g0, r2))
    g_in = exchange(final)
    attended, query_grads = call(
        unpack_kernel, (bf((rows, 2 * tok // rows * HEAD_SIZE)),) * 2, (od_in,)
    )
    key_grads, value_grads = call(
        unpack_kernel, (bf((rows, tok // rows * HEAD_SIZE)),) * 2, (g_in,)
    )
    return attended, query_grads, key_grads, value_grads


def solution(mesh):
    seq, head = mesh.devices.shape
    kv_heads = 8
    lo = kv_heads // head
    inner = Mesh(mesh.devices.reshape(seq // lo, lo, head), ("hi", "lo", "head"))
    tokens = P(("hi", "lo", "head"), None)
    return jax.shard_map(
        body,
        mesh=inner,
        in_specs=(tokens,) * 4 + (P(("hi", "lo")),),
        out_specs=(tokens,) * 4,
        check_vma=False,
    )
```

time: 173 us -> 74.4 us (0.43)
  the two profiles are of different devices: /device:TPU:2 before, /device:TPU:0 now
where the time goes in v1:
time: 74.4 us; the launch traced here: 73.7 us
  waiting for transfers between devices  22.7 us (31%)
  Pallas kernels  19.2 us (26%)
  starting transfers between devices  17 us (23%)
  blocking collectives  11.3 us (15%)
  local copies, waits for them, and re-layouts  2.82 us (4%)
    pallas_call x7, Pallas kernels, call(): pl.pallas_call(kernel, out_shape=outs, in_specs=[SM] * smem + [VM] * (len...  19.2 us
    ppermute x4, waiting for transfers between devices, ring(): return lax.ppermute(x, 'hi', [(i, (i + by) % n) for i in range(n)])  11.7 us
    all_to_all x1, blocking collectives, exchange(): lax.all_to_all(x, ('lo', 'head'), split_axis=0, concat_axis=0, tiled=True)  11.3 us
    all_to_all x3, waiting for transfers between devices, exchange(): lax.all_to_all(x, ('lo', 'head'), split_axis=0, concat_axis=0, tiled=True)  10.9 us
    all_to_all x3, starting transfers between devices, exchange(): lax.all_to_all(x, ('lo', 'head'), split_axis=0, concat_axis=0, tiled=True)  10.4 us
    ppermute x4, starting transfers between devices, ring(): return lax.ppermute(x, 'hi', [(i, (i + by) % n) for i in range(n)])  6.61 us
    unnamed x16, local copies, waits for them, and re-layouts  2.82 us
  transfers between devices with their start and end apart: 7, of which 6 were waited for; matrix products, arithmetic and copies ran while one was open for 0% of the time, Pallas kernels for 10%

profile of v1, /device:TPU:0, one launch (start us, length us, event | category | flops | bytes accessed | tf_op | source)
XLA Modules:
  0.0 73.7 jit_solution(11031347720261675260)
XLA Ops:
  0.6 1.7 %shard_map.84 = bf16[8,64,256]{2,1,0:T(8,128)(2,1)} custom-call(bf16[64,1024]{1,0:T(8,128)(2,1)} %k_ref.1, bf16[64,1024]{1,0:T(8,128)(2,1)} %v_ref.1), custom_call_target="tpu_custom_call" | custom-call | tf_op jit(solution)/shard_map/pallas_call | solution.py:135
  2.3 11.3 %all_to_all.20.kv0_ref = bf16[8,64,256]{2,1,0:T(8,128)(2,1)S(1)} all-to-all(bf16[8,64,256]{2,1,0:T(8,128)(2,1)} %shard_map.84), channel_id=1, replica_groups=mesh['hi'=4,'lo'=2,'head'=4] {'lo','head'}, dimensions={0} | all-to-all | bytes 524288 | tf_op jit(solution)/shard_map/all_to_all | solution.py:150
  13.7 1.6 %collective-permute-start = (bf16[8,64,256]{2,1,0:T(8,128)(2,1)S(1)}, bf16[8,64,256]{2,1,0:T(8,128)(2,1)S(1)}, u32[]{:S(2)}, u32[]{:S(2)}) collective-permute-start(bf16[8,64,256]{2,1,0:T(8,128)(2,1)S(1)} %all_to_all.20.kv0_ref), channel_id=1, source_target_pairs={{0,8},{8,16},{16,24},{24,0},{1,9},{9,17},{17,25},{25,1},{2,10},{10... | collective-permute-start | bytes 786440 | tf_op jit(solution)/shard_map/ppermute | solution.py:146
  15.2 1.9 %shard_map.85 = bf16[8,72,512]{2,1,0:T(8,128)(2,1)} custom-call(s32[1]{0:T(128)} %bitcast.base_ref, s32[2]{0:T(128)} %lo_ref.1, bf16[64,2048]{1,0:T(8,128)(2,1)} %q_ref.1, bf16[64,2048]{1,0:T(8,128)(2,1)} %g_ref.1), custom_call_target="tpu_custom_call" | custom-call | tf_op jit(solution)/shard_map/pallas_call | solution.py:135
  17.1 0.0 copy-done.3
  17.1 3.5 %all-to-all-start.1 = ((bf16[8,72,512]{2,1,0:T(8,128)(2,1)}), bf16[8,72,512]{2,1,0:T(8,128)(2,1)S(1)}, u32[]{:S(2)}, u32[]{:S(2)}) async-start(bf16[8,72,512]{2,1,0:T(8,128)(2,1)} %shard_map.85), calls=%async_computation.1 | async-start | bytes 1179648 | tf_op jit(solution)/shard_map/all_to_all | solution.py:150
  20.7 2.7 %collective-permute-done.kv1_ref = bf16[8,64,256]{2,1,0:T(8,128)(2,1)S(1)} collective-permute-done((bf16[8,64,256]{2,1,0:T(8,128)(2,1)S(1)}, bf16[8,64,256]{2,1,0:T(8,128)(2,1)S(1)}, u32[]{:S(2)}, u32[]{:S(2)}) %collective-permute-start) | collective-permute-done | bytes 262176 | tf_op jit(solution)/shard_map/ppermute | solution.py:146
  23.4 0.0 copy-start.4
  23.4 0.0 collective-permute-start.1
  23.4 6.8 %all-to-all-done.1.qg_ref = bf16[8,72,512]{2,1,0:T(8,128)(2,1)S(1)} async-done(((bf16[8,72,512]{2,1,0:T(8,128)(2,1)}), bf16[8,72,512]{2,1,0:T(8,128)(2,1)S(1)}, u32[]{:S(2)}, u32[]{:S(2)}) %all-to-all-start.1) | async-done | bytes 589856 | tf_op jit(solution)/shard_map/all_to_all | solution.py:150
  30.2 0.0 copy-start
  30.2 2.1 %collective-permute-done.1.kv2_ref = bf16[8,64,256]{2,1,0:T(8,128)(2,1)S(1)} collective-permute-done((bf16[8,64,256]{2,1,0:T(8,128)(2,1)S(1)}, bf16[8,64,256]{2,1,0:T(8,128)(2,1)S(1)}, u32[]{:S(2)}, u32[]{:S(2)}) %collective-permute-start.1) | collective-permute-done | bytes 262176 | tf_op jit(solution)/shard_map/ppermute | solution.py:146
  32.2 0.0 copy-done.4
  32.3 0.0 copy-done
  32.3 0.7 copy-done.5
  33.0 8.2 %shard_map.86 = (bf16[8,64,512]{2,1,0:T(8,128)(2,1)}, f32[8,64,256]{2,1,0:T(8,128)}, f32[8,64,256]{2,1,0:T(8,128)}, bf16[8,64,256]{2,1,0:T(8,128)(2,1)}) custom-call(bf16[8,72,512]{2,1,0:T(8,128)(2,1)} %copy-done, bf16[8,64,256]{2,1,0:T(8,128)(2,1)} %copy-done.3, bf16[8,64,256]{2,1,0:T(8,128)(2,1)} %copy-done.4, bf16[8,64,256]{2,1,0:T(8,128)(2,1)} %copy-done.5), custom_call_target="tpu_custom_call" | custom-call | tf_op jit(solution)/shard_map/pallas_call | solution.py:135
  41.2 1.0 %collective-permute-start.2 = (bf16[8,64,256]{2,1,0:T(8,128)(2,1)}, bf16[8,64,256]{2,1,0:T(8,128)(2,1)S(1)}, u32[]{:S(2)}, u32[]{:S(2)}) collective-permute-start(bf16[8,64,256]{2,1,0:T(8,128)(2,1)} %get-tuple-element.21), channel_id=1, source_target_pairs={{0,24},{8,0},{16,8},{24,16},{1,25},{9,1},{17,9},{25,17},{2,26},{10... | collective-permute-start | bytes 786440 | tf_op jit(solution)/shard_map/ppermute | solution.py:146
  42.2 3.5 %all-to-all-start.2 = ((bf16[8,64,512]{2,1,0:T(8,128)(2,1)}), bf16[8,64,512]{2,1,0:T(8,128)(2,1)S(1)}, u32[]{:S(2)}, u32[]{:S(2)}) async-start(bf16[8,64,512]{2,1,0:T(8,128)(2,1)} %get-tuple-element.16), calls=%async_computation.2 | async-start | bytes 1048576 | tf_op jit(solution)/shard_map/all_to_all | solution.py:150
  45.7 2.2 %collective-permute-done.2.b_ref = bf16[8,64,256]{2,1,0:T(8,128)(2,1)S(1)} collective-permute-done((bf16[8,64,256]{2,1,0:T(8,128)(2,1)}, bf16[8,64,256]{2,1,0:T(8,128)(2,1)S(1)}, u32[]{:S(2)}, u32[]{:S(2)}) %collective-permute-start.2) | collective-permute-done | bytes 262176 | tf_op jit(solution)/shard_map/ppermute | solution.py:146
  47.9 0.7 copy-done.6
  48.6 1.9 %shard_map.88 = bf16[8,64,256]{2,1,0:T(8,128)(2,1)} custom-call(f32[8,64,256]{2,1,0:T(8,128)} %get-tuple-element.20.a_ref, bf16[8,64,256]{2,1,0:T(8,128)(2,1)} %copy-done.6), custom_call_target="tpu_custom_call" | custom-call | tf_op jit(solution)/shard_map/pallas_call | solution.py:135
  50.5 4.0 %collective-permute-start.3 = (bf16[8,64,256]{2,1,0:T(8,128)(2,1)}, bf16[8,64,256]{2,1,0:T(8,128)(2,1)S(1)}, u32[]{:S(2)}, u32[]{:S(2)}) collective-permute-start(bf16[8,64,256]{2,1,0:T(8,128)(2,1)} %shard_map.88), channel_id=1, source_target_pairs={{0,24},{8,0},{16,8},{24,16},{1,25},{9,1},{17,9},{25,17},{2,26},{10... | collective-permute-start | bytes 786440 | tf_op jit(solution)/shard_map/ppermute | solution.py:146
  54.5 4.8 %collective-permute-done.3.b_ref = bf16[8,64,256]{2,1,0:T(8,128)(2,1)S(1)} collective-permute-done((bf16[8,64,256]{2,1,0:T(8,128)(2,1)}, bf16[8,64,256]{2,1,0:T(8,128)(2,1)S(1)}, u32[]{:S(2)}, u32[]{:S(2)}) %collective-permute-start.3) | collective-permute-done | bytes 262176 | tf_op jit(solution)/shard_map/ppermute | solution.py:146
  59.3 0.7 copy-done.7
  60.0 1.9 %shard_map.89 = bf16[8,64,256]{2,1,0:T(8,128)(2,1)} custom-call(f32[8,64,256]{2,1,0:T(8,128)} %get-tuple-element.19.a_ref, bf16[8,64,256]{2,1,0:T(8,128)(2,1)} %copy-done.7), custom_call_target="tpu_custom_call" | custom-call | tf_op jit(solution)/shard_map/pallas_call | solution.py:135
  61.8 0.0 all-to-all-done.2.a_ref
  61.8 3.4 %all-to-all-start.3 = ((bf16[8,64,256]{2,1,0:T(8,128)(2,1)}), bf16[8,64,256]{2,1,0:T(8,128)(2,1)S(1)}, u32[]{:S(2)}, u32[]{:S(2)}) async-start(bf16[8,64,256]{2,1,0:T(8,128)(2,1)} %shard_map.89), calls=%async_computation.3 | async-start | bytes 524288 | tf_op jit(solution)/shard_map/all_to_all | solution.py:150
  65.3 0.0 copy-done.1
  65.3 1.9 %shard_map.87 = (bf16[64,2048]{1,0:T(8,128)(2,1)}, bf16[64,2048]{1,0:T(8,128)(2,1)}) custom-call(bf16[8,64,512]{2,1,0:T(8,128)(2,1)} %copy-done.1), custom_call_target="tpu_custom_call" | custom-call | tf_op jit(solution)/shard_map/pallas_call | solution.py:135
  67.2 4.2 %all-to-all-done.3.a_ref = bf16[8,64,256]{2,1,0:T(8,128)(2,1)S(1)} async-done(((bf16[8,64,256]{2,1,0:T(8,128)(2,1)}), bf16[8,64,256]{2,1,0:T(8,128)(2,1)S(1)}, u32[]{:S(2)}, u32[]{:S(2)}) %all-to-all-start.3) | async-done | bytes 262176 | tf_op jit(solution)/shard_map/all_to_all | solution.py:150
  71.3 0.7 copy-done.2
  72.0 1.7 %shard_map.90 = (bf16[64,1024]{1,0:T(8,128)(2,1)}, bf16[64,1024]{1,0:T(8,128)(2,1)}) custom-call(bf16[8,64,256]{2,1,0:T(8,128)(2,1)} %copy-done.2), custom_call_target="tpu_custom_call" | custom-call | tf_op jit(solution)/shard_map/pallas_call | solution.py:135
  (6 shorter events, 0.0 us)
Async XLA Ops:
  13.7 3.5 %copy-start.3 = (bf16[8,64,256]{2,1,0:T(8,128)(2,1)}, bf16[8,64,256]{2,1,0:T(8,128)(2,1)S(1)}, u32[]{:S(2)}) copy-start(bf16[8,64,256]{2,1,0:T(8,128)(2,1)S(1)} %all_to_all.20.kv0_ref) | copy-start | bytes 786436
  13.7 9.7 %collective-permute-start = (bf16[8,64,256]{2,1,0:T(8,128)(2,1)S(1)}, bf16[8,64,256]{2,1,0:T(8,128)(2,1)S(1)}, u32[]{:S(2)}, u32[]{:S(2)}) collective-permute-start(bf16[8,64,256]{2,1,0:T(8,128)(2,1)S(1)} %all_to_all.20.kv0_ref), channel_id=1, source_target_pairs={{0,8},{8,16},{16,24},{24,0},{1,9},{9,17},{17,25},{25,1},{2,10},{10... | collective-permute-start | bytes 786440 | tf_op jit(solution)/shard_map/ppermute | solution.py:146
  17.1 13.0 %all-to-all-start.1 = ((bf16[8,72,512]{2,1,0:T(8,128)(2,1)}), bf16[8,72,512]{2,1,0:T(8,128)(2,1)S(1)}, u32[]{:S(2)}, u32[]{:S(2)}) async-start(bf16[8,72,512]{2,1,0:T(8,128)(2,1)} %shard_map.85), calls=%async_computation.1 | async-start | bytes 1179648 | tf_op jit(solution)/shard_map/all_to_all | solution.py:150
  23.4 8.9 %copy-start.4 = (bf16[8,64,256]{2,1,0:T(8,128)(2,1)}, bf16[8,64,256]{2,1,0:T(8,128)(2,1)S(1)}, u32[]{:S(2)}) copy-start(bf16[8,64,256]{2,1,0:T(8,128)(2,1)S(1)} %collective-permute-done.kv1_ref) | copy-start | bytes 786436
  23.4 8.9 %collective-permute-start.1 = (bf16[8,64,256]{2,1,0:T(8,128)(2,1)S(1)}, bf16[8,64,256]{2,1,0:T(8,128)(2,1)S(1)}, u32[]{:S(2)}, u32[]{:S(2)}) collective-permute-start(bf16[8,64,256]{2,1,0:T(8,128)(2,1)S(1)} %collective-permute-done.kv1_ref), channel_id=1, source_target_pairs={{0,8},{8,16},{16,24},{24,0},{1,9},{9,17},{17,25},{25,1},{2,10},{10... | collective-permute-start | bytes 786440 | tf_op jit(solution)/shard_map/ppermute | solution.py:146
  30.2 2.1 %copy-start = (bf16[8,72,512]{2,1,0:T(8,128)(2,1)}, bf16[8,72,512]{2,1,0:T(8,128)(2,1)S(1)}, u32[]{:S(2)}) copy-start(bf16[8,72,512]{2,1,0:T(8,128)(2,1)S(1)} %all-to-all-done.1.qg_ref) | copy-start | bytes 1769476
  32.3 0.7 copy-start.5
  41.2 6.7 %collective-permute-start.2 = (bf16[8,64,256]{2,1,0:T(8,128)(2,1)}, bf16[8,64,256]{2,1,0:T(8,128)(2,1)S(1)}, u32[]{:S(2)}, u32[]{:S(2)}) collective-permute-start(bf16[8,64,256]{2,1,0:T(8,128)(2,1)} %get-tuple-element.21), channel_id=1, source_target_pairs={{0,24},{8,0},{16,8},{24,16},{1,25},{9,1},{17,9},{25,17},{2,26},{10... | collective-permute-start | bytes 786440 | tf_op jit(solution)/shard_map/ppermute | solution.py:146
  42.2 19.7 %all-to-all-start.2 = ((bf16[8,64,512]{2,1,0:T(8,128)(2,1)}), bf16[8,64,512]{2,1,0:T(8,128)(2,1)S(1)}, u32[]{:S(2)}, u32[]{:S(2)}) async-start(bf16[8,64,512]{2,1,0:T(8,128)(2,1)} %get-tuple-element.16), calls=%async_computation.2 | async-start | bytes 1048576 | tf_op jit(solution)/shard_map/all_to_all | solution.py:150
  47.9 0.7 copy-start.6
  50.5 8.8 %collective-permute-start.3 = (bf16[8,64,256]{2,1,0:T(8,128)(2,1)}, bf16[8,64,256]{2,1,0:T(8,128)(2,1)S(1)}, u32[]{:S(2)}, u32[]{:S(2)}) collective-permute-start(bf16[8,64,256]{2,1,0:T(8,128)(2,1)} %shard_map.88), channel_id=1, source_target_pairs={{0,24},{8,0},{16,8},{24,16},{1,25},{9,1},{17,9},{25,17},{2,26},{10... | collective-permute-start | bytes 786440 | tf_op jit(solution)/shard_map/ppermute | solution.py:146
  59.3 0.7 copy-start.7
  61.8 3.4 %copy-start.1 = (bf16[8,64,512]{2,1,0:T(8,128)(2,1)}, bf16[8,64,512]{2,1,0:T(8,128)(2,1)S(1)}, u32[]{:S(2)}) copy-start(bf16[8,64,512]{2,1,0:T(8,128)(2,1)S(1)} %all-to-all-done.2.a_ref) | copy-start | bytes 1572868
  61.8 9.5 %all-to-all-start.3 = ((bf16[8,64,256]{2,1,0:T(8,128)(2,1)}), bf16[8,64,256]{2,1,0:T(8,128)(2,1)S(1)}, u32[]{:S(2)}, u32[]{:S(2)}) async-start(bf16[8,64,256]{2,1,0:T(8,128)(2,1)} %shard_map.89), calls=%async_computation.3 | async-start | bytes 524288 | tf_op jit(solution)/shard_map/all_to_all | solution.py:150
  71.3 0.7 copy-start.2

commit v2 on v1

v2 whole, which is shorter than its diff:
```python
import functools

import jax
import jax.numpy as jnp
from jax import lax
from jax.experimental import pallas as pl
from jax.experimental.pallas import tpu as pltpu
from jax.sharding import Mesh, PartitionSpec as P

HEAD_SIZE = 128
BLOCK = 128
WBLOCKS = 8
LOG2E = 1.4426950408889634

query_scale = 168.0 ** (-0.5)
neg_fill = -1e30
EXTRA = 8

VM = pl.BlockSpec(memory_space=pltpu.VMEM)
SM = pl.BlockSpec(memory_space=pltpu.SMEM)
HB = pl.BlockSpec(memory_space=pl.ANY)


def copy_all(pairs, sems):
    copies = [
        pltpu.make_async_copy(src, dst, sems.at[i]) for i, (src, dst) in enumerate(pairs)
    ]
    for copy in copies:
        copy.start()
    return copies


def pack_kv_kernel(k_ref, v_ref, o_ref, sems):
    pairs = []
    for i in range(o_ref.shape[0]):
        cols = slice(i * HEAD_SIZE, (i + 1) * HEAD_SIZE)
        pairs.append((k_ref.at[:, cols], o_ref.at[i, :, :HEAD_SIZE]))
        pairs.append((v_ref.at[:, cols], o_ref.at[i, :, HEAD_SIZE:]))
    for copy in copy_all(pairs, sems):
        copy.wait()


def pack_qg_kernel(base_ref, lo_ref, q_ref, g_ref, o_ref, sems):
    n, rows, _ = o_ref.shape
    rows -= EXTRA
    wide = q_ref.shape[1] // n
    pairs = []
    for i in range(n):
        cols = slice(i * wide, (i + 1) * wide)
        pairs.append((q_ref.at[:, cols], o_ref.at[i, :rows, :wide]))
        pairs.append((g_ref.at[:, cols], o_ref.at[i, :rows, wide:]))
    copies = copy_all(pairs, sems)
    lane = lax.broadcasted_iota(jnp.int32, (EXTRA, 2 * wide), 1)
    told = jnp.zeros((EXTRA, 2 * wide), jnp.float32)
    for j in range(lo_ref.shape[0]):
        back = (base_ref[0] + j - lo_ref[j]).astype(jnp.float32)
        told = jnp.where(lane // BLOCK == j, back, told)
    for i in range(n):
        o_ref[i, rows:, :] = told.astype(jnp.bfloat16)
    for copy in copies:
        copy.wait()


def stacked(qg_ref, i, rows, first):
    per = BLOCK // rows
    return jnp.concatenate(
        [
            qg_ref[i * per : (i + 1) * per, :rows, j * HEAD_SIZE : (j + 1) * HEAD_SIZE].reshape(
                BLOCK, HEAD_SIZE
            )
            for j in (first, first + 1)
        ],
        axis=0,
    )


def nt(a, b):
    return lax.dot_general(a, b, (((1,), (1,)), ((), ())), preferred_element_type=jnp.float32)


def tn(a, b):
    return lax.dot_general(a, b, (((0,), (0,)), ((), ())), preferred_element_type=jnp.float32)


def nn(a, b):
    return jnp.dot(a, b, preferred_element_type=jnp.float32)


def forward_kernel(head_count, qg_ref, kv0_ref, kv1_ref, kv2_ref,
                   k_s, v_s, o_ref, p_ref, dsf_ref, dots_ref, g2_ref, dk_s, dv_s):
    n, rows, _ = kv0_ref.shape
    tok = n * rows
    blocks = tok // BLOCK
    for part, ref in enumerate((kv2_ref, kv1_ref, kv0_ref)):
        k_s[part * tok : (part + 1) * tok] = ref[:, :, :HEAD_SIZE].reshape(tok, HEAD_SIZE)
        v_s[part * tok : (part + 1) * tok] = ref[:, :, HEAD_SIZE:].reshape(tok, HEAD_SIZE)
    dk_s[...] = jnp.zeros_like(dk_s)
    dv_s[...] = jnp.zeros_like(dv_s)
    span = (WBLOCKS + 1) * BLOCK
    seq_blocks = head_count * rows // BLOCK
    col = lax.broadcasted_iota(jnp.int32, (BLOCK, span), 1)
    row = lax.broadcasted_iota(jnp.int32, (BLOCK, span), 0)
    band = (col > row) & (col <= row + WBLOCKS * BLOCK)
    hi = lax.axis_index("hi")
    for i in range(blocks):
        first = 2 * tok + (i - WBLOCKS) * BLOCK
        keys = slice(first, first + span)
        far = slice(first, tok)
        width = tok - first
        q = stacked(qg_ref, i, rows, 0)
        g = stacked(qg_ref, i, rows, 2)
        owner = (i // seq_blocks) * head_count
        lane = (i % seq_blocks) * BLOCK
        back = qg_ref[owner, rows : rows + 1, lane : lane + 1].astype(jnp.float32)
        least = jnp.maximum(
            (WBLOCKS - back) * BLOCK,
            (WBLOCKS - (hi * blocks + i)).astype(jnp.float32) * BLOCK,
        )
        seen = band & (col.astype(jnp.float32) >= least)
        seen = jnp.concatenate([seen, seen], axis=0)
        s = jnp.where(seen, nt(q, k_s[keys]) * (query_scale * LOG2E), neg_fill)
        e = jnp.exp2(s - jnp.max(s, axis=1, keepdims=True))
        p = e * (1.0 / jnp.sum(e, axis=1, keepdims=True))
        pb = p.astype(jnp.bfloat16)
        o = nn(pb, v_s[keys]).astype(jnp.bfloat16)
        dots = jnp.sum(g.astype(jnp.float32) * o.astype(jnp.float32), axis=1, keepdims=True)
        o_ref[i] = o
        p_ref[i, :, width:] = pb[:, width:]
        dots_ref[i] = jnp.broadcast_to(dots, (2 * BLOCK, HEAD_SIZE))
        ds = (p[:, :width] * (nt(g, v_s[far]) - dots)).astype(jnp.bfloat16)
        dsf_ref[i, :, :width] = ds
        dk_s[far] += tn(ds, q)
        dv_s[far] += tn(pb[:, :width], g)
    g2_ref[:, :, :HEAD_SIZE] = (
        (query_scale * dk_s[...]).astype(jnp.bfloat16).reshape(n, rows, HEAD_SIZE)
    )
    g2_ref[:, :, HEAD_SIZE:] = dv_s[...].astype(jnp.bfloat16).reshape(n, rows, HEAD_SIZE)


def backward_kernel(qg_ref, k_s, v_s, o_ref, p_ref, dsf_ref, dots_ref,
                    od_ref, g1_ref, g0_ref, dk_s, dv_s):
    n, rows, _ = od_ref.shape
    tok = n * rows
    blocks = tok // BLOCK
    per = BLOCK // rows
    dk_s[...] = jnp.zeros_like(dk_s)
    dv_s[...] = jnp.zeros_like(dv_s)
    for i in range(blocks):
        first = 2 * tok + (i - WBLOCKS) * BLOCK
        last = first + (WBLOCKS + 1) * BLOCK
        width = tok - first
        near = slice(tok, last)
        here = slice(0, last - tok)
        q = stacked(qg_ref, i, rows, 0)
        g = stacked(qg_ref, i, rows, 2)
        pb = p_ref[i, :, width:]
        dots = dots_ref[i, :, :1]
        ds = (pb.astype(jnp.float32) * (nt(g, v_s[near]) - dots)).astype(jnp.bfloat16)
        dq = nn(ds, k_s[near]) + nn(dsf_ref[i, :, :width], k_s[first:tok])
        dq = (query_scale * dq).astype(jnp.bfloat16)
        o = o_ref[i]
        dk_s[here] += tn(ds, q)
        dv_s[here] += tn(pb, g)
        chunk = slice(i * per, (i + 1) * per)
        for u in range(2):
            part = slice(u * BLOCK, (u + 1) * BLOCK)
            od_ref[chunk, :, u * HEAD_SIZE : (u + 1) * HEAD_SIZE] = o[part].reshape(
                per, rows, HEAD_SIZE
            )
            od_ref[chunk, :, (2 + u) * HEAD_SIZE : (3 + u) * HEAD_SIZE] = dq[part].reshape(
                per, rows, HEAD_SIZE
            )
    for part, ref in enumerate((g1_ref, g0_ref)):
        own = slice(part * tok, (part + 1) * tok)
        ref[:, :, :HEAD_SIZE] = (query_scale * dk_s[own]).reshape(n, rows, HEAD_SIZE)
        ref[:, :, HEAD_SIZE:] = dv_s[own].reshape(n, rows, HEAD_SIZE)


def add_kernel(a_ref, b_ref, o_ref):
    o_ref[...] = (a_ref[...] + b_ref[...].astype(jnp.float32)).astype(jnp.bfloat16)


def unpack_kernel(a_ref, x_ref, y_ref, sems):
    wide = a_ref.shape[2] // 2
    pairs = []
    for i in range(a_ref.shape[0]):
        cols = slice(i * wide, (i + 1) * wide)
        pairs.append((a_ref.at[i, :, :wide], x_ref.at[:, cols]))
        pairs.append((a_ref.at[i, :, wide:], y_ref.at[:, cols]))
    for copy in copy_all(pairs, sems):
        copy.wait()


def call(kernel, outs, args, scratch=(), smem=0, outer=0, room=2):
    held = [
        x if i < smem + outer else pltpu.with_memory_space_constraint(x, pltpu.VMEM)
        for i, x in enumerate(args)
    ]
    return pl.pallas_call(
        kernel,
        out_shape=outs,
        in_specs=[SM] * smem + [HB] * outer + [VM] * (len(args) - smem - outer),
        out_specs=jax.tree.map(
            lambda o: HB if isinstance(o, jax.ShapeDtypeStruct) else VM,
            outs,
            is_leaf=lambda o: not isinstance(o, tuple),
        ),
        scratch_shapes=list(scratch),
        compiler_params=pltpu.CompilerParams(vmem_limit_bytes=room << 20),
    )(*held)


def ring(x, by):
    n = lax.axis_size("hi")
    return lax.ppermute(x, "hi", [(i, (i + by) % n) for i in range(n)])


def exchange(x):
    return lax.all_to_all(x, ("lo", "head"), split_axis=0, concat_axis=0, tiled=True)


def bf(*shape):
    return pltpu.VMEM(shape, jnp.bfloat16)


def f32(*shape):
    return pltpu.VMEM(shape, jnp.float32)


def out(*shape):
    return jax.ShapeDtypeStruct(shape, jnp.bfloat16)


def body(queries, keys, values, output_gradient, block_lo):
    rows = queries.shape[0]
    n = lax.axis_size("lo") * lax.axis_size("head")
    tok = n * rows
    blocks = tok // BLOCK
    heads = lax.axis_size("head")
    span = (WBLOCKS + 1) * BLOCK
    seq = lax.axis_index("hi") * lax.axis_size("lo") + lax.axis_index("lo")
    base = (seq * block_lo.shape[0]).astype(jnp.int32).reshape(1)
    sems = pltpu.SemaphoreType.DMA((2 * n,))

    kv_out = call(
        pack_kv_kernel, bf(n, rows, 2 * HEAD_SIZE), (keys, values), scratch=[sems], outer=2
    )
    qg_out = call(
        pack_qg_kernel,
        bf(n, rows + EXTRA, 4 * HEAD_SIZE),
        (base, block_lo, queries, output_gradient),
        scratch=[sems],
        smem=2,
        outer=2,
    )
    kv0 = exchange(kv_out)
    kv1 = ring(kv0, 1)
    kv0, qg_out = lax.optimization_barrier((kv0, qg_out))
    qg = exchange(qg_out)
    kv2 = ring(kv1, 1)
    k_all, v_all, o, p, dsf, dots, g2 = call(
        functools.partial(forward_kernel, heads),
        (
            bf(3 * tok, HEAD_SIZE),
            bf(3 * tok, HEAD_SIZE),
            bf(blocks, 2 * BLOCK, HEAD_SIZE),
            bf(blocks, 2 * BLOCK, span),
            bf(blocks, 2 * BLOCK, tok),
            f32(blocks, 2 * BLOCK, HEAD_SIZE),
            bf(n, rows, 2 * HEAD_SIZE),
        ),
        (qg, kv0, kv1, kv2),
        scratch=[f32(tok, HEAD_SIZE), f32(tok, HEAD_SIZE)],
        room=24,
    )
    r1 = ring(g2, -1)
    od, g1, g0 = call(
        backward_kernel,
        (
            bf(n, rows, 4 * HEAD_SIZE),
            f32(n, rows, 2 * HEAD_SIZE),
            f32(n, rows, 2 * HEAD_SIZE),
        ),
        (qg, k_all, v_all, o, p, dsf, dots),
        scratch=[f32(2 * tok, HEAD_SIZE), f32(2 * tok, HEAD_SIZE)],
        room=24,
    )
    od_in = exchange(od)
    t = call(add_kernel, bf(*g1.shape), (g1, r1))
    r2 = ring(t, -1)
    final = call(add_kernel, bf(*g0.shape), (g0, r2))
    g_in = exchange(final)
    attended, query_grads = call(
        unpack_kernel, (out(rows, 2 * n * HEAD_SIZE),) * 2, (od_in,), scratch=[sems]
    )
    key_grads, value_grads = call(
        unpack_kernel, (out(rows, n * HEAD_SIZE),) * 2, (g_in,), scratch=[sems]
    )
    return attended, query_grads, key_grads, value_grads


def solution(mesh):
    seq, head = mesh.devices.shape
    kv_heads = 8
    lo = kv_heads // head
    inner = Mesh(mesh.devices.reshape(seq // lo, lo, head), ("hi", "lo", "head"))
    tokens = P(("hi", "lo", "head"), None)
    return jax.shard_map(
        body,
        mesh=inner,
        in_specs=(tokens,) * 4 + (P(("hi", "lo")),),
        out_specs=(tokens,) * 4,
        check_vma=False,
    )
```

time: 74.4 us -> 66.7 us (0.90)
  Pallas kernels: 19.2 us -> 11.9 us
  waiting for transfers between devices: 22.7 us -> 19.8 us
  local copies, waits for them, and re-layouts: 2.82 us -> 4.35 us
  starting transfers between devices: 17 us -> 18.3 us
    pallas_call x7 -> x8, Pallas kernels: 19.2 us -> 11.9 us  [call(): pl.pallas_call(kernel, out_shape=outs, in_specs=[SM] * smem + [HB] * oute...]
    ppermute x4, waiting for transfers between devices: 11.7 us -> 6.77 us  [ring(): return lax.ppermute(x, 'hi', [(i, (i + by) % n) for i in range(n)])]
    all_to_all x3, waiting for transfers between devices: 10.9 us -> 13 us  [exchange(): lax.all_to_all(x, ('lo', 'head'), split_axis=0, concat_axis=0, tiled=True)]
    unnamed x16 -> x10, local copies, waits for them, and re-layouts: 2.82 us -> 4.35 us
    ppermute x4, starting transfers between devices: 6.61 us -> 7.41 us  [ring(): return lax.ppermute(x, 'hi', [(i, (i + by) % n) for i in range(n)])]
  transfers between devices with their start and end apart: 7 -> 7, of which waited for: 6 -> 5; matrix products, arithmetic and copies ran while one was open for 0% -> 0% of each run, Pallas kernels for 10% -> 9%
where the time goes in v2:
time: 66.7 us; the launch traced here: 66.2 us
  waiting for transfers between devices  19.8 us (30%)
  starting transfers between devices  18.3 us (27%)
  Pallas kernels  11.9 us (18%)
  blocking collectives  11.1 us (17%)
  local copies, waits for them, and re-layouts  4.35 us (7%)
  between operations  0.71 us (1%)
    all_to_all x3, waiting for transfers between devices, exchange(): lax.all_to_all(x, ('lo', 'head'), split_axis=0, concat_axis=0, tiled=True)  13 us
    pallas_call x8, Pallas kernels, call(): pl.pallas_call(kernel, out_shape=outs, in_specs=[SM] * smem + [HB] * oute...  11.9 us
    all_to_all x1, blocking collectives, exchange(): lax.all_to_all(x, ('lo', 'head'), split_axis=0, concat_axis=0, tiled=True)  11.1 us
    all_to_all x3, starting transfers between devices, exchange(): lax.all_to_all(x, ('lo', 'head'), split_axis=0, concat_axis=0, tiled=True)  10.9 us
    ppermute x4, starting transfers between devices, ring(): return lax.ppermute(x, 'hi', [(i, (i + by) % n) for i in range(n)])  7.41 us
    ppermute x4, waiting for transfers between devices, ring(): return lax.ppermute(x, 'hi', [(i, (i + by) % n) for i in range(n)])  6.77 us
    unnamed x10, local copies, waits for them, and re-layouts  4.35 us
  transfers between devices with their start and end apart: 7, of which 5 were waited for; matrix products, arithmetic and copies ran while one was open for 0% of the time, Pallas kernels for 9%

profile of v2, /device:TPU:0, one launch (start us, length us, event | category | flops | bytes accessed | tf_op | source)
XLA Modules:
  0.0 66.2 jit_solution(3212830236507295211)
XLA Ops:
  0.6 0.0 copy-start.2
  0.6 0.9 %copy-done.2 = bf16[64,1024]{1,0:T(8,128)(2,1)S(1)} copy-done((bf16[64,1024]{1,0:T(8,128)(2,1)S(1)}, bf16[64,1024]{1,0:T(8,128)(2,1)}, u32[]{:S(2)}) %copy-start.2) | copy-done | bytes 131096
  1.5 0.0 copy-start.3
  1.5 0.9 %copy-done.3 = bf16[64,1024]{1,0:T(8,128)(2,1)S(1)} copy-done((bf16[64,1024]{1,0:T(8,128)(2,1)S(1)}, bf16[64,1024]{1,0:T(8,128)(2,1)}, u32[]{:S(2)}) %copy-start.3) | copy-done | bytes 131096
  2.4 0.2 shard_map.84
  2.7 11.1 %all_to_all.20.kv0_ref = bf16[8,64,256]{2,1,0:T(8,128)(2,1)S(1)} all-to-all(bf16[8,64,256]{2,1,0:T(8,128)(2,1)S(1)} %shard_map.84), channel_id=1, replica_groups=mesh['hi'=4,'lo'=2,'head'=4] {'lo','head'}, dimensions={0} | all-to-all | bytes 524288 | tf_op jit(solution)/shard_map/all_to_all | solution.py:219
  13.8 1.6 %collective-permute-start = (bf16[8,64,256]{2,1,0:T(8,128)(2,1)S(1)}, bf16[8,64,256]{2,1,0:T(8,128)(2,1)S(1)}, u32[]{:S(2)}, u32[]{:S(2)}) collective-permute-start(bf16[8,64,256]{2,1,0:T(8,128)(2,1)S(1)} %all_to_all.20.kv0_ref), channel_id=1, source_target_pairs={{0,8},{8,16},{16,24},{24,0},{1,9},{9,17},{17,25},{25,1},{2,10},{10... | collective-permute-start | bytes 786440 | tf_op jit(solution)/shard_map/ppermute | solution.py:215
  15.4 0.0 copy-start
  15.4 0.9 %copy-done = bf16[64,2048]{1,0:T(8,128)(2,1)S(1)} copy-done((bf16[64,2048]{1,0:T(8,128)(2,1)S(1)}, bf16[64,2048]{1,0:T(8,128)(2,1)}, u32[]{:S(2)}) %copy-start) | copy-done | bytes 262168
  16.3 0.0 copy-start.1
  16.3 0.9 %copy-done.1 = bf16[64,2048]{1,0:T(8,128)(2,1)S(1)} copy-done((bf16[64,2048]{1,0:T(8,128)(2,1)S(1)}, bf16[64,2048]{1,0:T(8,128)(2,1)}, u32[]{:S(2)}) %copy-start.1) | copy-done | bytes 262168
  17.3 0.0 copy-start.4
  17.3 0.7 copy-done.4
  17.9 1.6 %shard_map.85 = bf16[8,72,512]{2,1,0:T(8,128)(2,1)} custom-call(s32[1]{0:T(128)} %bitcast.base_ref, s32[2]{0:T(128)S(1)} %copy-done.4, bf16[64,2048]{1,0:T(8,128)(2,1)S(1)} %copy-done, bf16[64,2048]{1,0:T(8,128)(2,1)S(1)} %copy-done.1), custom_call_target="tpu_custom_call" | custom-call | tf_op jit(solution)/shard_map/pallas_call | solution.py:199
  19.6 3.5 %all-to-all-start.1 = ((bf16[8,72,512]{2,1,0:T(8,128)(2,1)}), bf16[8,72,512]{2,1,0:T(8,128)(2,1)S(1)}, u32[]{:S(2)}, u32[]{:S(2)}) async-start(bf16[8,72,512]{2,1,0:T(8,128)(2,1)} %shard_map.85), calls=%async_computation.1 | async-start | bytes 1179648 | tf_op jit(solution)/shard_map/all_to_all | solution.py:219
  23.2 0.4 collective-permute-done.kv1_ref
  23.5 1.3 %collective-permute-start.1 = (bf16[8,64,256]{2,1,0:T(8,128)(2,1)S(1)}, bf16[8,64,256]{2,1,0:T(8,128)(2,1)S(1)}, u32[]{:S(2)}, u32[]{:S(2)}) collective-permute-start(bf16[8,64,256]{2,1,0:T(8,128)(2,1)S(1)} %collective-permute-done.kv1_ref), channel_id=1, source_target_pairs={{0,8},{8,16},{16,24},{24,0},{1,9},{9,17},{17,25},{25,1},{2,10},{10... | collective-permute-start | bytes 786440 | tf_op jit(solution)/shard_map/ppermute | solution.py:215
  24.8 7.8 %all-to-all-done.1.qg_ref = bf16[8,72,512]{2,1,0:T(8,128)(2,1)S(1)} async-done(((bf16[8,72,512]{2,1,0:T(8,128)(2,1)}), bf16[8,72,512]{2,1,0:T(8,128)(2,1)S(1)}, u32[]{:S(2)}, u32[]{:S(2)}) %all-to-all-start.1) | async-done | bytes 589856 | tf_op jit(solution)/shard_map/all_to_all | solution.py:219
  32.6 0.9 %collective-permute-done.1.kv2_ref = bf16[8,64,256]{2,1,0:T(8,128)(2,1)S(1)} collective-permute-done((bf16[8,64,256]{2,1,0:T(8,128)(2,1)S(1)}, bf16[8,64,256]{2,1,0:T(8,128)(2,1)S(1)}, u32[]{:S(2)}, u32[]{:S(2)}) %collective-permute-start.1) | collective-permute-done | bytes 262176 | tf_op jit(solution)/shard_map/ppermute | solution.py:215
  33.6 4.6 %shard_map.86 = (bf16[1536,128]{1,0:T(8,128)(2,1)S(1)}, bf16[1536,128]{1,0:T(8,128)(2,1)S(1)}, bf16[4,256,128]{2,1,0:T(8,128)(2,1)S(1)}, bf16[4,256,1152]{2,1,0:...) custom-call(bf16[8,72,512]{2,1,0:T(8,128)(2,1)S(1)} %all-to-all-done, ...), custom_call_target="tpu_custom_call" | custom-call | tf_op jit(solution)/shard_map/pallas_call | solution.py:199
  38.1 1.4 %collective-permute-start.2 = (bf16[8,64,256]{2,1,0:T(8,128)(2,1)S(1)}, bf16[8,64,256]{2,1,0:T(8,128)(2,1)S(1)}, u32[]{:S(2)}, u32[]{:S(2)}) collective-permute-start(bf16[8,64,256]{2,1,0:T(8,128)(2,1)S(1)} %get-tuple-element.33), channel_id=1, source_target_pairs={{0,24},{8,0},{16,8},{24,16},{1,25},{9,1},{17,9},{25,17},{2,26},{10... | collective-permute-start | bytes 786440 | tf_op jit(solution)/shard_map/ppermute | solution.py:215
  39.5 2.9 %shard_map.87 = (bf16[8,64,512]{2,1,0:T(8,128)(2,1)}, f32[8,64,256]{2,1,0:T(8,128)S(1)}, f32[8,64,256]{2,1,0:T(8,128)S(1)}) custom-call(bf16[8,72,512]{2,1,0:T(8,128)(2,1)S(1)} %all-to-all-done.1.qg_ref, bf16[1536,128]{1,0:T(8,128)(2,1)S(1)} %get-tuple-element.22.k_s, bf16[1536,128]{1,0:T(8,128)(2,1)S(1)} %get-tuple-element.23.v_s, ...), custom_call_target="tpu_custom_call" | custom-call | tf_op jit(solution)/shard_map/pallas_call | solution.py:199
  42.4 3.5 %all-to-all-start.2 = ((bf16[8,64,512]{2,1,0:T(8,128)(2,1)}), bf16[8,64,512]{2,1,0:T(8,128)(2,1)S(1)}, u32[]{:S(2)}, u32[]{:S(2)}) async-start(bf16[8,64,512]{2,1,0:T(8,128)(2,1)} %get-tuple-element.28), calls=%async_computation.2 | async-start | bytes 1048576 | tf_op jit(solution)/shard_map/all_to_all | solution.py:219
  45.9 0.0 collective-permute-done.2.b_ref
  46.0 3.2 %collective-permute-start.3 = (bf16[8,64,256]{2,1,0:T(8,128)(2,1)S(1)}, bf16[8,64,256]{2,1,0:T(8,128)(2,1)S(1)}, u32[]{:S(2)}, u32[]{:S(2)}) collective-permute-start(bf16[8,64,256]{2,1,0:T(8,128)(2,1)S(1)} %shard_map.89), channel_id=1, source_target_pairs={{0,24},{8,0},{16,8},{24,16},{1,25},{9,1},{17,9},{25,17},{2,26},{10... | collective-permute-start | bytes 786440 | tf_op jit(solution)/shard_map/ppermute | solution.py:215
  49.2 5.5 %collective-permute-done.3.b_ref = bf16[8,64,256]{2,1,0:T(8,128)(2,1)S(1)} collective-permute-done((bf16[8,64,256]{2,1,0:T(8,128)(2,1)S(1)}, bf16[8,64,256]{2,1,0:T(8,128)(2,1)S(1)}, u32[]{:S(2)}, u32[]{:S(2)}) %collective-permute-start.3) | collective-permute-done | bytes 262176 | tf_op jit(solution)/shard_map/ppermute | solution.py:215
  54.6 0.7 %shard_map.90 = bf16[8,64,256]{2,1,0:T(8,128)(2,1)} custom-call(f32[8,64,256]{2,1,0:T(8,128)S(1)} %get-tuple-element.31.a_ref, bf16[8,64,256]{2,1,0:T(8,128)(2,1)S(1)} %collective-permute-done.3.b_ref), custom_call_target="tpu_custom_call" | custom-call | tf_op jit(solution)/shard_map/pallas_call | solution.py:199
  55.4 0.0 all-to-all-done.2.a_ref
  55.4 3.8 %all-to-all-start.3 = ((bf16[8,64,256]{2,1,0:T(8,128)(2,1)}), bf16[8,64,256]{2,1,0:T(8,128)(2,1)S(1)}, u32[]{:S(2)}, u32[]{:S(2)}) async-start(bf16[8,64,256]{2,1,0:T(8,128)(2,1)} %shard_map.90), calls=%async_computation.3 | async-start | bytes 524288 | tf_op jit(solution)/shard_map/all_to_all | solution.py:219
  59.2 0.9 %shard_map.88 = (bf16[64,2048]{1,0:T(8,128)(2,1)}, bf16[64,2048]{1,0:T(8,128)(2,1)}) custom-call(bf16[8,64,512]{2,1,0:T(8,128)(2,1)S(1)} %all-to-all-done.2.a_ref), custom_call_target="tpu_custom_call" | custom-call | tf_op jit(solution)/shard_map/pallas_call | solution.py:199
  60.2 5.2 %all-to-all-done.3.a_ref = bf16[8,64,256]{2,1,0:T(8,128)(2,1)S(1)} async-done(((bf16[8,64,256]{2,1,0:T(8,128)(2,1)}), bf16[8,64,256]{2,1,0:T(8,128)(2,1)S(1)}, u32[]{:S(2)}, u32[]{:S(2)}) %all-to-all-start.3) | async-done | bytes 262176 | tf_op jit(solution)/shard_map/all_to_all | solution.py:219
  65.4 0.8 %shard_map.91 = (bf16[64,1024]{1,0:T(8,128)(2,1)}, bf16[64,1024]{1,0:T(8,128)(2,1)}) custom-call(bf16[8,64,256]{2,1,0:T(8,128)(2,1)S(1)} %all-to-all-done.3.a_ref), custom_call_target="tpu_custom_call" | custom-call | tf_op jit(solution)/shard_map/pallas_call | solution.py:199
  (1 shorter events, 0.0 us)
Async XLA Ops:
  0.6 0.9 %copy-start.2 = (bf16[64,1024]{1,0:T(8,128)(2,1)S(1)}, bf16[64,1024]{1,0:T(8,128)(2,1)}, u32[]{:S(2)}) copy-start(bf16[64,1024]{1,0:T(8,128)(2,1)} %k_ref.1) | copy-start | bytes 393220
  1.5 0.9 %copy-start.3 = (bf16[64,1024]{1,0:T(8,128)(2,1)S(1)}, bf16[64,1024]{1,0:T(8,128)(2,1)}, u32[]{:S(2)}) copy-start(bf16[64,1024]{1,0:T(8,128)(2,1)} %v_ref.1) | copy-start | bytes 393220
  13.8 9.7 %collective-permute-start = (bf16[8,64,256]{2,1,0:T(8,128)(2,1)S(1)}, bf16[8,64,256]{2,1,0:T(8,128)(2,1)S(1)}, u32[]{:S(2)}, u32[]{:S(2)}) collective-permute-start(bf16[8,64,256]{2,1,0:T(8,128)(2,1)S(1)} %all_to_all.20.kv0_ref), channel_id=1, source_target_pairs={{0,8},{8,16},{16,24},{24,0},{1,9},{9,17},{17,25},{25,1},{2,10},{10... | collective-permute-start | bytes 786440 | tf_op jit(solution)/shard_map/ppermute | solution.py:215
  15.4 0.9 %copy-start = (bf16[64,2048]{1,0:T(8,128)(2,1)S(1)}, bf16[64,2048]{1,0:T(8,128)(2,1)}, u32[]{:S(2)}) copy-start(bf16[64,2048]{1,0:T(8,128)(2,1)} %q_ref.1) | copy-start | bytes 786436
  16.3 0.9 %copy-start.1 = (bf16[64,2048]{1,0:T(8,128)(2,1)S(1)}, bf16[64,2048]{1,0:T(8,128)(2,1)}, u32[]{:S(2)}) copy-start(bf16[64,2048]{1,0:T(8,128)(2,1)} %g_ref.1) | copy-start | bytes 786436
  17.3 0.7 copy-start.4
  19.6 13.0 %all-to-all-start.1 = ((bf16[8,72,512]{2,1,0:T(8,128)(2,1)}), bf16[8,72,512]{2,1,0:T(8,128)(2,1)S(1)}, u32[]{:S(2)}, u32[]{:S(2)}) async-start(bf16[8,72,512]{2,1,0:T(8,128)(2,1)} %shard_map.85), calls=%async_computation.1 | async-start | bytes 1179648 | tf_op jit(solution)/shard_map/all_to_all | solution.py:219
  23.5 10.0 %collective-permute-start.1 = (bf16[8,64,256]{2,1,0:T(8,128)(2,1)S(1)}, bf16[8,64,256]{2,1,0:T(8,128)(2,1)S(1)}, u32[]{:S(2)}, u32[]{:S(2)}) collective-permute-start(bf16[8,64,256]{2,1,0:T(8,128)(2,1)S(1)} %collective-permute-done.kv1_ref), channel_id=1, source_target_pairs={{0,8},{8,16},{16,24},{24,0},{1,9},{9,17},{17,25},{25,1},{2,10},{10... | collective-permute-start | bytes 786440 | tf_op jit(solution)/shard_map/ppermute | solution.py:215
  38.1 7.8 %collective-permute-start.2 = (bf16[8,64,256]{2,1,0:T(8,128)(2,1)S(1)}, bf16[8,64,256]{2,1,0:T(8,128)(2,1)S(1)}, u32[]{:S(2)}, u32[]{:S(2)}) collective-permute-start(bf16[8,64,256]{2,1,0:T(8,128)(2,1)S(1)} %get-tuple-element.33), channel_id=1, source_target_pairs={{0,24},{8,0},{16,8},{24,16},{1,25},{9,1},{17,9},{25,17},{2,26},{10... | collective-permute-start | bytes 786440 | tf_op jit(solution)/shard_map/ppermute | solution.py:215
  42.4 13.0 %all-to-all-start.2 = ((bf16[8,64,512]{2,1,0:T(8,128)(2,1)}), bf16[8,64,512]{2,1,0:T(8,128)(2,1)S(1)}, u32[]{:S(2)}, u32[]{:S(2)}) async-start(bf16[8,64,512]{2,1,0:T(8,128)(2,1)} %get-tuple-element.28), calls=%async_computation.2 | async-start | bytes 1048576 | tf_op jit(solution)/shard_map/all_to_all | solution.py:219
  46.0 8.7 %collective-permute-start.3 = (bf16[8,64,256]{2,1,0:T(8,128)(2,1)S(1)}, bf16[8,64,256]{2,1,0:T(8,128)(2,1)S(1)}, u32[]{:S(2)}, u32[]{:S(2)}) collective-permute-start(bf16[8,64,256]{2,1,0:T(8,128)(2,1)S(1)} %shard_map.89), channel_id=1, source_target_pairs={{0,24},{8,0},{16,8},{24,16},{1,25},{9,1},{17,9},{25,17},{2,26},{10... | collective-permute-start | bytes 786440 | tf_op jit(solution)/shard_map/ppermute | solution.py:215
  55.4 10.0 %all-to-all-start.3 = ((bf16[8,64,256]{2,1,0:T(8,128)(2,1)}), bf16[8,64,256]{2,1,0:T(8,128)(2,1)S(1)}, u32[]{:S(2)}, u32[]{:S(2)}) async-start(bf16[8,64,256]{2,1,0:T(8,128)(2,1)} %shard_map.90), calls=%async_computation.3 | async-start | bytes 524288 | tf_op jit(solution)/shard_map/all_to_all | solution.py:219

commit v3 on v2

--- a/solution.py
+++ b/solution.py
@@ -17,7 +17,6 @@
 EXTRA = 8
 
 VM = pl.BlockSpec(memory_space=pltpu.VMEM)
-SM = pl.BlockSpec(memory_space=pltpu.SMEM)
 HB = pl.BlockSpec(memory_space=pl.ANY)
 
 
@@ -30,34 +29,34 @@
     return copies
 
 
-def pack_kv_kernel(k_ref, v_ref, o_ref, sems):
-    pairs = []
-    for i in range(o_ref.shape[0]):
-        cols = slice(i * HEAD_SIZE, (i + 1) * HEAD_SIZE)
-        pairs.append((k_ref.at[:, cols], o_ref.at[i, :, :HEAD_SIZE]))
-        pairs.append((v_ref.at[:, cols], o_ref.at[i, :, HEAD_SIZE:]))
-    for copy in copy_all(pairs, sems):
-        copy.wait()
-
-
-def pack_qg_kernel(base_ref, lo_ref, q_ref, g_ref, o_ref, sems):
-    n, rows, _ = o_ref.shape
-    rows -= EXTRA
+def pack_kernel(lo_ref, q_ref, k_ref, v_ref, g_ref, kv_ref, qg_ref, told_s, lo_s, lo_sem, sems):
+    n, rows, _ = kv_ref.shape
     wide = q_ref.shape[1] // n
+    fetch = pltpu.make_async_copy(lo_ref, lo_s, lo_sem)
+    fetch.start()
     pairs = []
     for i in range(n):
+        cols = slice(i * HEAD_SIZE, (i + 1) * HEAD_SIZE)
+        pairs.append((k_ref.at[:, cols], kv_ref.at[i, :, :HEAD_SIZE]))
+        pairs.append((v_ref.at[:, cols], kv_ref.at[i, :, HEAD_SIZE:]))
+    for i in range(n):
         cols = slice(i * wide, (i + 1) * wide)
-        pairs.append((q_ref.at[:, cols], o_ref.at[i, :rows, :wide]))
-        pairs.append((g_ref.at[:, cols], o_ref.at[i, :rows, wide:]))
+        pairs.append((q_ref.at[:, cols], qg_ref.at[i, :rows, :wide]))
+        pairs.append((g_ref.at[:, cols], qg_ref.at[i, :rows, wide:]))
     copies = copy_all(pairs, sems)
-    lane = lax.broadcasted_iota(jnp.int32, (EXTRA, 2 * wide), 1)
-    told = jnp.zeros((EXTRA, 2 * wide), jnp.float32)
-    for j in range(lo_ref.shape[0]):
-        back = (base_ref[0] + j - lo_ref[j]).astype(jnp.float32)
+    fetch.wait()
+    shards = lo_ref.shape[0]
+    base = (lax.axis_index("hi") * lax.axis_size("lo") + lax.axis_index("lo")) * shards
+    lane = lax.broadcasted_iota(jnp.int32, told_s.shape, 1)
+    told = jnp.zeros(told_s.shape, jnp.float32)
+    for j in range(shards):
+        back = (base + j - lo_s[j]).astype(jnp.float32)
         told = jnp.where(lane // BLOCK == j, back, told)
-    for i in range(n):
-        o_ref[i, rows:, :] = told.astype(jnp.bfloat16)
-    for copy in copies:
+    told_s[...] = told.astype(jnp.bfloat16)
+    more = copy_all(
+        [(told_s, qg_ref.at[i, rows:, :]) for i in range(n)], sems.at[pl.ds(4 * n, n)]
+    )
+    for copy in copies + more:
         copy.wait()
 
 
@@ -87,7 +86,7 @@
 
 
 def forward_kernel(head_count, qg_ref, kv0_ref, kv1_ref, kv2_ref,
-                   k_s, v_s, o_ref, p_ref, dsf_ref, dots_ref, g2_ref, dk_s, dv_s):
+                   k_s, v_s, o_ref, gs_ref, p_ref, dsf_ref, dots_ref, g2_ref, dk_s, dv_s):
     n, rows, _ = kv0_ref.shape
     tok = n * rows
     blocks = tok // BLOCK
@@ -96,15 +95,14 @@
         v_s[part * tok : (part + 1) * tok] = ref[:, :, HEAD_SIZE:].reshape(tok, HEAD_SIZE)
     dk_s[...] = jnp.zeros_like(dk_s)
     dv_s[...] = jnp.zeros_like(dv_s)
-    span = (WBLOCKS + 1) * BLOCK
     seq_blocks = head_count * rows // BLOCK
-    col = lax.broadcasted_iota(jnp.int32, (BLOCK, span), 1)
-    row = lax.broadcasted_iota(jnp.int32, (BLOCK, span), 0)
-    band = (col > row) & (col <= row + WBLOCKS * BLOCK)
+    col = lax.broadcasted_iota(jnp.int32, (2 * BLOCK, BLOCK), 1)
+    row = lax.broadcasted_iota(jnp.int32, (2 * BLOCK, BLOCK), 0) % BLOCK
     hi = lax.axis_index("hi")
+    scale = query_scale * LOG2E
     for i in range(blocks):
         first = 2 * tok + (i - WBLOCKS) * BLOCK
-        keys = slice(first, first + span)
+        keys = slice(first, first + (WBLOCKS + 1) * BLOCK)
         far = slice(first, tok)
         width = tok - first
         q = stacked(qg_ref, i, rows, 0)
@@ -112,32 +110,42 @@
         owner = (i // seq_blocks) * head_count
         lane = (i % seq_blocks) * BLOCK
         back = qg_ref[owner, rows : rows + 1, lane : lane + 1].astype(jnp.float32)
-        least = jnp.maximum(
-            (WBLOCKS - back) * BLOCK,
-            (WBLOCKS - (hi * blocks + i)).astype(jnp.float32) * BLOCK,
-        )
-        seen = band & (col.astype(jnp.float32) >= least)
-        seen = jnp.concatenate([seen, seen], axis=0)
-        s = jnp.where(seen, nt(q, k_s[keys]) * (query_scale * LOG2E), neg_fill)
-        e = jnp.exp2(s - jnp.max(s, axis=1, keepdims=True))
-        p = e * (1.0 / jnp.sum(e, axis=1, keepdims=True))
-        pb = p.astype(jnp.bfloat16)
-        o = nn(pb, v_s[keys]).astype(jnp.bfloat16)
+        back = jnp.minimum(back, (hi * blocks + i).astype(jnp.float32))
+        s = nt(q, k_s[keys])
+        parts = []
+        for j in range(WBLOCKS + 1):
+            part = s[:, j * BLOCK : (j + 1) * BLOCK]
+            if j == WBLOCKS:
+                part = jnp.where(col <= row, part, neg_fill)
+            else:
+                part = part + jnp.where(back < WBLOCKS - j, neg_fill, 0.0)
+            if j == 0:
+                part = jnp.where(col > row, part, neg_fill)
+            parts.append(part)
+        top = jnp.max(functools.reduce(jnp.maximum, parts), axis=1, keepdims=True)
+        parts = [jnp.exp2((part - top) * scale) for part in parts]
+        share = 1.0 / jnp.sum(functools.reduce(jnp.add, parts), axis=1, keepdims=True)
+        e = jnp.concatenate(parts, axis=1)
+        eb = e.astype(jnp.bfloat16)
+        o = (nn(eb, v_s[keys]) * share).astype(jnp.bfloat16)
         dots = jnp.sum(g.astype(jnp.float32) * o.astype(jnp.float32), axis=1, keepdims=True)
+        dots = dots * share
+        g = (g.astype(jnp.float32) * share).astype(jnp.bfloat16)
         o_ref[i] = o
-        p_ref[i, :, width:] = pb[:, width:]
+        gs_ref[i] = g
+        p_ref[i, :, width:] = eb[:, width:]
         dots_ref[i] = jnp.broadcast_to(dots, (2 * BLOCK, HEAD_SIZE))
-        ds = (p[:, :width] * (nt(g, v_s[far]) - dots)).astype(jnp.bfloat16)
+        ds = (e[:, :width] * (nt(g, v_s[far]) - dots)).astype(jnp.bfloat16)
         dsf_ref[i, :, :width] = ds
         dk_s[far] += tn(ds, q)
-        dv_s[far] += tn(pb[:, :width], g)
+        dv_s[far] += tn(eb[:, :width], g)
     g2_ref[:, :, :HEAD_SIZE] = (
         (query_scale * dk_s[...]).astype(jnp.bfloat16).reshape(n, rows, HEAD_SIZE)
     )
     g2_ref[:, :, HEAD_SIZE:] = dv_s[...].astype(jnp.bfloat16).reshape(n, rows, HEAD_SIZE)
 
 
-def backward_kernel(qg_ref, k_s, v_s, o_ref, p_ref, dsf_ref, dots_ref,
+def backward_kernel(qg_ref, k_s, v_s, o_ref, gs_ref, p_ref, dsf_ref, dots_ref,
                     od_ref, g1_ref, g0_ref, dk_s, dv_s):
     n, rows, _ = od_ref.shape
     tok = n * rows
@@ -152,7 +160,7 @@
         near = slice(tok, last)
         here = slice(0, last - tok)
         q = stacked(qg_ref, i, rows, 0)
-        g = stacked(qg_ref, i, rows, 2)
+        g = gs_ref[i]
         pb = p_ref[i, :, width:]
         dots = dots_ref[i, :, :1]
         ds = (pb.astype(jnp.float32) * (nt(g, v_s[near]) - dots)).astype(jnp.bfloat16)
@@ -180,26 +188,27 @@
     o_ref[...] = (a_ref[...] + b_ref[...].astype(jnp.float32)).astype(jnp.bfloat16)
 
 
-def unpack_kernel(a_ref, x_ref, y_ref, sems):
-    wide = a_ref.shape[2] // 2
+def unpack_kernel(a_ref, b_ref, o_ref, dq_ref, dk_ref, dv_ref, sems):
     pairs = []
-    for i in range(a_ref.shape[0]):
-        cols = slice(i * wide, (i + 1) * wide)
-        pairs.append((a_ref.at[i, :, :wide], x_ref.at[:, cols]))
-        pairs.append((a_ref.at[i, :, wide:], y_ref.at[:, cols]))
+    for ref, left, right in ((a_ref, o_ref, dq_ref), (b_ref, dk_ref, dv_ref)):
+        wide = ref.shape[2] // 2
+        for i in range(ref.shape[0]):
+            cols = slice(i * wide, (i + 1) * wide)
+            pairs.append((ref.at[i, :, :wide], left.at[:, cols]))
+            pairs.append((ref.at[i, :, wide:], right.at[:, cols]))
     for copy in copy_all(pairs, sems):
         copy.wait()
 
 
-def call(kernel, outs, args, scratch=(), smem=0, outer=0, room=2):
+def call(kernel, outs, args, scratch=(), outer=0, room=2):
     held = [
-        x if i < smem + outer else pltpu.with_memory_space_constraint(x, pltpu.VMEM)
+        pltpu.with_memory_space_constraint(x, pltpu.HBM if i < outer else pltpu.VMEM)
         for i, x in enumerate(args)
     ]
     return pl.pallas_call(
         kernel,
         out_shape=outs,
-        in_specs=[SM] * smem + [HB] * outer + [VM] * (len(args) - smem - outer),
+        in_specs=[HB] * outer + [VM] * (len(args) - outer),
         out_specs=jax.tree.map(
             lambda o: HB if isinstance(o, jax.ShapeDtypeStruct) else VM,
             outs,
@@ -238,31 +247,31 @@
     blocks = tok // BLOCK
     heads = lax.axis_size("head")
     span = (WBLOCKS + 1) * BLOCK
-    seq = lax.axis_index("hi") * lax.axis_size("lo") + lax.axis_index("lo")
-    base = (seq * block_lo.shape[0]).astype(jnp.int32).reshape(1)
-    sems = pltpu.SemaphoreType.DMA((2 * n,))
-
-    kv_out = call(
-        pack_kv_kernel, bf(n, rows, 2 * HEAD_SIZE), (keys, values), scratch=[sems], outer=2
-    )
-    qg_out = call(
-        pack_qg_kernel,
-        bf(n, rows + EXTRA, 4 * HEAD_SIZE),
-        (base, block_lo, queries, output_gradient),
-        scratch=[sems],
-        smem=2,
-        outer=2,
+    dma = pltpu.SemaphoreType.DMA
+
+    kv_out, qg_out = call(
+        pack_kernel,
+        (bf(n, rows, 2 * HEAD_SIZE), out(n, rows + EXTRA, 4 * HEAD_SIZE)),
+        (block_lo, queries, keys, values, output_gradient),
+        scratch=[
+            bf(EXTRA, 4 * HEAD_SIZE),
+            pltpu.SMEM(block_lo.shape, jnp.int32),
+            dma,
+            dma((5 * n,)),
+        ],
+        outer=5,
     )
     kv0 = exchange(kv_out)
     kv1 = ring(kv0, 1)
     kv0, qg_out = lax.optimization_barrier((kv0, qg_out))
     qg = exchange(qg_out)
     kv2 = ring(kv1, 1)
-    k_all, v_all, o, p, dsf, dots, g2 = call(
+    k_all, v_all, o, gs, p, dsf, dots, g2 = call(
         functools.partial(forward_kernel, heads),
         (
             bf(3 * tok, HEAD_SIZE),
             bf(3 * tok, HEAD_SIZE),
+            bf(blocks, 2 * BLOCK, HEAD_SIZE),
             bf(blocks, 2 * BLOCK, HEAD_SIZE),
             bf(blocks, 2 * BLOCK, span),
             bf(blocks, 2 * BLOCK, tok),
@@ -281,7 +290,7 @@
             f32(n, rows, 2 * HEAD_SIZE),
             f32(n, rows, 2 * HEAD_SIZE),
         ),
-        (qg, k_all, v_all, o, p, dsf, dots),
+        (qg, k_all, v_all, o, gs, p, dsf, dots),
         scratch=[f32(2 * tok, HEAD_SIZE), f32(2 * tok, HEAD_SIZE)],
         room=24,
     )
@@ -290,13 +299,12 @@
     r2 = ring(t, -1)
     final = call(add_kernel, bf(*g0.shape), (g0, r2))
     g_in = exchange(final)
-    attended, query_grads = call(
-        unpack_kernel, (out(rows, 2 * n * HEAD_SIZE),) * 2, (od_in,), scratch=[sems]
-    )
-    key_grads, value_grads = call(
-        unpack_kernel, (out(rows, n * HEAD_SIZE),) * 2, (g_in,), scratch=[sems]
-    )
-    return attended, query_grads, key_grads, value_grads
+    return call(
+        unpack_kernel,
+        (out(rows, 2 * n * HEAD_SIZE),) * 2 + (out(rows, n * HEAD_SIZE),) * 2,
+        (od_in, g_in),
+        scratch=[dma((4 * n,))],
+    )
 
 
 def solution(mesh):

time: 66.7 us -> 78.8 us (1.18)
  Pallas kernels: 11.9 us -> 25.8 us
  blocking collectives: 11.1 us -> 20.9 us
  starting transfers between devices: 18.3 us -> 10.6 us
  local copies, waits for them, and re-layouts: 4.35 us -> 0 us
    pallas_call x8 -> x6, Pallas kernels: 11.9 us -> 25.8 us  [call(): pl.pallas_call(kernel, out_shape=outs, in_specs=[HB] * outer + [VM] * (le...]
    all_to_all x1 -> x2, blocking collectives: 11.1 us -> 20.9 us  [exchange(): lax.all_to_all(x, ('lo', 'head'), split_axis=0, concat_axis=0, tiled=True)]
    ppermute x4, waiting for transfers between devices: 6.77 us -> 15.6 us  [ring(): return lax.ppermute(x, 'hi', [(i, (i + by) % n) for i in range(n)])]
    all_to_all x3 -> x2, waiting for transfers between devices: 13 us -> 4.89 us  [exchange(): lax.all_to_all(x, ('lo', 'head'), split_axis=0, concat_axis=0, tiled=True)]
    unnamed x10 -> x0, local copies, waits for them, and re-layouts: 4.35 us -> none
    all_to_all x3 -> x2, starting transfers between devices: 10.9 us -> 7.03 us  [exchange(): lax.all_to_all(x, ('lo', 'head'), split_axis=0, concat_axis=0, tiled=True)]
    ppermute x4, starting transfers between devices: 7.41 us -> 3.55 us  [ring(): return lax.ppermute(x, 'hi', [(i, (i + by) % n) for i in range(n)])]
  transfers between devices with their start and end apart: 7 -> 6, of which waited for: 5 -> 4; matrix products, arithmetic and copies ran while one was open for 0% -> 0% of each run, Pallas kernels for 9% -> 4%
where the time goes in v3:
time: 78.8 us; the launch traced here: 78.4 us
  Pallas kernels  25.8 us (33%)
  blocking collectives  20.9 us (27%)
  waiting for transfers between devices  20.5 us (26%)
  starting transfers between devices  10.6 us (13%)
    pallas_call x6, Pallas kernels, call(): pl.pallas_call(kernel, out_shape=outs, in_specs=[HB] * outer + [VM] * (le...  25.8 us
    all_to_all x2, blocking collectives, exchange(): lax.all_to_all(x, ('lo', 'head'), split_axis=0, concat_axis=0, tiled=True)  20.9 us
    ppermute x4, waiting for transfers between devices, ring(): return lax.ppermute(x, 'hi', [(i, (i + by) % n) for i in range(n)])  15.6 us
    all_to_all x2, starting transfers between devices, exchange(): lax.all_to_all(x, ('lo', 'head'), split_axis=0, concat_axis=0, tiled=True)  7.03 us
    all_to_all x2, waiting for transfers between devices, exchange(): lax.all_to_all(x, ('lo', 'head'), split_axis=0, concat_axis=0, tiled=True)  4.89 us
    ppermute x4, starting transfers between devices, ring(): return lax.ppermute(x, 'hi', [(i, (i + by) % n) for i in range(n)])  3.55 us
  transfers between devices with their start and end apart: 6, of which 4 were waited for; matrix products, arithmetic and copies ran while one was open for 0% of the time, Pallas kernels for 4%

profile of v3, /device:TPU:0, one launch (start us, length us, event | category | flops | bytes accessed | tf_op | source)
XLA Modules:
  0.0 78.4 jit_solution(9033633200068205361)
XLA Ops:
  0.6 17.4 %shard_map.84 = (bf16[8,64,256]{2,1,0:T(8,128)(2,1)S(1)}, bf16[8,72,512]{2,1,0:T(8,128)(2,1)}) custom-call(s32[2]{0:T(128)} %lo_ref.1, bf16[64,2048]{1,0:T(8,128)(2,1)} %q_ref.1, bf16[64,1024]{1,0:T(8,128)(2,1)} %k_ref.1, bf16[64,1024]{1,0:T(8,128)(2,1)} %v_ref.1, bf16[64,2048]{1,0:T(8,128)(2,1)} %g_ref.1), custom_call_target="tpu_custom_call" | custom-call | tf_op jit(solution)/shard_map/pallas_call | solution.py:208
  18.0 11.1 %all_to_all.20.kv0_ref = bf16[8,64,256]{2,1,0:T(8,128)(2,1)S(1)} all-to-all(bf16[8,64,256]{2,1,0:T(8,128)(2,1)S(1)} %get-tuple-element.19), channel_id=1, replica_groups=mesh['hi'=4,'lo'=2,'head'=4] {'lo','head'}, dimensions={0} | all-to-all | bytes 524288 | tf_op jit(solution)/shard_map/all_to_all | solution.py:228
  29.1 1.6 %collective-permute-start = (bf16[8,64,256]{2,1,0:T(8,128)(2,1)S(1)}, bf16[8,64,256]{2,1,0:T(8,128)(2,1)S(1)}, u32[]{:S(2)}, u32[]{:S(2)}) collective-permute-start(bf16[8,64,256]{2,1,0:T(8,128)(2,1)S(1)} %all_to_all.20.kv0_ref), channel_id=1, source_target_pairs={{0,8},{8,16},{16,24},{24,0},{1,9},{9,17},{17,25},{25,1},{2,10},{10... | collective-permute-start | bytes 786440 | tf_op jit(solution)/shard_map/ppermute | solution.py:224
  30.7 3.5 %all-to-all-start.1 = ((bf16[8,72,512]{2,1,0:T(8,128)(2,1)}), bf16[8,72,512]{2,1,0:T(8,128)(2,1)S(1)}, u32[]{:S(2)}, u32[]{:S(2)}) async-start(bf16[8,72,512]{2,1,0:T(8,128)(2,1)} %get-tuple-element.21), calls=%async_computation.1 | async-start | bytes 1179648 | tf_op jit(solution)/shard_map/all_to_all | solution.py:228
  34.3 4.6 %collective-permute-done.kv1_ref = bf16[8,64,256]{2,1,0:T(8,128)(2,1)S(1)} collective-permute-done((bf16[8,64,256]{2,1,0:T(8,128)(2,1)S(1)}, bf16[8,64,256]{2,1,0:T(8,128)(2,1)S(1)}, u32[]{:S(2)}, u32[]{:S(2)}) %collective-permute-start) | collective-permute-done | bytes 262176 | tf_op jit(solution)/shard_map/ppermute | solution.py:224
  38.9 0.0 collective-permute-start.1
  38.9 4.9 %all-to-all-done.1.qg_ref = bf16[8,72,512]{2,1,0:T(8,128)(2,1)S(1)} async-done(((bf16[8,72,512]{2,1,0:T(8,128)(2,1)}), bf16[8,72,512]{2,1,0:T(8,128)(2,1)S(1)}, u32[]{:S(2)}, u32[]{:S(2)}) %all-to-all-start.1) | async-done | bytes 589856 | tf_op jit(solution)/shard_map/all_to_all | solution.py:228
  43.7 4.0 %collective-permute-done.1.kv2_ref = bf16[8,64,256]{2,1,0:T(8,128)(2,1)S(1)} collective-permute-done((bf16[8,64,256]{2,1,0:T(8,128)(2,1)S(1)}, bf16[8,64,256]{2,1,0:T(8,128)(2,1)S(1)}, u32[]{:S(2)}, u32[]{:S(2)}) %collective-permute-start.1) | collective-permute-done | bytes 262176 | tf_op jit(solution)/shard_map/ppermute | solution.py:224
  47.7 4.3 %shard_map.85 = (bf16[1536,128]{1,0:T(8,128)(2,1)S(1)}, bf16[1536,128]{1,0:T(8,128)(2,1)S(1)}, bf16[4,256,128]{2,1,0:T(8,128)(2,1)S(1)}, bf16[4,256,128]{2,1,0:T...) custom-call(bf16[8,72,512]{2,1,0:T(8,128)(2,1)S(1)} %all-to-all-done, ...), custom_call_target="tpu_custom_call" | custom-call | tf_op jit(solution)/shard_map/pallas_call | solution.py:208
  52.0 0.1 collective-permute-start.2
  52.1 2.9 %shard_map.86 = (bf16[8,64,512]{2,1,0:T(8,128)(2,1)}, f32[8,64,256]{2,1,0:T(8,128)S(1)}, f32[8,64,256]{2,1,0:T(8,128)S(1)}) custom-call(bf16[8,72,512]{2,1,0:T(8,128)(2,1)S(1)} %all-to-all-done.1.qg_ref, bf16[1536,128]{1,0:T(8,128)(2,1)S(1)} %get-tuple-element.23.k_s, bf16[1536,128]{1,0:T(8,128)(2,1)S(1)} %get-tuple-element.24.v_s, ...), custom_call_target="tpu_custom_call" | custom-call | tf_op jit(solution)/shard_map/pallas_call | solution.py:208
  55.0 3.5 %all-to-all-start.2 = ((bf16[8,64,512]{2,1,0:T(8,128)(2,1)}), bf16[8,64,512]{2,1,0:T(8,128)(2,1)S(1)}, u32[]{:S(2)}, u32[]{:S(2)}) async-start(bf16[8,64,512]{2,1,0:T(8,128)(2,1)} %get-tuple-element.30), calls=%async_computation.2 | async-start | bytes 1048576 | tf_op jit(solution)/shard_map/all_to_all | solution.py:228
  58.5 0.0 collective-permute-done.2.b_ref
  58.5 1.9 %collective-permute-start.3 = (bf16[8,64,256]{2,1,0:T(8,128)(2,1)S(1)}, bf16[8,64,256]{2,1,0:T(8,128)(2,1)S(1)}, u32[]{:S(2)}, u32[]{:S(2)}) collective-permute-start(bf16[8,64,256]{2,1,0:T(8,128)(2,1)S(1)} %shard_map.87), channel_id=1, source_target_pairs={{0,24},{8,0},{16,8},{24,16},{1,25},{9,1},{17,9},{25,17},{2,26},{10... | collective-permute-start | bytes 786440 | tf_op jit(solution)/shard_map/ppermute | solution.py:224
  60.5 7.0 %collective-permute-done.3.b_ref = bf16[8,64,256]{2,1,0:T(8,128)(2,1)S(1)} collective-permute-done((bf16[8,64,256]{2,1,0:T(8,128)(2,1)S(1)}, bf16[8,64,256]{2,1,0:T(8,128)(2,1)S(1)}, u32[]{:S(2)}, u32[]{:S(2)}) %collective-permute-start.3) | collective-permute-done | bytes 262176 | tf_op jit(solution)/shard_map/ppermute | solution.py:224
  67.5 0.0 all-to-all-done.2.a_ref
  67.5 9.8 %all_to_all.21.b_ref = bf16[8,64,256]{2,1,0:T(8,128)(2,1)S(1)} all-to-all(bf16[8,64,256]{2,1,0:T(8,128)(2,1)S(1)} %shard_map.88), channel_id=1, replica_groups=mesh['hi'=4,'lo'=2,'head'=4] {'lo','head'}, dimensions={0} | all-to-all | bytes 524288 | tf_op jit(solution)/shard_map/all_to_all | solution.py:228
  77.3 1.1 %shard_map.89 = (bf16[64,2048]{1,0:T(8,128)(2,1)}, bf16[64,2048]{1,0:T(8,128)(2,1)}, bf16[64,1024]{1,0:T(8,128)(2,1)}, bf16[64,1024]{1,0:T(8,128)(2,1)}) custom-call(bf16[8,64,512]{2,1,0:T(8,128)(2,1)S(1)} %all-to-all-done.2.a_ref, bf16[8,64,256]{2,1,0:T(8,128)(2,1)S(1)} %all_to_all.21.b_ref), custom_call_target="tpu_custom_call" | custom-call | tf_op jit(solution)/shard_map/pallas_call | solution.py:208
  (2 shorter events, 0.1 us)
Async XLA Ops:
  29.1 9.7 %collective-permute-start = (bf16[8,64,256]{2,1,0:T(8,128)(2,1)S(1)}, bf16[8,64,256]{2,1,0:T(8,128)(2,1)S(1)}, u32[]{:S(2)}, u32[]{:S(2)}) collective-permute-start(bf16[8,64,256]{2,1,0:T(8,128)(2,1)S(1)} %all_to_all.20.kv0_ref), channel_id=1, source_target_pairs={{0,8},{8,16},{16,24},{24,0},{1,9},{9,17},{17,25},{25,1},{2,10},{10... | collective-permute-start | bytes 786440 | tf_op jit(solution)/shard_map/ppermute | solution.py:224
  30.7 13.0 %all-to-all-start.1 = ((bf16[8,72,512]{2,1,0:T(8,128)(2,1)}), bf16[8,72,512]{2,1,0:T(8,128)(2,1)S(1)}, u32[]{:S(2)}, u32[]{:S(2)}) async-start(bf16[8,72,512]{2,1,0:T(8,128)(2,1)} %get-tuple-element.21), calls=%async_computation.1 | async-start | bytes 1179648 | tf_op jit(solution)/shard_map/all_to_all | solution.py:228
  38.9 8.9 %collective-permute-start.1 = (bf16[8,64,256]{2,1,0:T(8,128)(2,1)S(1)}, bf16[8,64,256]{2,1,0:T(8,128)(2,1)S(1)}, u32[]{:S(2)}, u32[]{:S(2)}) collective-permute-start(bf16[8,64,256]{2,1,0:T(8,128)(2,1)S(1)} %collective-permute-done.kv1_ref), channel_id=1, source_target_pairs={{0,8},{8,16},{16,24},{24,0},{1,9},{9,17},{17,25},{25,1},{2,10},{10... | collective-permute-start | bytes 786440 | tf_op jit(solution)/shard_map/ppermute | solution.py:224
  52.0 6.5 %collective-permute-start.2 = (bf16[8,64,256]{2,1,0:T(8,128)(2,1)S(1)}, bf16[8,64,256]{2,1,0:T(8,128)(2,1)S(1)}, u32[]{:S(2)}, u32[]{:S(2)}) collective-permute-start(bf16[8,64,256]{2,1,0:T(8,128)(2,1)S(1)} %get-tuple-element.33), channel_id=1, source_target_pairs={{0,24},{8,0},{16,8},{24,16},{1,25},{9,1},{17,9},{25,17},{2,26},{10... | collective-permute-start | bytes 786440 | tf_op jit(solution)/shard_map/ppermute | solution.py:224
  55.0 12.5 %all-to-all-start.2 = ((bf16[8,64,512]{2,1,0:T(8,128)(2,1)}), bf16[8,64,512]{2,1,0:T(8,128)(2,1)S(1)}, u32[]{:S(2)}, u32[]{:S(2)}) async-start(bf16[8,64,512]{2,1,0:T(8,128)(2,1)} %get-tuple-element.30), calls=%async_computation.2 | async-start | bytes 1048576 | tf_op jit(solution)/shard_map/all_to_all | solution.py:228
  58.5 8.9 %collective-permute-start.3 = (bf16[8,64,256]{2,1,0:T(8,128)(2,1)S(1)}, bf16[8,64,256]{2,1,0:T(8,128)(2,1)S(1)}, u32[]{:S(2)}, u32[]{:S(2)}) collective-permute-start(bf16[8,64,256]{2,1,0:T(8,128)(2,1)S(1)} %shard_map.87), channel_id=1, source_target_pairs={{0,24},{8,0},{16,8},{24,16},{1,25},{9,1},{17,9},{25,17},{2,26},{10... | collective-permute-start | bytes 786440 | tf_op jit(solution)/shard_map/ppermute | solution.py:224

commit v4 on v3

--- a/solution.py
+++ b/solution.py
@@ -29,34 +29,36 @@
     return copies
 
 
-def pack_kernel(lo_ref, q_ref, k_ref, v_ref, g_ref, kv_ref, qg_ref, told_s, lo_s, lo_sem, sems):
+def pack_kernel(lo_ref, q_ref, k_ref, v_ref, g_ref, kv_ref, qg_ref, qg_s, lo_s, lo_sem, sems, out_sems):
     n, rows, _ = kv_ref.shape
     wide = q_ref.shape[1] // n
     fetch = pltpu.make_async_copy(lo_ref, lo_s, lo_sem)
     fetch.start()
-    pairs = []
+    kv_pairs, qg_pairs = [], []
     for i in range(n):
         cols = slice(i * HEAD_SIZE, (i + 1) * HEAD_SIZE)
-        pairs.append((k_ref.at[:, cols], kv_ref.at[i, :, :HEAD_SIZE]))
-        pairs.append((v_ref.at[:, cols], kv_ref.at[i, :, HEAD_SIZE:]))
-    for i in range(n):
+        kv_pairs.append((k_ref.at[:, cols], kv_ref.at[i, :, :HEAD_SIZE]))
+        kv_pairs.append((v_ref.at[:, cols], kv_ref.at[i, :, HEAD_SIZE:]))
         cols = slice(i * wide, (i + 1) * wide)
-        pairs.append((q_ref.at[:, cols], qg_ref.at[i, :rows, :wide]))
-        pairs.append((g_ref.at[:, cols], qg_ref.at[i, :rows, wide:]))
-    copies = copy_all(pairs, sems)
+        qg_pairs.append((q_ref.at[:, cols], qg_s.at[i, :rows, :wide]))
+        qg_pairs.append((g_ref.at[:, cols], qg_s.at[i, :rows, wide:]))
+    copies = copy_all(qg_pairs + kv_pairs, sems)
     fetch.wait()
     shards = lo_ref.shape[0]
     base = (lax.axis_index("hi") * lax.axis_size("lo") + lax.axis_index("lo")) * shards
-    lane = lax.broadcasted_iota(jnp.int32, told_s.shape, 1)
-    told = jnp.zeros(told_s.shape, jnp.float32)
+    lane = lax.broadcasted_iota(jnp.int32, (EXTRA, 2 * wide), 1)
+    told = jnp.zeros((EXTRA, 2 * wide), jnp.float32)
     for j in range(shards):
         back = (base + j - lo_s[j]).astype(jnp.float32)
         told = jnp.where(lane // BLOCK == j, back, told)
-    told_s[...] = told.astype(jnp.bfloat16)
-    more = copy_all(
-        [(told_s, qg_ref.at[i, rows:, :]) for i in range(n)], sems.at[pl.ds(4 * n, n)]
-    )
-    for copy in copies + more:
+    outward = []
+    for i in range(n):
+        qg_s[i, rows:, :] = told.astype(jnp.bfloat16)
+        copies[2 * i].wait()
+        copies[2 * i + 1].wait()
+        outward.append(pltpu.make_async_copy(qg_s.at[i], qg_ref.at[i], out_sems.at[i]))
+        outward[i].start()
+    for copy in copies[2 * n :] + outward:
         copy.wait()
 
 
@@ -224,6 +226,12 @@
     return lax.ppermute(x, "hi", [(i, (i + by) % n) for i in range(n)])
 
 
+def relay(x, by):
+    n = lax.axis_size("hi")
+    pairs = [(i, i + 1) for i in range(1, n - 1)]
+    return lax.ppermute(x, "hi", pairs if by == 1 else [(j, i) for i, j in pairs])
+
+
 def exchange(x):
     return lax.all_to_all(x, ("lo", "head"), split_axis=0, concat_axis=0, tiled=True)
 
@@ -254,10 +262,11 @@
         (bf(n, rows, 2 * HEAD_SIZE), out(n, rows + EXTRA, 4 * HEAD_SIZE)),
         (block_lo, queries, keys, values, output_gradient),
         scratch=[
-            bf(EXTRA, 4 * HEAD_SIZE),
+            bf(n, rows + EXTRA, 4 * HEAD_SIZE),
             pltpu.SMEM(block_lo.shape, jnp.int32),
             dma,
-            dma((5 * n,)),
+            dma((4 * n,)),
+            dma((n,)),
         ],
         outer=5,
     )
@@ -265,7 +274,7 @@
     kv1 = ring(kv0, 1)
     kv0, qg_out = lax.optimization_barrier((kv0, qg_out))
     qg = exchange(qg_out)
-    kv2 = ring(kv1, 1)
+    kv2 = relay(kv1, 1)
     k_all, v_all, o, gs, p, dsf, dots, g2 = call(
         functools.partial(forward_kernel, heads),
         (
@@ -282,7 +291,7 @@
         scratch=[f32(tok, HEAD_SIZE), f32(tok, HEAD_SIZE)],
         room=24,
     )
-    r1 = ring(g2, -1)
+    r1 = relay(g2, -1)
     od, g1, g0 = call(
         backward_kernel,
         (

time: 78.8 us -> 64.9 us (0.82)
  Pallas kernels: 25.8 us -> 10.4 us
  starting transfers between devices: 10.6 us -> 17.4 us
  waiting for transfers between devices: 20.5 us -> 14.9 us
    pallas_call x6, Pallas kernels: 25.8 us -> 10.4 us  [call(): pl.pallas_call(kernel, out_shape=outs, in_specs=[HB] * outer + [VM] * (le...]
    ppermute x4 -> x2, starting transfers between devices: 3.55 us -> 9.07 us  [ring(): return lax.ppermute(x, 'hi', [(i, (i + by) % n) for i in range(n)])]
    ppermute x4 -> x2, waiting for transfers between devices: 15.6 us -> 10.7 us  [ring(): return lax.ppermute(x, 'hi', [(i, (i + by) % n) for i in range(n)])]
    ppermute x0 -> x2, starting transfers between devices: none -> 1.34 us  [relay(): lax.ppermute(x, 'hi', pairs if by == 1 else [(j, i) for i, j in pairs])]
  transfers between devices with their start and end apart: 6 -> 6, of which waited for: 4 -> 3; matrix products, arithmetic and copies ran while one was open for 0% -> 0% of each run, Pallas kernels for 4% -> 5%
where the time goes in v4:
time: 64.9 us; the launch traced here: 64.4 us
  blocking collectives  20.9 us (32%)
  starting transfers between devices  17.4 us (27%)
  waiting for transfers between devices  14.9 us (23%)
  Pallas kernels  10.4 us (16%)
  between operations  0.71 us (1%)
    all_to_all x2, blocking collectives, exchange(): lax.all_to_all(x, ('lo', 'head'), split_axis=0, concat_axis=0, tiled=True)  20.9 us
    ppermute x2, waiting for transfers between devices, ring(): return lax.ppermute(x, 'hi', [(i, (i + by) % n) for i in range(n)])  10.7 us
    pallas_call x6, Pallas kernels, call(): pl.pallas_call(kernel, out_shape=outs, in_specs=[HB] * outer + [VM] * (le...  10.4 us
    ppermute x2, starting transfers between devices, ring(): return lax.ppermute(x, 'hi', [(i, (i + by) % n) for i in range(n)])  9.07 us
    all_to_all x2, starting transfers between devices, exchange(): lax.all_to_all(x, ('lo', 'head'), split_axis=0, concat_axis=0, tiled=True)  7.03 us
    all_to_all x2, waiting for transfers between devices, exchange(): lax.all_to_all(x, ('lo', 'head'), split_axis=0, concat_axis=0, tiled=True)  4.21 us
    ppermute x2, starting transfers between devices, relay(): lax.ppermute(x, 'hi', pairs if by == 1 else [(j, i) for i, j in pairs])  1.34 us
  transfers between devices with their start and end apart: 6, of which 3 were waited for; matrix products, arithmetic and copies ran while one was open for 0% of the time, Pallas kernels for 5%

profile of v4, /device:TPU:0, one launch (start us, length us, event | category | flops | bytes accessed | tf_op | source)
XLA Modules:
  0.0 64.4 jit_solution(17741901674911042292)
XLA Ops:
  0.6 2.0 %shard_map.84 = (bf16[8,64,256]{2,1,0:T(8,128)(2,1)S(1)}, bf16[8,72,512]{2,1,0:T(8,128)(2,1)}) custom-call(s32[2]{0:T(128)} %lo_ref.1, bf16[64,2048]{1,0:T(8,128)(2,1)} %q_ref.1, bf16[64,1024]{1,0:T(8,128)(2,1)} %k_ref.1, bf16[64,1024]{1,0:T(8,128)(2,1)} %v_ref.1, bf16[64,2048]{1,0:T(8,128)(2,1)} %g_ref.1), custom_call_target="tpu_custom_call" | custom-call | tf_op jit(solution)/shard_map/pallas_call | solution.py:210
  2.7 11.1 %all_to_all.20.kv0_ref = bf16[8,64,256]{2,1,0:T(8,128)(2,1)S(1)} all-to-all(bf16[8,64,256]{2,1,0:T(8,128)(2,1)S(1)} %get-tuple-element.19), channel_id=1, replica_groups=mesh['hi'=4,'lo'=2,'head'=4] {'lo','head'}, dimensions={0} | all-to-all | bytes 524288 | tf_op jit(solution)/shard_map/all_to_all | solution.py:236
  13.8 1.6 %collective-permute-start = (bf16[8,64,256]{2,1,0:T(8,128)(2,1)S(1)}, bf16[8,64,256]{2,1,0:T(8,128)(2,1)S(1)}, u32[]{:S(2)}, u32[]{:S(2)}) collective-permute-start(bf16[8,64,256]{2,1,0:T(8,128)(2,1)S(1)} %all_to_all.20.kv0_ref), channel_id=1, source_target_pairs={{0,8},{8,16},{16,24},{24,0},{1,9},{9,17},{17,25},{25,1},{2,10},{10... | collective-permute-start | bytes 786440 | tf_op jit(solution)/shard_map/ppermute | solution.py:226
  15.4 3.5 %all-to-all-start.1 = ((bf16[8,72,512]{2,1,0:T(8,128)(2,1)}), bf16[8,72,512]{2,1,0:T(8,128)(2,1)S(1)}, u32[]{:S(2)}, u32[]{:S(2)}) async-start(bf16[8,72,512]{2,1,0:T(8,128)(2,1)} %get-tuple-element.21), calls=%async_computation.1 | async-start | bytes 1179648 | tf_op jit(solution)/shard_map/all_to_all | solution.py:236
  18.9 4.6 %collective-permute-done.kv1_ref = bf16[8,64,256]{2,1,0:T(8,128)(2,1)S(1)} collective-permute-done((bf16[8,64,256]{2,1,0:T(8,128)(2,1)S(1)}, bf16[8,64,256]{2,1,0:T(8,128)(2,1)S(1)}, u32[]{:S(2)}, u32[]{:S(2)}) %collective-permute-start) | collective-permute-done | bytes 262176 | tf_op jit(solution)/shard_map/ppermute | solution.py:226
  23.5 0.7 %collective-permute-start.1 = (bf16[8,64,256]{2,1,0:T(8,128)(2,1)S(1)}, bf16[8,64,256]{2,1,0:T(8,128)(2,1)S(1)}, u32[]{:S(2)}, u32[]{:S(2)}) collective-permute-start(bf16[8,64,256]{2,1,0:T(8,128)(2,1)S(1)} %collective-permute-done.kv1_ref), channel_id=1, source_target_pairs={{8,16},{16,24},{9,17},{17,25},{10,18},{18,26},{11,19},{19,27},{12,... | collective-permute-start | bytes 786440 | tf_op jit(solution)/shard_map/ppermute | solution.py:232
  24.2 4.2 %all-to-all-done.1.qg_ref = bf16[8,72,512]{2,1,0:T(8,128)(2,1)S(1)} async-done(((bf16[8,72,512]{2,1,0:T(8,128)(2,1)}), bf16[8,72,512]{2,1,0:T(8,128)(2,1)S(1)}, u32[]{:S(2)}, u32[]{:S(2)}) %all-to-all-start.1) | async-done | bytes 589856 | tf_op jit(solution)/shard_map/all_to_all | solution.py:236
  28.4 0.0 collective-permute-done.1.kv2_ref
  28.4 4.3 %shard_map.85 = (bf16[1536,128]{1,0:T(8,128)(2,1)S(1)}, bf16[1536,128]{1,0:T(8,128)(2,1)S(1)}, bf16[4,256,128]{2,1,0:T(8,128)(2,1)S(1)}, bf16[4,256,128]{2,1,0:T...) custom-call(bf16[8,72,512]{2,1,0:T(8,128)(2,1)S(1)} %all-to-all-done, ...), custom_call_target="tpu_custom_call" | custom-call | tf_op jit(solution)/shard_map/pallas_call | solution.py:210
  32.7 0.7 %collective-permute-start.2 = (bf16[8,64,256]{2,1,0:T(8,128)(2,1)S(1)}, bf16[8,64,256]{2,1,0:T(8,128)(2,1)S(1)}, u32[]{:S(2)}, u32[]{:S(2)}) collective-permute-start(bf16[8,64,256]{2,1,0:T(8,128)(2,1)S(1)} %get-tuple-element.33), channel_id=1, source_target_pairs={{16,8},{24,16},{17,9},{25,17},{18,10},{26,18},{19,11},{27,19},{20,... | collective-permute-start | bytes 786440 | tf_op jit(solution)/shard_map/ppermute | solution.py:232
  33.4 2.9 %shard_map.86 = (bf16[8,64,512]{2,1,0:T(8,128)(2,1)}, f32[8,64,256]{2,1,0:T(8,128)S(1)}, f32[8,64,256]{2,1,0:T(8,128)S(1)}) custom-call(bf16[8,72,512]{2,1,0:T(8,128)(2,1)S(1)} %all-to-all-done.1.qg_ref, bf16[1536,128]{1,0:T(8,128)(2,1)S(1)} %get-tuple-element.23.k_s, bf16[1536,128]{1,0:T(8,128)(2,1)S(1)} %get-tuple-element.24.v_s, ...), custom_call_target="tpu_custom_call" | custom-call | tf_op jit(solution)/shard_map/pallas_call | solution.py:210
  36.3 3.5 %all-to-all-start.2 = ((bf16[8,64,512]{2,1,0:T(8,128)(2,1)}), bf16[8,64,512]{2,1,0:T(8,128)(2,1)S(1)}, u32[]{:S(2)}, u32[]{:S(2)}) async-start(bf16[8,64,512]{2,1,0:T(8,128)(2,1)} %get-tuple-element.30), calls=%async_computation.2 | async-start | bytes 1048576 | tf_op jit(solution)/shard_map/all_to_all | solution.py:236
  39.8 0.0 collective-permute-done.2.b_ref
  39.8 7.5 %collective-permute-start.3 = (bf16[8,64,256]{2,1,0:T(8,128)(2,1)S(1)}, bf16[8,64,256]{2,1,0:T(8,128)(2,1)S(1)}, u32[]{:S(2)}, u32[]{:S(2)}) collective-permute-start(bf16[8,64,256]{2,1,0:T(8,128)(2,1)S(1)} %shard_map.87), channel_id=1, source_target_pairs={{0,24},{8,0},{16,8},{24,16},{1,25},{9,1},{17,9},{25,17},{2,26},{10... | collective-permute-start | bytes 786440 | tf_op jit(solution)/shard_map/ppermute | solution.py:226
  47.3 6.1 %collective-permute-done.3.b_ref = bf16[8,64,256]{2,1,0:T(8,128)(2,1)S(1)} collective-permute-done((bf16[8,64,256]{2,1,0:T(8,128)(2,1)S(1)}, bf16[8,64,256]{2,1,0:T(8,128)(2,1)S(1)}, u32[]{:S(2)}, u32[]{:S(2)}) %collective-permute-start.3) | collective-permute-done | bytes 262176 | tf_op jit(solution)/shard_map/ppermute | solution.py:226
  53.5 0.0 all-to-all-done.2.a_ref
  53.5 9.8 %all_to_all.21.b_ref = bf16[8,64,256]{2,1,0:T(8,128)(2,1)S(1)} all-to-all(bf16[8,64,256]{2,1,0:T(8,128)(2,1)S(1)} %shard_map.88), channel_id=1, replica_groups=mesh['hi'=4,'lo'=2,'head'=4] {'lo','head'}, dimensions={0} | all-to-all | bytes 524288 | tf_op jit(solution)/shard_map/all_to_all | solution.py:236
  63.3 1.1 %shard_map.89 = (bf16[64,2048]{1,0:T(8,128)(2,1)}, bf16[64,2048]{1,0:T(8,128)(2,1)}, bf16[64,1024]{1,0:T(8,128)(2,1)}, bf16[64,1024]{1,0:T(8,128)(2,1)}) custom-call(bf16[8,64,512]{2,1,0:T(8,128)(2,1)S(1)} %all-to-all-done.2.a_ref, bf16[8,64,256]{2,1,0:T(8,128)(2,1)S(1)} %all_to_all.21.b_ref), custom_call_target="tpu_custom_call" | custom-call | tf_op jit(solution)/shard_map/pallas_call | solution.py:210
  (2 shorter events, 0.1 us)
Async XLA Ops:
  13.8 9.7 %collective-permute-start = (bf16[8,64,256]{2,1,0:T(8,128)(2,1)S(1)}, bf16[8,64,256]{2,1,0:T(8,128)(2,1)S(1)}, u32[]{:S(2)}, u32[]{:S(2)}) collective-permute-start(bf16[8,64,256]{2,1,0:T(8,128)(2,1)S(1)} %all_to_all.20.kv0_ref), channel_id=1, source_target_pairs={{0,8},{8,16},{16,24},{24,0},{1,9},{9,17},{17,25},{25,1},{2,10},{10... | collective-permute-start | bytes 786440 | tf_op jit(solution)/shard_map/ppermute | solution.py:226
  15.4 13.0 %all-to-all-start.1 = ((bf16[8,72,512]{2,1,0:T(8,128)(2,1)}), bf16[8,72,512]{2,1,0:T(8,128)(2,1)S(1)}, u32[]{:S(2)}, u32[]{:S(2)}) async-start(bf16[8,72,512]{2,1,0:T(8,128)(2,1)} %get-tuple-element.21), calls=%async_computation.1 | async-start | bytes 1179648 | tf_op jit(solution)/shard_map/all_to_all | solution.py:236
  23.5 4.9 %collective-permute-start.1 = (bf16[8,64,256]{2,1,0:T(8,128)(2,1)S(1)}, bf16[8,64,256]{2,1,0:T(8,128)(2,1)S(1)}, u32[]{:S(2)}, u32[]{:S(2)}) collective-permute-start(bf16[8,64,256]{2,1,0:T(8,128)(2,1)S(1)} %collective-permute-done.kv1_ref), channel_id=1, source_target_pairs={{8,16},{16,24},{9,17},{17,25},{10,18},{18,26},{11,19},{19,27},{12,... | collective-permute-start | bytes 786440 | tf_op jit(solution)/shard_map/ppermute | solution.py:232
  32.7 7.1 %collective-permute-start.2 = (bf16[8,64,256]{2,1,0:T(8,128)(2,1)S(1)}, bf16[8,64,256]{2,1,0:T(8,128)(2,1)S(1)}, u32[]{:S(2)}, u32[]{:S(2)}) collective-permute-start(bf16[8,64,256]{2,1,0:T(8,128)(2,1)S(1)} %get-tuple-element.33), channel_id=1, source_target_pairs={{16,8},{24,16},{17,9},{25,17},{18,10},{26,18},{19,11},{27,19},{20,... | collective-permute-start | bytes 786440 | tf_op jit(solution)/shard_map/ppermute | solution.py:232
  36.3 17.2 %all-to-all-start.2 = ((bf16[8,64,512]{2,1,0:T(8,128)(2,1)}), bf16[8,64,512]{2,1,0:T(8,128)(2,1)S(1)}, u32[]{:S(2)}, u32[]{:S(2)}) async-start(bf16[8,64,512]{2,1,0:T(8,128)(2,1)} %get-tuple-element.30), calls=%async_computation.2 | async-start | bytes 1048576 | tf_op jit(solution)/shard_map/all_to_all | solution.py:236
  39.8 13.6 %collective-permute-start.3 = (bf16[8,64,256]{2,1,0:T(8,128)(2,1)S(1)}, bf16[8,64,256]{2,1,0:T(8,128)(2,1)S(1)}, u32[]{:S(2)}, u32[]{:S(2)}) collective-permute-start(bf16[8,64,256]{2,1,0:T(8,128)(2,1)S(1)} %shard_map.87), channel_id=1, source_target_pairs={{0,24},{8,0},{16,8},{24,16},{1,25},{9,1},{17,9},{25,17},{2,26},{10... | collective-permute-start | bytes 786440 | tf_op jit(solution)/shard_map/ppermute | solution.py:226

commit v5 on v4

--- a/solution.py
+++ b/solution.py
@@ -87,67 +87,137 @@
     return jnp.dot(a, b, preferred_element_type=jnp.float32)
 
 
-def forward_kernel(head_count, qg_ref, kv0_ref, kv1_ref, kv2_ref,
-                   k_s, v_s, o_ref, gs_ref, p_ref, dsf_ref, dots_ref, g2_ref, dk_s, dv_s):
+def spread(a, b):
+    lane = lax.broadcasted_iota(jnp.int32, (a.shape[0], HEAD_SIZE), 1)
+    return jnp.where(lane < HEAD_SIZE // 2, a, b)
+
+
+def softmax_parts(s, cols, back, scale):
+    col = lax.broadcasted_iota(jnp.int32, (2 * BLOCK, BLOCK), 1)
+    row = lax.broadcasted_iota(jnp.int32, (2 * BLOCK, BLOCK), 0) % BLOCK
+    parts = []
+    for at, j in enumerate(cols):
+        part = s[:, at * BLOCK : (at + 1) * BLOCK]
+        if j == WBLOCKS:
+            part = jnp.where(col <= row, part, neg_fill)
+        else:
+            part = part + jnp.where(back < WBLOCKS - j, neg_fill, 0.0)
+        if j == 0:
+            part = jnp.where(col > row, part, neg_fill)
+        parts.append(part)
+    top = jnp.max(functools.reduce(jnp.maximum, parts), axis=1, keepdims=True)
+    parts = [jnp.exp2((part - top) * scale) for part in parts]
+    total = jnp.sum(functools.reduce(jnp.add, parts), axis=1, keepdims=True)
+    return jnp.concatenate(parts, axis=1), top, total
+
+
+def blocks_back(qg_ref, i, rows, head_count):
+    blocks = qg_ref.shape[0] * rows // BLOCK
+    seq_blocks = head_count * rows // BLOCK
+    owner = (i // seq_blocks) * head_count
+    lane = (i % seq_blocks) * BLOCK
+    back = qg_ref[owner, rows : rows + 1, lane : lane + 1].astype(jnp.float32)
+    return jnp.minimum(back, (lax.axis_index("hi") * blocks + i).astype(jnp.float32))
+
+
+def near_kernel(head_count, qg_ref, kv0_ref, kv1_ref, k_s, v_s, o_ref, p_ref, stat_ref):
     n, rows, _ = kv0_ref.shape
     tok = n * rows
     blocks = tok // BLOCK
-    for part, ref in enumerate((kv2_ref, kv1_ref, kv0_ref)):
+    for part, ref in enumerate((kv1_ref, kv0_ref)):
         k_s[part * tok : (part + 1) * tok] = ref[:, :, :HEAD_SIZE].reshape(tok, HEAD_SIZE)
         v_s[part * tok : (part + 1) * tok] = ref[:, :, HEAD_SIZE:].reshape(tok, HEAD_SIZE)
-    dk_s[...] = jnp.zeros_like(dk_s)
-    dv_s[...] = jnp.zeros_like(dv_s)
-    seq_blocks = head_count * rows // BLOCK
-    col = lax.broadcasted_iota(jnp.int32, (2 * BLOCK, BLOCK), 1)
-    row = lax.broadcasted_iota(jnp.int32, (2 * BLOCK, BLOCK), 0) % BLOCK
+
+    def step(i, start):
+        keys = slice(start, tok + (i + 1) * BLOCK)
+        count = keys.stop // BLOCK - start // BLOCK
+        back = blocks_back(qg_ref, i, rows, head_count)
+        s = nt(stacked(qg_ref, i, rows, 0), k_s[keys])
+        e, top, total = softmax_parts(
+            s, range(WBLOCKS + 1 - count, WBLOCKS + 1), back, query_scale * LOG2E
+        )
+        eb = e.astype(jnp.bfloat16)
+        o_ref[i] = nn(eb, v_s[keys])
+        p_ref[i, :, keys] = eb
+        stat_ref[i] = spread(top, total)
+
     hi = lax.axis_index("hi")
+
+    @pl.when(hi == 0)
+    def _():
+        for i in range(blocks):
+            step(i, tok)
+
+    @pl.when(hi > 0)
+    def _():
+        for i in range(blocks):
+            step(i, 0)
+
+
+def far_kernel(head_count, qg_ref, kv2_ref, near_ref, stat_ref,
+               k_s, o_ref, gs_ref, dsf_ref, dots_ref, g2_ref, v_s, dk_s, dv_s):
+    n, rows, _ = kv2_ref.shape
+    tok = n * rows
+    blocks = tok // BLOCK
     scale = query_scale * LOG2E
-    for i in range(blocks):
-        first = 2 * tok + (i - WBLOCKS) * BLOCK
-        keys = slice(first, first + (WBLOCKS + 1) * BLOCK)
-        far = slice(first, tok)
-        width = tok - first
+
+    def step(i, far_seen):
         q = stacked(qg_ref, i, rows, 0)
-        g = stacked(qg_ref, i, rows, 2)
-        owner = (i // seq_blocks) * head_count
-        lane = (i % seq_blocks) * BLOCK
-        back = qg_ref[owner, rows : rows + 1, lane : lane + 1].astype(jnp.float32)
-        back = jnp.minimum(back, (hi * blocks + i).astype(jnp.float32))
-        s = nt(q, k_s[keys])
-        parts = []
-        for j in range(WBLOCKS + 1):
-            part = s[:, j * BLOCK : (j + 1) * BLOCK]
-            if j == WBLOCKS:
-                part = jnp.where(col <= row, part, neg_fill)
-            else:
-                part = part + jnp.where(back < WBLOCKS - j, neg_fill, 0.0)
-            if j == 0:
-                part = jnp.where(col > row, part, neg_fill)
-            parts.append(part)
-        top = jnp.max(functools.reduce(jnp.maximum, parts), axis=1, keepdims=True)
-        parts = [jnp.exp2((part - top) * scale) for part in parts]
-        share = 1.0 / jnp.sum(functools.reduce(jnp.add, parts), axis=1, keepdims=True)
-        e = jnp.concatenate(parts, axis=1)
-        eb = e.astype(jnp.bfloat16)
-        o = (nn(eb, v_s[keys]) * share).astype(jnp.bfloat16)
-        dots = jnp.sum(g.astype(jnp.float32) * o.astype(jnp.float32), axis=1, keepdims=True)
-        dots = dots * share
-        g = (g.astype(jnp.float32) * share).astype(jnp.bfloat16)
+        g = stacked(qg_ref, i, rows, 2).astype(jnp.float32)
+        top = stat_ref[i, :, :1]
+        total = stat_ref[i, :, HEAD_SIZE // 2 : HEAD_SIZE // 2 + 1]
+        if far_seen:
+            far = slice(i * BLOCK, tok)
+            width = tok - i * BLOCK
+            back = blocks_back(qg_ref, i, rows, head_count)
+            s = nt(q, k_s[far])
+            e, far_top, far_total = softmax_parts(s, range(width // BLOCK), back, scale)
+            eb = e.astype(jnp.bfloat16)
+            most = jnp.maximum(top, far_top)
+            near = jnp.exp2((top - most) * scale)
+            away = jnp.exp2((far_top - most) * scale)
+            share = 1.0 / (near * total + away * far_total)
+            near = near * share
+            away = away * share
+            o = near_ref[i] * near + nn(eb, v_s[far]) * away
+        else:
+            near = 1.0 / total
+            o = near_ref[i] * near
+        o = o.astype(jnp.bfloat16)
+        dots = jnp.sum(g * o.astype(jnp.float32), axis=1, keepdims=True)
         o_ref[i] = o
-        gs_ref[i] = g
-        p_ref[i, :, width:] = eb[:, width:]
-        dots_ref[i] = jnp.broadcast_to(dots, (2 * BLOCK, HEAD_SIZE))
-        ds = (e[:, :width] * (nt(g, v_s[far]) - dots)).astype(jnp.bfloat16)
-        dsf_ref[i, :, :width] = ds
-        dk_s[far] += tn(ds, q)
-        dv_s[far] += tn(eb[:, :width], g)
-    g2_ref[:, :, :HEAD_SIZE] = (
-        (query_scale * dk_s[...]).astype(jnp.bfloat16).reshape(n, rows, HEAD_SIZE)
-    )
-    g2_ref[:, :, HEAD_SIZE:] = dv_s[...].astype(jnp.bfloat16).reshape(n, rows, HEAD_SIZE)
-
-
-def backward_kernel(qg_ref, k_s, v_s, o_ref, gs_ref, p_ref, dsf_ref, dots_ref,
+        gs_ref[i] = (g * near).astype(jnp.bfloat16)
+        dots_ref[i] = jnp.broadcast_to(dots * near, (2 * BLOCK, HEAD_SIZE))
+        if far_seen:
+            g = (g * away).astype(jnp.bfloat16)
+            ds = (e * (nt(g, v_s[far]) - dots * away)).astype(jnp.bfloat16)
+            dsf_ref[i, :, :width] = ds
+            dk_s[far] += tn(ds, q)
+            dv_s[far] += tn(eb, g)
+
+    hi = lax.axis_index("hi")
+
+    @pl.when(hi == 0)
+    def _():
+        for i in range(blocks):
+            step(i, False)
+        g2_ref[...] = jnp.zeros_like(g2_ref)
+
+    @pl.when(hi > 0)
+    def _():
+        k_s[...] = kv2_ref[:, :, :HEAD_SIZE].reshape(tok, HEAD_SIZE)
+        v_s[...] = kv2_ref[:, :, HEAD_SIZE:].reshape(tok, HEAD_SIZE)
+        dk_s[...] = jnp.zeros_like(dk_s)
+        dv_s[...] = jnp.zeros_like(dv_s)
+        for i in range(blocks):
+            step(i, True)
+        g2_ref[:, :, :HEAD_SIZE] = (
+            (query_scale * dk_s[...]).astype(jnp.bfloat16).reshape(n, rows, HEAD_SIZE)
+        )
+        g2_ref[:, :, HEAD_SIZE:] = dv_s[...].astype(jnp.bfloat16).reshape(n, rows, HEAD_SIZE)
+
+
+def backward_kernel(qg_ref, k_s, v_s, kf_ref, o_ref, gs_ref, p_ref, dsf_ref, dots_ref,
                     od_ref, g1_ref, g0_ref, dk_s, dv_s):
     n, rows, _ = od_ref.shape
     tok = n * rows
@@ -155,22 +225,21 @@
     per = BLOCK // rows
     dk_s[...] = jnp.zeros_like(dk_s)
     dv_s[...] = jnp.zeros_like(dv_s)
-    for i in range(blocks):
-        first = 2 * tok + (i - WBLOCKS) * BLOCK
-        last = first + (WBLOCKS + 1) * BLOCK
-        width = tok - first
-        near = slice(tok, last)
-        here = slice(0, last - tok)
+
+    def step(i, own_only):
+        near = slice(tok if own_only else 0, tok + (i + 1) * BLOCK)
         q = stacked(qg_ref, i, rows, 0)
         g = gs_ref[i]
-        pb = p_ref[i, :, width:]
+        pb = p_ref[i, :, near]
         dots = dots_ref[i, :, :1]
         ds = (pb.astype(jnp.float32) * (nt(g, v_s[near]) - dots)).astype(jnp.bfloat16)
-        dq = nn(ds, k_s[near]) + nn(dsf_ref[i, :, :width], k_s[first:tok])
+        dq = nn(ds, k_s[near])
+        if not own_only:
+            dq = dq + nn(dsf_ref[i, :, : tok - i * BLOCK], kf_ref[i * BLOCK :])
         dq = (query_scale * dq).astype(jnp.bfloat16)
         o = o_ref[i]
-        dk_s[here] += tn(ds, q)
-        dv_s[here] += tn(pb, g)
+        dk_s[near] += tn(ds, q)
+        dv_s[near] += tn(pb, g)
         chunk = slice(i * per, (i + 1) * per)
         for u in range(2):
             part = slice(u * BLOCK, (u + 1) * BLOCK)
@@ -180,6 +249,19 @@
             od_ref[chunk, :, (2 + u) * HEAD_SIZE : (3 + u) * HEAD_SIZE] = dq[part].reshape(
                 per, rows, HEAD_SIZE
             )
+
+    hi = lax.axis_index("hi")
+
+    @pl.when(hi == 0)
+    def _():
+        for i in range(blocks):
+            step(i, True)
+
+    @pl.when(hi > 0)
+    def _():
+        for i in range(blocks):
+            step(i, False)
+
     for part, ref in enumerate((g1_ref, g0_ref)):
         own = slice(part * tok, (part + 1) * tok)
         ref[:, :, :HEAD_SIZE] = (query_scale * dk_s[own]).reshape(n, rows, HEAD_SIZE)
@@ -226,10 +308,9 @@
     return lax.ppermute(x, "hi", [(i, (i + by) % n) for i in range(n)])
 
 
-def relay(x, by):
+def relay(x):
     n = lax.axis_size("hi")
-    pairs = [(i, i + 1) for i in range(1, n - 1)]
-    return lax.ppermute(x, "hi", pairs if by == 1 else [(j, i) for i, j in pairs])
+    return lax.ppermute(x, "hi", [(i, i + 1) for i in range(1, n - 1)])
 
 
 def exchange(x):
@@ -254,7 +335,6 @@
     tok = n * rows
     blocks = tok // BLOCK
     heads = lax.axis_size("head")
-    span = (WBLOCKS + 1) * BLOCK
     dma = pltpu.SemaphoreType.DMA
 
     kv_out, qg_out = call(
@@ -274,24 +354,34 @@
     kv1 = ring(kv0, 1)
     kv0, qg_out = lax.optimization_barrier((kv0, qg_out))
     qg = exchange(qg_out)
-    kv2 = relay(kv1, 1)
-    k_all, v_all, o, gs, p, dsf, dots, g2 = call(
-        functools.partial(forward_kernel, heads),
+    kv2 = relay(kv1)
+    k_all, v_all, near, p, stat = call(
+        functools.partial(near_kernel, heads),
         (
-            bf(3 * tok, HEAD_SIZE),
-            bf(3 * tok, HEAD_SIZE),
+            bf(2 * tok, HEAD_SIZE),
+            bf(2 * tok, HEAD_SIZE),
+            f32(blocks, 2 * BLOCK, HEAD_SIZE),
+            bf(blocks, 2 * BLOCK, 2 * tok),
+            f32(blocks, 2 * BLOCK, HEAD_SIZE),
+        ),
+        (qg, kv0, kv1),
+        room=20,
+    )
+    k_far, o, gs, dsf, dots, g2 = call(
+        functools.partial(far_kernel, heads),
+        (
+            bf(tok, HEAD_SIZE),
             bf(blocks, 2 * BLOCK, HEAD_SIZE),
             bf(blocks, 2 * BLOCK, HEAD_SIZE),
-            bf(blocks, 2 * BLOCK, span),
             bf(blocks, 2 * BLOCK, tok),
             f32(blocks, 2 * BLOCK, HEAD_SIZE),
             bf(n, rows, 2 * HEAD_SIZE),
         ),
-        (qg, kv0, kv1, kv2),
-        scratch=[f32(tok, HEAD_SIZE), f32(tok, HEAD_SIZE)],
-        room=24,
-    )
-    r1 = relay(g2, -1)
+        (qg, kv2, near, stat),
+        scratch=[bf(tok, HEAD_SIZE), f32(tok, HEAD_SIZE), f32(tok, HEAD_SIZE)],
+        room=20,
+    )
+    r1 = ring(g2, -1)
     od, g1, g0 = call(
         backward_kernel,
         (
@@ -299,7 +389,7 @@
             f32(n, rows, 2 * HEAD_SIZE),
             f32(n, rows, 2 * HEAD_SIZE),
         ),
-        (qg, k_all, v_all, o, gs, p, dsf, dots),
+        (qg, k_all, v_all, k_far, o, gs, p, dsf, dots),
         scratch=[f32(2 * tok, HEAD_SIZE), f32(2 * tok, HEAD_SIZE)],
         room=24,
     )

time: 64.9 us -> 63.4 us (0.977)
  Pallas kernels: 10.4 us -> 7.74 us
  starting transfers between devices: 17.4 us -> 18.6 us
    pallas_call x6 -> x7, Pallas kernels: 10.4 us -> 7.74 us  [call(): pl.pallas_call(kernel, out_shape=outs, in_specs=[HB] * outer + [VM] * (le...]
    ppermute x2 -> x3, starting transfers between devices: 9.07 us -> 11 us  [ring(): return lax.ppermute(x, 'hi', [(i, (i + by) % n) for i in range(n)])]
    ppermute x2 -> x1, starting transfers between devices: 1.34 us -> 0.67 us  [relay(): return lax.ppermute(x, 'hi', [(i, i + 1) for i in range(1, n - 1)])]
    ppermute x2 -> x3, waiting for transfers between devices: 10.7 us -> 10.7 us  [ring(): return lax.ppermute(x, 'hi', [(i, (i + by) % n) for i in range(n)])]
  transfers between devices with their start and end apart: 6 -> 6, of which waited for: 3 -> 3; matrix products, arithmetic and copies ran while one was open for 0% -> 0% of each run, Pallas kernels for 5% -> 6%
where the time goes in v5:
time: 63.4 us; the launch traced here: 62.9 us
  blocking collectives  20.9 us (33%)
  starting transfers between devices  18.6 us (29%)
  waiting for transfers between devices  15 us (24%)
  Pallas kernels  7.74 us (12%)
  between operations  0.71 us (1%)
    all_to_all x2, blocking collectives, exchange(): lax.all_to_all(x, ('lo', 'head'), split_axis=0, concat_axis=0, tiled=True)  20.9 us
    ppermute x3, starting transfers between devices, ring(): return lax.ppermute(x, 'hi', [(i, (i + by) % n) for i in range(n)])  11 us
    ppermute x3, waiting for transfers between devices, ring(): return lax.ppermute(x, 'hi', [(i, (i + by) % n) for i in range(n)])  10.7 us
    pallas_call x7, Pallas kernels, call(): pl.pallas_call(kernel, out_shape=outs, in_specs=[HB] * outer + [VM] * (le...  7.74 us
    all_to_all x2, starting transfers between devices, exchange(): lax.all_to_all(x, ('lo', 'head'), split_axis=0, concat_axis=0, tiled=True)  7.03 us
    all_to_all x2, waiting for transfers between devices, exchange(): lax.all_to_all(x, ('lo', 'head'), split_axis=0, concat_axis=0, tiled=True)  4.22 us
  transfers between devices with their start and end apart: 6, of which 3 were waited for; matrix products, arithmetic and copies ran while one was open for 0% of the time, Pallas kernels for 6%

profile of v5, /device:TPU:0, one launch (start us, length us, event | category | flops | bytes accessed | tf_op | source)
XLA Modules:
  0.0 62.9 jit_solution(28621658400850271)
XLA Ops:
  0.6 2.0 %shard_map.84 = (bf16[8,64,256]{2,1,0:T(8,128)(2,1)S(1)}, bf16[8,72,512]{2,1,0:T(8,128)(2,1)}) custom-call(s32[2]{0:T(128)} %lo_ref.1, bf16[64,2048]{1,0:T(8,128)(2,1)} %q_ref.1, bf16[64,1024]{1,0:T(8,128)(2,1)} %k_ref.1, bf16[64,1024]{1,0:T(8,128)(2,1)} %v_ref.1, bf16[64,2048]{1,0:T(8,128)(2,1)} %g_ref.1), custom_call_target="tpu_custom_call" | custom-call | tf_op jit(solution)/shard_map/pallas_call | solution.py:292
  2.7 11.1 %all_to_all.20.kv0_ref = bf16[8,64,256]{2,1,0:T(8,128)(2,1)S(1)} all-to-all(bf16[8,64,256]{2,1,0:T(8,128)(2,1)S(1)} %get-tuple-element.22), channel_id=1, replica_groups=mesh['hi'=4,'lo'=2,'head'=4] {'lo','head'}, dimensions={0} | all-to-all | bytes 524288 | tf_op jit(solution)/shard_map/all_to_all | solution.py:317
  13.8 1.6 %collective-permute-start = (bf16[8,64,256]{2,1,0:T(8,128)(2,1)S(1)}, bf16[8,64,256]{2,1,0:T(8,128)(2,1)S(1)}, u32[]{:S(2)}, u32[]{:S(2)}) collective-permute-start(bf16[8,64,256]{2,1,0:T(8,128)(2,1)S(1)} %all_to_all.20.kv0_ref), channel_id=1, source_target_pairs={{0,8},{8,16},{16,24},{24,0},{1,9},{9,17},{17,25},{25,1},{2,10},{10... | collective-permute-start | bytes 786440 | tf_op jit(solution)/shard_map/ppermute | solution.py:308
  15.4 3.5 %all-to-all-start.1 = ((bf16[8,72,512]{2,1,0:T(8,128)(2,1)}), bf16[8,72,512]{2,1,0:T(8,128)(2,1)S(1)}, u32[]{:S(2)}, u32[]{:S(2)}) async-start(bf16[8,72,512]{2,1,0:T(8,128)(2,1)} %get-tuple-element.24), calls=%async_computation.1 | async-start | bytes 1179648 | tf_op jit(solution)/shard_map/all_to_all | solution.py:317
  18.9 4.6 %collective-permute-done.kv1_ref = bf16[8,64,256]{2,1,0:T(8,128)(2,1)S(1)} collective-permute-done((bf16[8,64,256]{2,1,0:T(8,128)(2,1)S(1)}, bf16[8,64,256]{2,1,0:T(8,128)(2,1)S(1)}, u32[]{:S(2)}, u32[]{:S(2)}) %collective-permute-start) | collective-permute-done | bytes 262176 | tf_op jit(solution)/shard_map/ppermute | solution.py:308
  23.5 0.7 %collective-permute-start.1 = (bf16[8,64,256]{2,1,0:T(8,128)(2,1)S(1)}, bf16[8,64,256]{2,1,0:T(8,128)(2,1)S(1)}, u32[]{:S(2)}, u32[]{:S(2)}) collective-permute-start(bf16[8,64,256]{2,1,0:T(8,128)(2,1)S(1)} %collective-permute-done.kv1_ref), channel_id=1, source_target_pairs={{8,16},{16,24},{9,17},{17,25},{10,18},{18,26},{11,19},{19,27},{12,... | collective-permute-start | bytes 786440 | tf_op jit(solution)/shard_map/ppermute | solution.py:313
  24.2 4.2 %all-to-all-done.1.qg_ref = bf16[8,72,512]{2,1,0:T(8,128)(2,1)S(1)} async-done(((bf16[8,72,512]{2,1,0:T(8,128)(2,1)}), bf16[8,72,512]{2,1,0:T(8,128)(2,1)S(1)}, u32[]{:S(2)}, u32[]{:S(2)}) %all-to-all-start.1) | async-done | bytes 589856 | tf_op jit(solution)/shard_map/all_to_all | solution.py:317
  28.4 1.4 %shard_map.85 = (bf16[1024,128]{1,0:T(8,128)(2,1)S(1)}, bf16[1024,128]{1,0:T(8,128)(2,1)S(1)}, f32[4,256,128]{2,1,0:T(8,128)S(1)}, bf16[4,256,1024]{2,1,0:T(8,128)(2,1)S(1)}, f32[4,256,128]{2,1,0:T(8,128)S(1)}) custom-call(bf16[8,72,512]{2,1,0:T(8,128)(2,1)S(1)} %all-to-all-done.1.qg_ref, bf16[8,64,256]{2,1,0:T(8,128)(2,1)S(1)} %all_to_all.20.kv0_ref, ...), custom_call_target="tpu_custom_call" | custom-call | tf_op jit(solution)/shard_map/pallas_call | solution.py:292
  29.8 0.0 collective-permute-done.1.kv2_ref
  29.8 0.8 %shard_map.86 = (bf16[512,128]{1,0:T(8,128)(2,1)S(1)}, bf16[4,256,128]{2,1,0:T(8,128)(2,1)S(1)}, bf16[4,256,128]{2,1,0:T(8,128)(2,1)S(1)}, bf16[4,256,512]{2,1,0...) custom-call(bf16[8,72,512]{2,1,0:T(8,128)(2,1)S(1)} %all-to-all-done.1.qg_ref, ...), custom_call_target="tpu_custom_call" | custom-call | tf_op jit(solution)/shard_map/pallas_call | solution.py:292
  30.6 6.9 %collective-permute-start.2 = (bf16[8,64,256]{2,1,0:T(8,128)(2,1)S(1)}, bf16[8,64,256]{2,1,0:T(8,128)(2,1)S(1)}, u32[]{:S(2)}, u32[]{:S(2)}) collective-permute-start(bf16[8,64,256]{2,1,0:T(8,128)(2,1)S(1)} %get-tuple-element.39), channel_id=1, source_target_pairs={{0,24},{8,0},{16,8},{24,16},{1,25},{9,1},{17,9},{25,17},{2,26},{10... | collective-permute-start | bytes 786440 | tf_op jit(solution)/shard_map/ppermute | solution.py:308
  37.4 2.3 %shard_map.87 = (bf16[8,64,512]{2,1,0:T(8,128)(2,1)}, f32[8,64,256]{2,1,0:T(8,128)S(1)}, f32[8,64,256]{2,1,0:T(8,128)S(1)}) custom-call(bf16[8,72,512]{2,1,0:T(8,128)(2,1)S(1)} %all-to-all-done.1.qg_ref, bf16[1024,128]{1,0:T(8,128)(2,1)S(1)} %get-tuple-element.26.k_s, bf16[1024,128]{1,0:T(8,128)(2,1)S(1)} %get-tuple-element.27.v_s, ...), custom_call_target="tpu_custom_call" | custom-call | tf_op jit(solution)/shard_map/pallas_call | solution.py:292
  39.8 3.5 %all-to-all-start.2 = ((bf16[8,64,512]{2,1,0:T(8,128)(2,1)}), bf16[8,64,512]{2,1,0:T(8,128)(2,1)S(1)}, u32[]{:S(2)}, u32[]{:S(2)}) async-start(bf16[8,64,512]{2,1,0:T(8,128)(2,1)} %get-tuple-element.36), calls=%async_computation.2 | async-start | bytes 1048576 | tf_op jit(solution)/shard_map/all_to_all | solution.py:317
  43.3 0.0 collective-permute-done.2.b_ref
  43.3 2.5 %collective-permute-start.3 = (bf16[8,64,256]{2,1,0:T(8,128)(2,1)S(1)}, bf16[8,64,256]{2,1,0:T(8,128)(2,1)S(1)}, u32[]{:S(2)}, u32[]{:S(2)}) collective-permute-start(bf16[8,64,256]{2,1,0:T(8,128)(2,1)S(1)} %shard_map.88), channel_id=1, source_target_pairs={{0,24},{8,0},{16,8},{24,16},{1,25},{9,1},{17,9},{25,17},{2,26},{10... | collective-permute-start | bytes 786440 | tf_op jit(solution)/shard_map/ppermute | solution.py:308
  45.8 6.1 %collective-permute-done.3.b_ref = bf16[8,64,256]{2,1,0:T(8,128)(2,1)S(1)} collective-permute-done((bf16[8,64,256]{2,1,0:T(8,128)(2,1)S(1)}, bf16[8,64,256]{2,1,0:T(8,128)(2,1)S(1)}, u32[]{:S(2)}, u32[]{:S(2)}) %collective-permute-start.3) | collective-permute-done | bytes 262176 | tf_op jit(solution)/shard_map/ppermute | solution.py:308
  52.0 0.0 all-to-all-done.2.a_ref
  52.0 9.8 %all_to_all.21.b_ref = bf16[8,64,256]{2,1,0:T(8,128)(2,1)S(1)} all-to-all(bf16[8,64,256]{2,1,0:T(8,128)(2,1)S(1)} %shard_map.89), channel_id=1, replica_groups=mesh['hi'=4,'lo'=2,'head'=4] {'lo','head'}, dimensions={0} | all-to-all | bytes 524288 | tf_op jit(solution)/shard_map/all_to_all | solution.py:317
  61.8 1.1 %shard_map.90 = (bf16[64,2048]{1,0:T(8,128)(2,1)}, bf16[64,2048]{1,0:T(8,128)(2,1)}, bf16[64,1024]{1,0:T(8,128)(2,1)}, bf16[64,1024]{1,0:T(8,128)(2,1)}) custom-call(bf16[8,64,512]{2,1,0:T(8,128)(2,1)S(1)} %all-to-all-done.2.a_ref, bf16[8,64,256]{2,1,0:T(8,128)(2,1)S(1)} %all_to_all.21.b_ref), custom_call_target="tpu_custom_call" | custom-call | tf_op jit(solution)/shard_map/pallas_call | solution.py:292
  (2 shorter events, 0.1 us)
Async XLA Ops:
  13.8 9.7 %collective-permute-start = (bf16[8,64,256]{2,1,0:T(8,128)(2,1)S(1)}, bf16[8,64,256]{2,1,0:T(8,128)(2,1)S(1)}, u32[]{:S(2)}, u32[]{:S(2)}) collective-permute-start(bf16[8,64,256]{2,1,0:T(8,128)(2,1)S(1)} %all_to_all.20.kv0_ref), channel_id=1, source_target_pairs={{0,8},{8,16},{16,24},{24,0},{1,9},{9,17},{17,25},{25,1},{2,10},{10... | collective-permute-start | bytes 786440 | tf_op jit(solution)/shard_map/ppermute | solution.py:308
  15.4 13.0 %all-to-all-start.1 = ((bf16[8,72,512]{2,1,0:T(8,128)(2,1)}), bf16[8,72,512]{2,1,0:T(8,128)(2,1)S(1)}, u32[]{:S(2)}, u32[]{:S(2)}) async-start(bf16[8,72,512]{2,1,0:T(8,128)(2,1)} %get-tuple-element.24), calls=%async_computation.1 | async-start | bytes 1179648 | tf_op jit(solution)/shard_map/all_to_all | solution.py:317
  23.5 6.3 %collective-permute-start.1 = (bf16[8,64,256]{2,1,0:T(8,128)(2,1)S(1)}, bf16[8,64,256]{2,1,0:T(8,128)(2,1)S(1)}, u32[]{:S(2)}, u32[]{:S(2)}) collective-permute-start(bf16[8,64,256]{2,1,0:T(8,128)(2,1)S(1)} %collective-permute-done.kv1_ref), channel_id=1, source_target_pairs={{8,16},{16,24},{9,17},{17,25},{10,18},{18,26},{11,19},{19,27},{12,... | collective-permute-start | bytes 786440 | tf_op jit(solution)/shard_map/ppermute | solution.py:313
  30.6 12.7 %collective-permute-start.2 = (bf16[8,64,256]{2,1,0:T(8,128)(2,1)S(1)}, bf16[8,64,256]{2,1,0:T(8,128)(2,1)S(1)}, u32[]{:S(2)}, u32[]{:S(2)}) collective-permute-start(bf16[8,64,256]{2,1,0:T(8,128)(2,1)S(1)} %get-tuple-element.39), channel_id=1, source_target_pairs={{0,24},{8,0},{16,8},{24,16},{1,25},{9,1},{17,9},{25,17},{2,26},{10... | collective-permute-start | bytes 786440 | tf_op jit(solution)/shard_map/ppermute | solution.py:308
  39.8 12.3 %all-to-all-start.2 = ((bf16[8,64,512]{2,1,0:T(8,128)(2,1)}), bf16[8,64,512]{2,1,0:T(8,128)(2,1)S(1)}, u32[]{:S(2)}, u32[]{:S(2)}) async-start(bf16[8,64,512]{2,1,0:T(8,128)(2,1)} %get-tuple-element.36), calls=%async_computation.2 | async-start | bytes 1048576 | tf_op jit(solution)/shard_map/all_to_all | solution.py:317
  43.3 8.7 %collective-permute-start.3 = (bf16[8,64,256]{2,1,0:T(8,128)(2,1)S(1)}, bf16[8,64,256]{2,1,0:T(8,128)(2,1)S(1)}, u32[]{:S(2)}, u32[]{:S(2)}) collective-permute-start(bf16[8,64,256]{2,1,0:T(8,128)(2,1)S(1)} %shard_map.88), channel_id=1, source_target_pairs={{0,24},{8,0},{16,8},{24,16},{1,25},{9,1},{17,9},{25,17},{2,26},{10... | collective-permute-start | bytes 786440 | tf_op jit(solution)/shard_map/ppermute | solution.py:308

commit v6 on v5

--- a/solution.py
+++ b/solution.py
@@ -308,9 +308,10 @@
     return lax.ppermute(x, "hi", [(i, (i + by) % n) for i in range(n)])
 
 
-def relay(x):
+def line(x, by, least=0):
     n = lax.axis_size("hi")
-    return lax.ppermute(x, "hi", [(i, i + 1) for i in range(1, n - 1)])
+    pairs = [(i, i + 1) for i in range(least, n - 1)]
+    return lax.ppermute(x, "hi", pairs if by == 1 else [(j, i) for i, j in pairs])
 
 
 def exchange(x):
@@ -354,7 +355,7 @@
     kv1 = ring(kv0, 1)
     kv0, qg_out = lax.optimization_barrier((kv0, qg_out))
     qg = exchange(qg_out)
-    kv2 = relay(kv1)
+    kv2 = line(kv1, 1, 1)
     k_all, v_all, near, p, stat = call(
         functools.partial(near_kernel, heads),
         (
@@ -381,7 +382,7 @@
         scratch=[bf(tok, HEAD_SIZE), f32(tok, HEAD_SIZE), f32(tok, HEAD_SIZE)],
         room=20,
     )
-    r1 = ring(g2, -1)
+    r1 = line(g2, -1, 1)
     od, g1, g0 = call(
         backward_kernel,
         (
@@ -395,7 +396,7 @@
     )
     od_in = exchange(od)
     t = call(add_kernel, bf(*g1.shape), (g1, r1))
-    r2 = ring(t, -1)
+    r2 = line(t, -1)
     final = call(add_kernel, bf(*g0.shape), (g0, r2))
     g_in = exchange(final)
     return call(

time: 63.4 us -> 63.5 us (level)
  waiting for transfers between devices: 15 us -> 22.6 us
  starting transfers between devices: 18.6 us -> 11.2 us
    ppermute x1 -> x3, waiting for transfers between devices: 0.01 us -> 13.8 us  [line(): lax.ppermute(x, 'hi', pairs if by == 1 else [(j, i) for i, j in pairs])]
    ppermute x3 -> x1, starting transfers between devices: 11 us -> 1.58 us  [ring(): return lax.ppermute(x, 'hi', [(i, (i + by) % n) for i in range(n)])]
    ppermute x3 -> x1, waiting for transfers between devices: 10.7 us -> 4.6 us  [ring(): return lax.ppermute(x, 'hi', [(i, (i + by) % n) for i in range(n)])]
    ppermute x1 -> x3, starting transfers between devices: 0.67 us -> 2.64 us  [line(): lax.ppermute(x, 'hi', pairs if by == 1 else [(j, i) for i, j in pairs])]
where the time goes in v6:
time: 63.5 us; the launch traced here: 63 us
  waiting for transfers between devices  22.6 us (36%)
  blocking collectives  20.7 us (33%)
  starting transfers between devices  11.2 us (18%)
  Pallas kernels  7.74 us (12%)
  between operations  0.73 us (1%)
    all_to_all x2, blocking collectives, exchange(): lax.all_to_all(x, ('lo', 'head'), split_axis=0, concat_axis=0, tiled=True)  20.7 us
    ppermute x3, waiting for transfers between devices, line(): lax.ppermute(x, 'hi', pairs if by == 1 else [(j, i) for i, j in pairs])  13.8 us
    pallas_call x7, Pallas kernels, call(): pl.pallas_call(kernel, out_shape=outs, in_specs=[HB] * outer + [VM] * (le...  7.74 us
    all_to_all x2, starting transfers between devices, exchange(): lax.all_to_all(x, ('lo', 'head'), split_axis=0, concat_axis=0, tiled=True)  7.03 us
    ppermute x1, waiting for transfers between devices, ring(): return lax.ppermute(x, 'hi', [(i, (i + by) % n) for i in range(n)])  4.6 us
    all_to_all x2, waiting for transfers between devices, exchange(): lax.all_to_all(x, ('lo', 'head'), split_axis=0, concat_axis=0, tiled=True)  4.21 us
    ppermute x3, starting transfers between devices, line(): lax.ppermute(x, 'hi', pairs if by == 1 else [(j, i) for i, j in pairs])  2.64 us
    ppermute x1, starting transfers between devices, ring(): return lax.ppermute(x, 'hi', [(i, (i + by) % n) for i in range(n)])  1.58 us
  transfers between devices with their start and end apart: 6, of which 3 were waited for; matrix products, arithmetic and copies ran while one was open for 0% of the time, Pallas kernels for 6%

profile of v6, /device:TPU:0, one launch (start us, length us, event | category | flops | bytes accessed | tf_op | source)
XLA Modules:
  0.0 63.0 jit_solution(12152678043532380525)
XLA Ops:
  0.6 2.0 %shard_map.84 = (bf16[8,64,256]{2,1,0:T(8,128)(2,1)S(1)}, bf16[8,72,512]{2,1,0:T(8,128)(2,1)}) custom-call(s32[2]{0:T(128)} %lo_ref.1, bf16[64,2048]{1,0:T(8,128)(2,1)} %q_ref.1, bf16[64,1024]{1,0:T(8,128)(2,1)} %k_ref.1, bf16[64,1024]{1,0:T(8,128)(2,1)} %v_ref.1, bf16[64,2048]{1,0:T(8,128)(2,1)} %g_ref.1), custom_call_target="tpu_custom_call" | custom-call | tf_op jit(solution)/shard_map/pallas_call | solution.py:292
  2.7 11.1 %all_to_all.20.kv0_ref = bf16[8,64,256]{2,1,0:T(8,128)(2,1)S(1)} all-to-all(bf16[8,64,256]{2,1,0:T(8,128)(2,1)S(1)} %get-tuple-element.22), channel_id=1, replica_groups=mesh['hi'=4,'lo'=2,'head'=4] {'lo','head'}, dimensions={0} | all-to-all | bytes 524288 | tf_op jit(solution)/shard_map/all_to_all | solution.py:318
  13.8 1.6 %collective-permute-start = (bf16[8,64,256]{2,1,0:T(8,128)(2,1)S(1)}, bf16[8,64,256]{2,1,0:T(8,128)(2,1)S(1)}, u32[]{:S(2)}, u32[]{:S(2)}) collective-permute-start(bf16[8,64,256]{2,1,0:T(8,128)(2,1)S(1)} %all_to_all.20.kv0_ref), channel_id=1, source_target_pairs={{0,8},{8,16},{16,24},{24,0},{1,9},{9,17},{17,25},{25,1},{2,10},{10... | collective-permute-start | bytes 786440 | tf_op jit(solution)/shard_map/ppermute | solution.py:308
  15.4 3.5 %all-to-all-start.1 = ((bf16[8,72,512]{2,1,0:T(8,128)(2,1)}), bf16[8,72,512]{2,1,0:T(8,128)(2,1)S(1)}, u32[]{:S(2)}, u32[]{:S(2)}) async-start(bf16[8,72,512]{2,1,0:T(8,128)(2,1)} %get-tuple-element.24), calls=%async_computation.1 | async-start | bytes 1179648 | tf_op jit(solution)/shard_map/all_to_all | solution.py:318
  18.9 4.6 %collective-permute-done.kv1_ref = bf16[8,64,256]{2,1,0:T(8,128)(2,1)S(1)} collective-permute-done((bf16[8,64,256]{2,1,0:T(8,128)(2,1)S(1)}, bf16[8,64,256]{2,1,0:T(8,128)(2,1)S(1)}, u32[]{:S(2)}, u32[]{:S(2)}) %collective-permute-start) | collective-permute-done | bytes 262176 | tf_op jit(solution)/shard_map/ppermute | solution.py:308
  23.5 0.7 %collective-permute-start.1 = (bf16[8,64,256]{2,1,0:T(8,128)(2,1)S(1)}, bf16[8,64,256]{2,1,0:T(8,128)(2,1)S(1)}, u32[]{:S(2)}, u32[]{:S(2)}) collective-permute-start(bf16[8,64,256]{2,1,0:T(8,128)(2,1)S(1)} %collective-permute-done.kv1_ref), channel_id=1, source_target_pairs={{8,16},{16,24},{9,17},{17,25},{10,18},{18,26},{11,19},{19,27},{12,... | collective-permute-start | bytes 786440 | tf_op jit(solution)/shard_map/ppermute | solution.py:314
  24.2 4.2 %all-to-all-done.1.qg_ref = bf16[8,72,512]{2,1,0:T(8,128)(2,1)S(1)} async-done(((bf16[8,72,512]{2,1,0:T(8,128)(2,1)}), bf16[8,72,512]{2,1,0:T(8,128)(2,1)S(1)}, u32[]{:S(2)}, u32[]{:S(2)}) %all-to-all-start.1) | async-done | bytes 589856 | tf_op jit(solution)/shard_map/all_to_all | solution.py:318
  28.4 1.4 %shard_map.85 = (bf16[1024,128]{1,0:T(8,128)(2,1)S(1)}, bf16[1024,128]{1,0:T(8,128)(2,1)S(1)}, f32[4,256,128]{2,1,0:T(8,128)S(1)}, bf16[4,256,1024]{2,1,0:T(8,128)(2,1)S(1)}, f32[4,256,128]{2,1,0:T(8,128)S(1)}) custom-call(bf16[8,72,512]{2,1,0:T(8,128)(2,1)S(1)} %all-to-all-done.1.qg_ref, bf16[8,64,256]{2,1,0:T(8,128)(2,1)S(1)} %all_to_all.20.kv0_ref, ...), custom_call_target="tpu_custom_call" | custom-call | tf_op jit(solution)/shard_map/pallas_call | solution.py:292
  29.8 0.0 collective-permute-done.1.kv2_ref
  29.8 0.8 %shard_map.86 = (bf16[512,128]{1,0:T(8,128)(2,1)S(1)}, bf16[4,256,128]{2,1,0:T(8,128)(2,1)S(1)}, bf16[4,256,128]{2,1,0:T(8,128)(2,1)S(1)}, bf16[4,256,512]{2,1,0...) custom-call(bf16[8,72,512]{2,1,0:T(8,128)(2,1)S(1)} %all-to-all-done.1.qg_ref, ...), custom_call_target="tpu_custom_call" | custom-call | tf_op jit(solution)/shard_map/pallas_call | solution.py:292
  30.6 0.7 %collective-permute-start.2 = (bf16[8,64,256]{2,1,0:T(8,128)(2,1)S(1)}, bf16[8,64,256]{2,1,0:T(8,128)(2,1)S(1)}, u32[]{:S(2)}, u32[]{:S(2)}) collective-permute-start(bf16[8,64,256]{2,1,0:T(8,128)(2,1)S(1)} %get-tuple-element.39), channel_id=1, source_target_pairs={{16,8},{24,16},{17,9},{25,17},{18,10},{26,18},{19,11},{27,19},{20,... | collective-permute-start | bytes 786440 | tf_op jit(solution)/shard_map/ppermute | solution.py:314
  31.3 2.3 %shard_map.87 = (bf16[8,64,512]{2,1,0:T(8,128)(2,1)}, f32[8,64,256]{2,1,0:T(8,128)S(1)}, f32[8,64,256]{2,1,0:T(8,128)S(1)}) custom-call(bf16[8,72,512]{2,1,0:T(8,128)(2,1)S(1)} %all-to-all-done.1.qg_ref, bf16[1024,128]{1,0:T(8,128)(2,1)S(1)} %get-tuple-element.26.k_s, bf16[1024,128]{1,0:T(8,128)(2,1)S(1)} %get-tuple-element.27.v_s, ...), custom_call_target="tpu_custom_call" | custom-call | tf_op jit(solution)/shard_map/pallas_call | solution.py:292
  33.6 3.5 %all-to-all-start.2 = ((bf16[8,64,512]{2,1,0:T(8,128)(2,1)}), bf16[8,64,512]{2,1,0:T(8,128)(2,1)S(1)}, u32[]{:S(2)}, u32[]{:S(2)}) async-start(bf16[8,64,512]{2,1,0:T(8,128)(2,1)} %get-tuple-element.36), calls=%async_computation.2 | async-start | bytes 1048576 | tf_op jit(solution)/shard_map/all_to_all | solution.py:318
  37.1 0.0 collective-permute-done.2.b_ref
  37.1 1.3 %collective-permute-start.3 = (bf16[8,64,256]{2,1,0:T(8,128)(2,1)S(1)}, bf16[8,64,256]{2,1,0:T(8,128)(2,1)S(1)}, u32[]{:S(2)}, u32[]{:S(2)}) collective-permute-start(bf16[8,64,256]{2,1,0:T(8,128)(2,1)S(1)} %shard_map.88), channel_id=1, source_target_pairs={{8,0},{16,8},{24,16},{9,1},{17,9},{25,17},{10,2},{18,10},{26,18},{... | collective-permute-start | bytes 786440 | tf_op jit(solution)/shard_map/ppermute | solution.py:314
  38.4 13.8 %collective-permute-done.3.b_ref = bf16[8,64,256]{2,1,0:T(8,128)(2,1)S(1)} collective-permute-done((bf16[8,64,256]{2,1,0:T(8,128)(2,1)S(1)}, bf16[8,64,256]{2,1,0:T(8,128)(2,1)S(1)}, u32[]{:S(2)}, u32[]{:S(2)}) %collective-permute-start.3) | collective-permute-done | bytes 262176 | tf_op jit(solution)/shard_map/ppermute | solution.py:314
  52.3 0.0 all-to-all-done.2.a_ref
  52.3 9.6 %all_to_all.21.b_ref = bf16[8,64,256]{2,1,0:T(8,128)(2,1)S(1)} all-to-all(bf16[8,64,256]{2,1,0:T(8,128)(2,1)S(1)} %shard_map.89), channel_id=1, replica_groups=mesh['hi'=4,'lo'=2,'head'=4] {'lo','head'}, dimensions={0} | all-to-all | bytes 524288 | tf_op jit(solution)/shard_map/all_to_all | solution.py:318
  61.9 1.1 %shard_map.90 = (bf16[64,2048]{1,0:T(8,128)(2,1)}, bf16[64,2048]{1,0:T(8,128)(2,1)}, bf16[64,1024]{1,0:T(8,128)(2,1)}, bf16[64,1024]{1,0:T(8,128)(2,1)}) custom-call(bf16[8,64,512]{2,1,0:T(8,128)(2,1)S(1)} %all-to-all-done.2.a_ref, bf16[8,64,256]{2,1,0:T(8,128)(2,1)S(1)} %all_to_all.21.b_ref), custom_call_target="tpu_custom_call" | custom-call | tf_op jit(solution)/shard_map/pallas_call | solution.py:292
  (2 shorter events, 0.1 us)
Async XLA Ops:
  13.8 9.7 %collective-permute-start = (bf16[8,64,256]{2,1,0:T(8,128)(2,1)S(1)}, bf16[8,64,256]{2,1,0:T(8,128)(2,1)S(1)}, u32[]{:S(2)}, u32[]{:S(2)}) collective-permute-start(bf16[8,64,256]{2,1,0:T(8,128)(2,1)S(1)} %all_to_all.20.kv0_ref), channel_id=1, source_target_pairs={{0,8},{8,16},{16,24},{24,0},{1,9},{9,17},{17,25},{25,1},{2,10},{10... | collective-permute-start | bytes 786440 | tf_op jit(solution)/shard_map/ppermute | solution.py:308
  15.4 13.0 %all-to-all-start.1 = ((bf16[8,72,512]{2,1,0:T(8,128)(2,1)}), bf16[8,72,512]{2,1,0:T(8,128)(2,1)S(1)}, u32[]{:S(2)}, u32[]{:S(2)}) async-start(bf16[8,72,512]{2,1,0:T(8,128)(2,1)} %get-tuple-element.24), calls=%async_computation.1 | async-start | bytes 1179648 | tf_op jit(solution)/shard_map/all_to_all | solution.py:318
  23.5 6.3 %collective-permute-start.1 = (bf16[8,64,256]{2,1,0:T(8,128)(2,1)S(1)}, bf16[8,64,256]{2,1,0:T(8,128)(2,1)S(1)}, u32[]{:S(2)}, u32[]{:S(2)}) collective-permute-start(bf16[8,64,256]{2,1,0:T(8,128)(2,1)S(1)} %collective-permute-done.kv1_ref), channel_id=1, source_target_pairs={{8,16},{16,24},{9,17},{17,25},{10,18},{18,26},{11,19},{19,27},{12,... | collective-permute-start | bytes 786440 | tf_op jit(solution)/shard_map/ppermute | solution.py:314
  30.6 6.5 %collective-permute-start.2 = (bf16[8,64,256]{2,1,0:T(8,128)(2,1)S(1)}, bf16[8,64,256]{2,1,0:T(8,128)(2,1)S(1)}, u32[]{:S(2)}, u32[]{:S(2)}) collective-permute-start(bf16[8,64,256]{2,1,0:T(8,128)(2,1)S(1)} %get-tuple-element.39), channel_id=1, source_target_pairs={{16,8},{24,16},{17,9},{25,17},{18,10},{26,18},{19,11},{27,19},{20,... | collective-permute-start | bytes 786440 | tf_op jit(solution)/shard_map/ppermute | solution.py:314
  33.6 18.7 %all-to-all-start.2 = ((bf16[8,64,512]{2,1,0:T(8,128)(2,1)}), bf16[8,64,512]{2,1,0:T(8,128)(2,1)S(1)}, u32[]{:S(2)}, u32[]{:S(2)}) async-start(bf16[8,64,512]{2,1,0:T(8,128)(2,1)} %get-tuple-element.36), calls=%async_computation.2 | async-start | bytes 1048576 | tf_op jit(solution)/shard_map/all_to_all | solution.py:318
  37.1 15.1 %collective-permute-start.3 = (bf16[8,64,256]{2,1,0:T(8,128)(2,1)S(1)}, bf16[8,64,256]{2,1,0:T(8,128)(2,1)S(1)}, u32[]{:S(2)}, u32[]{:S(2)}) collective-permute-start(bf16[8,64,256]{2,1,0:T(8,128)(2,1)S(1)} %shard_map.88), channel_id=1, source_target_pairs={{8,0},{16,8},{24,16},{9,1},{17,9},{25,17},{10,2},{18,10},{26,18},{... | collective-permute-start | bytes 786440 | tf_op jit(solution)/shard_map/ppermute | solution.py:314

commit v7 on v6

--- a/solution.py
+++ b/solution.py
@@ -154,8 +154,44 @@
             step(i, 0)
 
 
-def far_kernel(head_count, qg_ref, kv2_ref, near_ref, stat_ref,
-               k_s, o_ref, gs_ref, dsf_ref, dots_ref, g2_ref, v_s, dk_s, dv_s):
+def backward_step(i, start, refs, od_ref, dk_s, dv_s):
+    qg_ref, k_s, v_s, kf_ref, o_ref, gs_ref, p_ref, dsf_ref, dots_ref = refs
+    n, rows, _ = od_ref.shape
+    tok = n * rows
+    per = BLOCK // rows
+    near = slice(start, tok + (i + 1) * BLOCK)
+    q = stacked(qg_ref, i, rows, 0)
+    g = gs_ref[i]
+    pb = p_ref[i, :, near]
+    dots = dots_ref[i, :, :1]
+    ds = (pb.astype(jnp.float32) * (nt(g, v_s[near]) - dots)).astype(jnp.bfloat16)
+    dq = nn(ds, k_s[near])
+    if kf_ref is not None:
+        dq = dq + nn(dsf_ref[i, :, : tok - i * BLOCK], kf_ref[i * BLOCK :])
+    dq = (query_scale * dq).astype(jnp.bfloat16)
+    o = o_ref[i]
+    dk_s[near] += tn(ds, q)
+    dv_s[near] += tn(pb, g)
+    chunk = slice(i * per, (i + 1) * per)
+    for u in range(2):
+        part = slice(u * BLOCK, (u + 1) * BLOCK)
+        od_ref[chunk, :, u * HEAD_SIZE : (u + 1) * HEAD_SIZE] = o[part].reshape(
+            per, rows, HEAD_SIZE
+        )
+        od_ref[chunk, :, (2 + u) * HEAD_SIZE : (3 + u) * HEAD_SIZE] = dq[part].reshape(
+            per, rows, HEAD_SIZE
+        )
+
+
+def hand_over(ref, dk, dv):
+    n, rows, _ = ref.shape
+    ref[:, :, :HEAD_SIZE] = (query_scale * dk).astype(ref.dtype).reshape(n, rows, HEAD_SIZE)
+    ref[:, :, HEAD_SIZE:] = dv.astype(ref.dtype).reshape(n, rows, HEAD_SIZE)
+
+
+def far_kernel(head_count, qg_ref, kv2_ref, near_ref, stat_ref, kn_ref, vn_ref, p_ref,
+               k_s, o_ref, gs_ref, dsf_ref, dots_ref, g2_ref, od_ref, g1_ref, g0_ref,
+               v_s, dk_s, dv_s):
     n, rows, _ = kv2_ref.shape
     tok = n * rows
     blocks = tok // BLOCK
@@ -199,73 +235,52 @@
 
     @pl.when(hi == 0)
     def _():
+        own = slice(tok, 2 * tok)
+        dk_s[own] = jnp.zeros((tok, HEAD_SIZE), jnp.float32)
+        dv_s[own] = jnp.zeros((tok, HEAD_SIZE), jnp.float32)
+        refs = (qg_ref, kn_ref, vn_ref, None, o_ref, gs_ref, p_ref, None, dots_ref)
         for i in range(blocks):
             step(i, False)
+            backward_step(i, tok, refs, od_ref, dk_s, dv_s)
+        hand_over(g0_ref, dk_s[own], dv_s[own])
+        g1_ref[...] = jnp.zeros_like(g1_ref)
         g2_ref[...] = jnp.zeros_like(g2_ref)
 
     @pl.when(hi > 0)
     def _():
         k_s[...] = kv2_ref[:, :, :HEAD_SIZE].reshape(tok, HEAD_SIZE)
         v_s[...] = kv2_ref[:, :, HEAD_SIZE:].reshape(tok, HEAD_SIZE)
+        whole = slice(0, tok)
+        dk_s[whole] = jnp.zeros((tok, HEAD_SIZE), jnp.float32)
+        dv_s[whole] = jnp.zeros((tok, HEAD_SIZE), jnp.float32)
+        for i in range(blocks):
+            step(i, True)
+        hand_over(g2_ref, dk_s[whole], dv_s[whole])
+
+
+def backward_kernel(qg_ref, k_s, v_s, kf_ref, o_ref, gs_ref, p_ref, dsf_ref, dots_ref,
+                    od_in, g1_in, g0_in, od_ref, g1_ref, g0_ref, dk_s, dv_s):
+    n, rows, _ = od_ref.shape
+    tok = n * rows
+    refs = (qg_ref, k_s, v_s, kf_ref, o_ref, gs_ref, p_ref, dsf_ref, dots_ref)
+
+    hi = lax.axis_index("hi")
+
+    @pl.when(hi == 0)
+    def _():
+        od_ref[...] = od_in[...]
+        g1_ref[...] = g1_in[...]
+        g0_ref[...] = g0_in[...]
+
+    @pl.when(hi > 0)
+    def _():
         dk_s[...] = jnp.zeros_like(dk_s)
         dv_s[...] = jnp.zeros_like(dv_s)
-        for i in range(blocks):
-            step(i, True)
-        g2_ref[:, :, :HEAD_SIZE] = (
-            (query_scale * dk_s[...]).astype(jnp.bfloat16).reshape(n, rows, HEAD_SIZE)
-        )
-        g2_ref[:, :, HEAD_SIZE:] = dv_s[...].astype(jnp.bfloat16).reshape(n, rows, HEAD_SIZE)
-
-
-def backward_kernel(qg_ref, k_s, v_s, kf_ref, o_ref, gs_ref, p_ref, dsf_ref, dots_ref,
-                    od_ref, g1_ref, g0_ref, dk_s, dv_s):
-    n, rows, _ = od_ref.shape
-    tok = n * rows
-    blocks = tok // BLOCK
-    per = BLOCK // rows
-    dk_s[...] = jnp.zeros_like(dk_s)
-    dv_s[...] = jnp.zeros_like(dv_s)
-
-    def step(i, own_only):
-        near = slice(tok if own_only else 0, tok + (i + 1) * BLOCK)
-        q = stacked(qg_ref, i, rows, 0)
-        g = gs_ref[i]
-        pb = p_ref[i, :, near]
-        dots = dots_ref[i, :, :1]
-        ds = (pb.astype(jnp.float32) * (nt(g, v_s[near]) - dots)).astype(jnp.bfloat16)
-        dq = nn(ds, k_s[near])
-        if not own_only:
-            dq = dq + nn(dsf_ref[i, :, : tok - i * BLOCK], kf_ref[i * BLOCK :])
-        dq = (query_scale * dq).astype(jnp.bfloat16)
-        o = o_ref[i]
-        dk_s[near] += tn(ds, q)
-        dv_s[near] += tn(pb, g)
-        chunk = slice(i * per, (i + 1) * per)
-        for u in range(2):
-            part = slice(u * BLOCK, (u + 1) * BLOCK)
-            od_ref[chunk, :, u * HEAD_SIZE : (u + 1) * HEAD_SIZE] = o[part].reshape(
-                per, rows, HEAD_SIZE
-            )
-            od_ref[chunk, :, (2 + u) * HEAD_SIZE : (3 + u) * HEAD_SIZE] = dq[part].reshape(
-                per, rows, HEAD_SIZE
-            )
-
-    hi = lax.axis_index("hi")
-
-    @pl.when(hi == 0)
-    def _():
-        for i in range(blocks):
-            step(i, True)
-
-    @pl.when(hi > 0)
-    def _():
-        for i in range(blocks):
-            step(i, False)
-
-    for part, ref in enumerate((g1_ref, g0_ref)):
-        own = slice(part * tok, (part + 1) * tok)
-        ref[:, :, :HEAD_SIZE] = (query_scale * dk_s[own]).reshape(n, rows, HEAD_SIZE)
-        ref[:, :, HEAD_SIZE:] = dv_s[own].reshape(n, rows, HEAD_SIZE)
+        for i in range(tok // BLOCK):
+            backward_step(i, 0, refs, od_ref, dk_s, dv_s)
+        for part, ref in enumerate((g1_ref, g0_ref)):
+            own = slice(part * tok, (part + 1) * tok)
+            hand_over(ref, dk_s[own], dv_s[own])
 
 
 def add_kernel(a_ref, b_ref, o_ref):
@@ -368,7 +383,7 @@
         (qg, kv0, kv1),
         room=20,
     )
-    k_far, o, gs, dsf, dots, g2 = call(
+    k_far, o, gs, dsf, dots, g2, od, g1, g0 = call(
         functools.partial(far_kernel, heads),
         (
             bf(tok, HEAD_SIZE),
@@ -377,12 +392,15 @@
             bf(blocks, 2 * BLOCK, tok),
             f32(blocks, 2 * BLOCK, HEAD_SIZE),
             bf(n, rows, 2 * HEAD_SIZE),
+            bf(n, rows, 4 * HEAD_SIZE),
+            f32(n, rows, 2 * HEAD_SIZE),
+            f32(n, rows, 2 * HEAD_SIZE),
         ),
-        (qg, kv2, near, stat),
-        scratch=[bf(tok, HEAD_SIZE), f32(tok, HEAD_SIZE), f32(tok, HEAD_SIZE)],
+        (qg, kv2, near, stat, k_all, v_all, p),
+        scratch=[bf(tok, HEAD_SIZE), f32(2 * tok, HEAD_SIZE), f32(2 * tok, HEAD_SIZE)],
         room=20,
     )
-    r1 = line(g2, -1, 1)
+    r1 = ring(g2, -1)
     od, g1, g0 = call(
         backward_kernel,
         (
@@ -390,13 +408,13 @@
             f32(n, rows, 2 * HEAD_SIZE),
             f32(n, rows, 2 * HEAD_SIZE),
         ),
-        (qg, k_all, v_all, k_far, o, gs, p, dsf, dots),
+        (qg, k_all, v_all, k_far, o, gs, p, dsf, dots, od, g1, g0),
         scratch=[f32(2 * tok, HEAD_SIZE), f32(2 * tok, HEAD_SIZE)],
         room=24,
     )
     od_in = exchange(od)
     t = call(add_kernel, bf(*g1.shape), (g1, r1))
-    r2 = line(t, -1)
+    r2 = ring(t, -1)
     final = call(add_kernel, bf(*g0.shape), (g0, r2))
     g_in = exchange(final)
     return call(

time: 63.5 us -> 62.1 us (0.978)
  waiting for transfers between devices: 22.6 us -> 13.6 us
  starting transfers between devices: 11.2 us -> 18.8 us
    ppermute x3 -> x1, waiting for transfers between devices: 13.8 us -> 0.01 us  [line(): lax.ppermute(x, 'hi', pairs if by == 1 else [(j, i) for i, j in pairs])]
    ppermute x1 -> x3, starting transfers between devices: 1.58 us -> 11.1 us  [ring(): return lax.ppermute(x, 'hi', [(i, (i + by) % n) for i in range(n)])]
    ppermute x1 -> x3, waiting for transfers between devices: 4.6 us -> 9.42 us  [ring(): return lax.ppermute(x, 'hi', [(i, (i + by) % n) for i in range(n)])]
    ppermute x3 -> x1, starting transfers between devices: 2.64 us -> 0.67 us  [line(): lax.ppermute(x, 'hi', pairs if by == 1 else [(j, i) for i, j in pairs])]
  transfers between devices with their start and end apart: 6 -> 6, of which waited for: 3 -> 3; matrix products, arithmetic and copies ran while one was open for 0% -> 0% of each run, Pallas kernels for 6% -> 4%
where the time goes in v7:
time: 62.1 us; the launch traced here: 61.6 us
  blocking collectives  20.9 us (34%)
  starting transfers between devices  18.8 us (30%)
  waiting for transfers between devices  13.6 us (22%)
  Pallas kernels  7.6 us (12%)
  between operations  0.72 us (1%)
    all_to_all x2, blocking collectives, exchange(): lax.all_to_all(x, ('lo', 'head'), split_axis=0, concat_axis=0, tiled=True)  20.9 us
    ppermute x3, starting transfers between devices, ring(): return lax.ppermute(x, 'hi', [(i, (i + by) % n) for i in range(n)])  11.1 us
    ppermute x3, waiting for transfers between devices, ring(): return lax.ppermute(x, 'hi', [(i, (i + by) % n) for i in range(n)])  9.42 us
    pallas_call x7, Pallas kernels, call(): pl.pallas_call(kernel, out_shape=outs, in_specs=[HB] * outer + [VM] * (le...  7.6 us
    all_to_all x2, starting transfers between devices, exchange(): lax.all_to_all(x, ('lo', 'head'), split_axis=0, concat_axis=0, tiled=True)  7.03 us
    all_to_all x2, waiting for transfers between devices, exchange(): lax.all_to_all(x, ('lo', 'head'), split_axis=0, concat_axis=0, tiled=True)  4.21 us
  transfers between devices with their start and end apart: 6, of which 3 were waited for; matrix products, arithmetic and copies ran while one was open for 0% of the time, Pallas kernels for 4%

profile of v7, /device:TPU:0, one launch (start us, length us, event | category | flops | bytes accessed | tf_op | source)
XLA Modules:
  0.0 61.6 jit_solution(8564311198917522012)
XLA Ops:
  0.6 2.0 %shard_map.84 = (bf16[8,64,256]{2,1,0:T(8,128)(2,1)S(1)}, bf16[8,72,512]{2,1,0:T(8,128)(2,1)}) custom-call(s32[2]{0:T(128)} %lo_ref.1, bf16[64,2048]{1,0:T(8,128)(2,1)} %q_ref.1, bf16[64,1024]{1,0:T(8,128)(2,1)} %k_ref.1, bf16[64,1024]{1,0:T(8,128)(2,1)} %v_ref.1, bf16[64,2048]{1,0:T(8,128)(2,1)} %g_ref.1), custom_call_target="tpu_custom_call" | custom-call | tf_op jit(solution)/shard_map/pallas_call | solution.py:307
  2.7 11.1 %all_to_all.20.kv0_ref = bf16[8,64,256]{2,1,0:T(8,128)(2,1)S(1)} all-to-all(bf16[8,64,256]{2,1,0:T(8,128)(2,1)S(1)} %get-tuple-element.25), channel_id=1, replica_groups=mesh['hi'=4,'lo'=2,'head'=4] {'lo','head'}, dimensions={0} | all-to-all | bytes 524288 | tf_op jit(solution)/shard_map/all_to_all | solution.py:333
  13.8 1.6 %collective-permute-start = (bf16[8,64,256]{2,1,0:T(8,128)(2,1)S(1)}, bf16[8,64,256]{2,1,0:T(8,128)(2,1)S(1)}, u32[]{:S(2)}, u32[]{:S(2)}) collective-permute-start(bf16[8,64,256]{2,1,0:T(8,128)(2,1)S(1)} %all_to_all.20.kv0_ref), channel_id=1, source_target_pairs={{0,8},{8,16},{16,24},{24,0},{1,9},{9,17},{17,25},{25,1},{2,10},{10... | collective-permute-start | bytes 786440 | tf_op jit(solution)/shard_map/ppermute | solution.py:323
  15.4 3.5 %all-to-all-start.1 = ((bf16[8,72,512]{2,1,0:T(8,128)(2,1)}), bf16[8,72,512]{2,1,0:T(8,128)(2,1)S(1)}, u32[]{:S(2)}, u32[]{:S(2)}) async-start(bf16[8,72,512]{2,1,0:T(8,128)(2,1)} %get-tuple-element.27), calls=%async_computation.1 | async-start | bytes 1179648 | tf_op jit(solution)/shard_map/all_to_all | solution.py:333
  18.9 4.6 %collective-permute-done.kv1_ref = bf16[8,64,256]{2,1,0:T(8,128)(2,1)S(1)} collective-permute-done((bf16[8,64,256]{2,1,0:T(8,128)(2,1)S(1)}, bf16[8,64,256]{2,1,0:T(8,128)(2,1)S(1)}, u32[]{:S(2)}, u32[]{:S(2)}) %collective-permute-start) | collective-permute-done | bytes 262176 | tf_op jit(solution)/shard_map/ppermute | solution.py:323
  23.5 0.7 %collective-permute-start.1 = (bf16[8,64,256]{2,1,0:T(8,128)(2,1)S(1)}, bf16[8,64,256]{2,1,0:T(8,128)(2,1)S(1)}, u32[]{:S(2)}, u32[]{:S(2)}) collective-permute-start(bf16[8,64,256]{2,1,0:T(8,128)(2,1)S(1)} %collective-permute-done.kv1_ref), channel_id=1, source_target_pairs={{8,16},{16,24},{9,17},{17,25},{10,18},{18,26},{11,19},{19,27},{12,... | collective-permute-start | bytes 786440 | tf_op jit(solution)/shard_map/ppermute | solution.py:329
  24.2 4.2 %all-to-all-done.1.qg_ref = bf16[8,72,512]{2,1,0:T(8,128)(2,1)S(1)} async-done(((bf16[8,72,512]{2,1,0:T(8,128)(2,1)}), bf16[8,72,512]{2,1,0:T(8,128)(2,1)S(1)}, u32[]{:S(2)}, u32[]{:S(2)}) %all-to-all-start.1) | async-done | bytes 589856 | tf_op jit(solution)/shard_map/all_to_all | solution.py:333
  28.4 1.4 %shard_map.85 = (bf16[1024,128]{1,0:T(8,128)(2,1)S(1)}, bf16[1024,128]{1,0:T(8,128)(2,1)S(1)}, f32[4,256,128]{2,1,0:T(8,128)S(1)}, bf16[4,256,1024]{2,1,0:T(8,128)(2,1)S(1)}, f32[4,256,128]{2,1,0:T(8,128)S(1)}) custom-call(bf16[8,72,512]{2,1,0:T(8,128)(2,1)S(1)} %all-to-all-done.1.qg_ref, bf16[8,64,256]{2,1,0:T(8,128)(2,1)S(1)} %all_to_all.20.kv0_ref, ...), custom_call_target="tpu_custom_call" | custom-call | tf_op jit(solution)/shard_map/pallas_call | solution.py:307
  29.8 0.0 collective-permute-done.1.kv2_ref
  29.8 2.1 %shard_map.86 = (bf16[512,128]{1,0:T(8,128)(2,1)S(1)}, bf16[4,256,128]{2,1,0:T(8,128)(2,1)S(1)}, bf16[4,256,128]{2,1,0:T(8,128)(2,1)S(1)}, bf16[4,256,512]{2,1,0...) custom-call(bf16[8,72,512]{2,1,0:T(8,128)(2,1)S(1)} %all-to-all-done, ...), custom_call_target="tpu_custom_call" | custom-call | tf_op jit(solution)/shard_map/pallas_call | solution.py:307
  31.9 5.6 %collective-permute-start.2 = (bf16[8,64,256]{2,1,0:T(8,128)(2,1)S(1)}, bf16[8,64,256]{2,1,0:T(8,128)(2,1)S(1)}, u32[]{:S(2)}, u32[]{:S(2)}) collective-permute-start(bf16[8,64,256]{2,1,0:T(8,128)(2,1)S(1)} %get-tuple-element.45), channel_id=1, source_target_pairs={{0,24},{8,0},{16,8},{24,16},{1,25},{9,1},{17,9},{25,17},{2,26},{10... | collective-permute-start | bytes 786440 | tf_op jit(solution)/shard_map/ppermute | solution.py:323
  37.4 0.9 %shard_map.87 = (bf16[8,64,512]{2,1,0:T(8,128)(2,1)}, f32[8,64,256]{2,1,0:T(8,128)S(1)}, f32[8,64,256]{2,1,0:T(8,128)S(1)}) custom-call(bf16[8,72,512]{2,1,0:T(8,128)(2,1)S(1)} %all-to-all-done.1.qg_ref, bf16[1024,128]{1,0:T(8,128)(2,1)S(1)} %get-tuple-element.29.kn_ref.k_s, bf16[1024,128]{1,0:T(8,128)(2,1)S(1)} %get-tuple-element.30.vn_ref.v_s, ...), custom_call_target="tpu_custom_call" | custom-call | tf_op jit(solution)/shard_map/pallas_call | solution.py:307
  38.3 3.5 %all-to-all-start.2 = ((bf16[8,64,512]{2,1,0:T(8,128)(2,1)}), bf16[8,64,512]{2,1,0:T(8,128)(2,1)S(1)}, u32[]{:S(2)}, u32[]{:S(2)}) async-start(bf16[8,64,512]{2,1,0:T(8,128)(2,1)} %get-tuple-element.42), calls=%async_computation.2 | async-start | bytes 1048576 | tf_op jit(solution)/shard_map/all_to_all | solution.py:333
  41.8 0.0 collective-permute-done.2.b_ref
  41.9 3.9 %collective-permute-start.3 = (bf16[8,64,256]{2,1,0:T(8,128)(2,1)S(1)}, bf16[8,64,256]{2,1,0:T(8,128)(2,1)S(1)}, u32[]{:S(2)}, u32[]{:S(2)}) collective-permute-start(bf16[8,64,256]{2,1,0:T(8,128)(2,1)S(1)} %shard_map.88), channel_id=1, source_target_pairs={{0,24},{8,0},{16,8},{24,16},{1,25},{9,1},{17,9},{25,17},{2,26},{10... | collective-permute-start | bytes 786440 | tf_op jit(solution)/shard_map/ppermute | solution.py:323
  45.8 4.8 %collective-permute-done.3.b_ref = bf16[8,64,256]{2,1,0:T(8,128)(2,1)S(1)} collective-permute-done((bf16[8,64,256]{2,1,0:T(8,128)(2,1)S(1)}, bf16[8,64,256]{2,1,0:T(8,128)(2,1)S(1)}, u32[]{:S(2)}, u32[]{:S(2)}) %collective-permute-start.3) | collective-permute-done | bytes 262176 | tf_op jit(solution)/shard_map/ppermute | solution.py:323
  50.7 0.0 all-to-all-done.2.a_ref
  50.7 9.8 %all_to_all.21.b_ref = bf16[8,64,256]{2,1,0:T(8,128)(2,1)S(1)} all-to-all(bf16[8,64,256]{2,1,0:T(8,128)(2,1)S(1)} %shard_map.89), channel_id=1, replica_groups=mesh['hi'=4,'lo'=2,'head'=4] {'lo','head'}, dimensions={0} | all-to-all | bytes 524288 | tf_op jit(solution)/shard_map/all_to_all | solution.py:333
  60.5 1.1 %shard_map.90 = (bf16[64,2048]{1,0:T(8,128)(2,1)}, bf16[64,2048]{1,0:T(8,128)(2,1)}, bf16[64,1024]{1,0:T(8,128)(2,1)}, bf16[64,1024]{1,0:T(8,128)(2,1)}) custom-call(bf16[8,64,512]{2,1,0:T(8,128)(2,1)S(1)} %all-to-all-done.2.a_ref, bf16[8,64,256]{2,1,0:T(8,128)(2,1)S(1)} %all_to_all.21.b_ref), custom_call_target="tpu_custom_call" | custom-call | tf_op jit(solution)/shard_map/pallas_call | solution.py:307
  (2 shorter events, 0.1 us)
Async XLA Ops:
  13.8 9.7 %collective-permute-start = (bf16[8,64,256]{2,1,0:T(8,128)(2,1)S(1)}, bf16[8,64,256]{2,1,0:T(8,128)(2,1)S(1)}, u32[]{:S(2)}, u32[]{:S(2)}) collective-permute-start(bf16[8,64,256]{2,1,0:T(8,128)(2,1)S(1)} %all_to_all.20.kv0_ref), channel_id=1, source_target_pairs={{0,8},{8,16},{16,24},{24,0},{1,9},{9,17},{17,25},{25,1},{2,10},{10... | collective-permute-start | bytes 786440 | tf_op jit(solution)/shard_map/ppermute | solution.py:323
  15.4 13.0 %all-to-all-start.1 = ((bf16[8,72,512]{2,1,0:T(8,128)(2,1)}), bf16[8,72,512]{2,1,0:T(8,128)(2,1)S(1)}, u32[]{:S(2)}, u32[]{:S(2)}) async-start(bf16[8,72,512]{2,1,0:T(8,128)(2,1)} %get-tuple-element.27), calls=%async_computation.1 | async-start | bytes 1179648 | tf_op jit(solution)/shard_map/all_to_all | solution.py:333
  23.5 6.3 %collective-permute-start.1 = (bf16[8,64,256]{2,1,0:T(8,128)(2,1)S(1)}, bf16[8,64,256]{2,1,0:T(8,128)(2,1)S(1)}, u32[]{:S(2)}, u32[]{:S(2)}) collective-permute-start(bf16[8,64,256]{2,1,0:T(8,128)(2,1)S(1)} %collective-permute-done.kv1_ref), channel_id=1, source_target_pairs={{8,16},{16,24},{9,17},{17,25},{10,18},{18,26},{11,19},{19,27},{12,... | collective-permute-start | bytes 786440 | tf_op jit(solution)/shard_map/ppermute | solution.py:329
  31.9 10.0 %collective-permute-start.2 = (bf16[8,64,256]{2,1,0:T(8,128)(2,1)S(1)}, bf16[8,64,256]{2,1,0:T(8,128)(2,1)S(1)}, u32[]{:S(2)}, u32[]{:S(2)}) collective-permute-start(bf16[8,64,256]{2,1,0:T(8,128)(2,1)S(1)} %get-tuple-element.45), channel_id=1, source_target_pairs={{0,24},{8,0},{16,8},{24,16},{1,25},{9,1},{17,9},{25,17},{2,26},{10... | collective-permute-start | bytes 786440 | tf_op jit(solution)/shard_map/ppermute | solution.py:323
  38.3 12.4 %all-to-all-start.2 = ((bf16[8,64,512]{2,1,0:T(8,128)(2,1)}), bf16[8,64,512]{2,1,0:T(8,128)(2,1)S(1)}, u32[]{:S(2)}, u32[]{:S(2)}) async-start(bf16[8,64,512]{2,1,0:T(8,128)(2,1)} %get-tuple-element.42), calls=%async_computation.2 | async-start | bytes 1048576 | tf_op jit(solution)/shard_map/all_to_all | solution.py:333
  41.9 8.7 %collective-permute-start.3 = (bf16[8,64,256]{2,1,0:T(8,128)(2,1)S(1)}, bf16[8,64,256]{2,1,0:T(8,128)(2,1)S(1)}, u32[]{:S(2)}, u32[]{:S(2)}) collective-permute-start(bf16[8,64,256]{2,1,0:T(8,128)(2,1)S(1)} %shard_map.88), channel_id=1, source_target_pairs={{0,24},{8,0},{16,8},{24,16},{1,25},{9,1},{17,9},{25,17},{2,26},{10... | collective-permute-start | bytes 786440 | tf_op jit(solution)/shard_map/ppermute | solution.py:323
